TPU v7x, 256 devices: a whole 4x4x8 slice. The times are simulated.
256 devices in a mesh: space: 64 (over x, z, core), mode: 4 (over y).
Axes of the slice: x: 4, y: 4, z: 8, core: 2. Of those that a mesh axis runs over, the one named last changes fastest.
Arguments:
- modes_in: bfloat16 [120, 131072], P('mode', 'space'), may hold values from -6 to 6
- blocks: bfloat16 [5, 4608, 128, 128], P(None, 'space'), may hold values from -0.25 to 0.25
- block_cols: int32 [1152, 4], P('space'), may hold values from 0 to 15
- send_slot: int32 [16384], P('space'), may hold values from 0 to 511, as said below
- recv_row: int32 [32768], P('space'), may hold values from 0 to 2048, as said below
- mix_cols: int32 [5, 120, 8], replicated, may hold values from 0 to 120, as said below
- mix_coef: float32 [5, 120, 8], replicated, as said below
Outputs:
- first_apply: bfloat16 [120, 131072], P('mode', 'space')
- second_apply: bfloat16 [120, 131072], P('mode', 'space')
Inputs may be any that keep to these rules, and one draw needn't show every extreme that they name: Interface row e of subdomain d goes to subdomain send_slot[d * 256 + e] // 8 at position send_slot[d * 256 + e] % 8. A subdomain's entries are distinct, and for each destination they fill positions from 0 upward, at most 8; one destination, the same for all subdomains, gets 8 rows from every subdomain. `recv_row`: entry o * 64 * 8 + d * 8 + p is the own degree of freedom of subdomain o at which position p from subdomain d is added; it is 2048 exactly where subdomain d sends fewer than p + 1 rows to o. Live entries may repeat. `mix_cols`: column 120 marks a padded slot. Each row of each term has from 4 to 8 live slots, both reached; live columns may repeat. `mix_coef`: zero exactly on padded slots.
All inputs are finite; a program needn't handle non-finite values.
Results may differ from a plain program's by a relative error of at most 0.022.
Values may be sent and summed in bfloat16 or wider, within the bound.
No kernel may reach another device: no remote copies, remote signals or barrier semaphores. Data moves between devices by JAX's collectives and lax.ppermute only.
A program may use at most 64 MiB of HBM per device.

v0:
```python
import jax
import jax.numpy as jnp
from jax import lax
from jax.sharding import PartitionSpec as P


def dense_mixer(mix_cols, mix_coef):
    mode_count = mix_coef.shape[1]
    columns = jnp.arange(mode_count, dtype=jnp.int32)
    onehot_table = (mix_cols[..., None] == columns).astype(jnp.float32)
    return jnp.sum(mix_coef[..., None] * onehot_table, axis=2).astype(jnp.bfloat16)


def block_rows(field_blocks, stiffness, block_cols):
    picked = field_blocks[:, :, block_cols, :]
    return jnp.einsum("mkcnd,kcnde->mce", picked, stiffness, preferred_element_type=jnp.float32)


def local(modes_in, blocks, block_cols, send_slot, recv_row, mix_cols, mix_coef):
    chaos_mixer = dense_mixer(mix_cols, mix_coef)
    term_count = blocks.shape[0]
    block_size = blocks.shape[-1]
    out_blocks, stored = block_cols.shape
    stiffness = blocks.reshape(term_count, out_blocks, stored, block_size, block_size)
    modes_dev, owned_dofs = modes_in.shape
    owned_blocks = owned_dofs // block_size
    slot_total = recv_row.shape[0]

    def send_partials(partials):
        flat_rows = partials.reshape(modes_dev, -1)
        packed = jnp.zeros((modes_dev, slot_total), jnp.float32).at[:, send_slot].set(flat_rows)
        return lax.all_to_all(
            packed.astype(jnp.bfloat16), "space", split_axis=1, concat_axis=1, tiled=True
        ).astype(packed.dtype)

    def mix_field(field_now):
        regrouped = lax.all_to_all(field_now, "mode", split_axis=1, concat_axis=0, tiled=True)
        mixed_all = jnp.einsum(
            "kij,jn->ikn", chaos_mixer, regrouped, preferred_element_type=jnp.float32
        ).astype(jnp.bfloat16)
        return lax.all_to_all(mixed_all, "mode", split_axis=0, concat_axis=2, tiled=True)

    def one_apply(field_now):
        mixed_field = mix_field(field_now)
        field_blocks = mixed_field.reshape(modes_dev, term_count, owned_blocks, block_size)
        products = block_rows(field_blocks, stiffness, block_cols)
        arrived = send_partials(products[:, owned_blocks:])
        owned_part = products[:, :owned_blocks]
        owned_flat = owned_part.reshape(modes_dev, owned_dofs)
        summed = owned_flat.at[:, recv_row].add(arrived, mode="drop")
        return summed.astype(jnp.bfloat16)

    first_apply = one_apply(modes_in)
    second_apply = one_apply(first_apply)
    return (first_apply, second_apply)


def solution(mesh):
    in_specs = (
        P("mode", "space"),
        P(None, "space", None, None),
        P("space", None),
        P("space"),
        P("space"),
        P(),
        P(),
    )
    out_specs = (P("mode", "space"), P("mode", "space"))
    return jax.shard_map(local, mesh=mesh, in_specs=in_specs, out_specs=out_specs, check_vma=False)
```

profile of v0, /device:TPU:1, one launch (start us, length us, event | category | flops | bytes accessed | tf_op | source)
XLA Modules:
  0.0 132.8 jit_solution(6629927610011276790)
XLA Ops:
  0.6 1.0 all_to_all.62
  1.6 0.7 copy.74
  2.3 5.0 %all-to-all-start = ((bf16[30,4,512]{2,0,1:T(8,128)(2,1)}), bf16[30,4,512]{2,0,1:T(8,128)(2,1)S(1)}, u32[]{:S(2)}, u32[]{:S(2)}) async-start(bf16[30,4,512]{2,0,1:T(8,128)(2,1)} %copy.74), calls=%async_computation | async-start | bytes 262144 | tf_op jit(solution)/shard_map/all_to_all | solution.py:37
  7.3 0.9 copy.73
  8.2 0.0 copy-start
  8.2 0.0 copy-start.2
  8.2 0.9 copy.72
  9.1 3.5 %select_reduce_fusion = bf16[5,120,120]{2,1,0:T(8,128)(2,1)S(1)} fusion(f32[5,120,8]{2,1,0:T(8,128)S(1)} %copy.73, s32[5,120,8]{2,1,0:T(8,128)S(1)} %copy.72), kind=kLoop, calls=%fused_computation.12 | loop fusion | flops 1656000 | bytes 182400 | tf_op jit(solution)/shard_map/reduce_sum | solution.py:11
  12.6 0.0 all-to-all-done
  12.6 0.3 fusion.6
  13.0 1.2 copy.75
  14.1 4.2 %all-to-all-start.1 = ((bf16[120,5,512]{2,1,0:T(8,128)(2,1)}), bf16[120,5,512]{2,1,0:T(8,128)(2,1)S(1)}, u32[]{:S(2)}, u32[]{:S(2)}) async-start(bf16[120,5,512]{2,1,0:T(8,128)(2,1)} %copy.75), calls=%async_computation.1 | async-start | bytes 1966080 | tf_op jit(solution)/shard_map/all_to_all | solution.py:41
  18.4 0.0 copy-done
  18.4 0.1 copy.78
  18.5 0.1 reshape.54
  18.6 0.0 copy-done.2
  18.6 12.1 %all-to-all-done.1 = bf16[120,5,512]{2,1,0:T(8,128)(2,1)S(1)} async-done(((bf16[120,5,512]{2,1,0:T(8,128)(2,1)}), bf16[120,5,512]{2,1,0:T(8,128)(2,1)S(1)}, u32[]{:S(2)}, u32[]{:S(2)}) %all-to-all-start.1) | async-done | bytes 614432 | tf_op jit(solution)/shard_map/all_to_all | solution.py:41
  30.7 0.5 copy.77
  31.3 0.2 reshape.43
  31.5 0.2 copy.79
  31.7 2.8 %gather_fusion = bf16[72,30,5,128]{3,1,2,0:T(8,128)(2,1)} fusion(bf16[30,5,16,128]{3,0,2,1:T(8,128)(2,1)S(1)} %copy.79, s32[1024]{0:T(1024)S(1)} %pad_clamp_fusion), kind=kCustom, calls=%fused_computation | custom fusion | bytes 5529888 | tf_op jit(solution)/shard_map/gather | solution.py:15
  34.4 2.9 %copy.80 = bf16[72,30,5,128]{3,0,2,1:T(8,128)(2,1)S(1)} copy(bf16[72,30,5,128]{3,1,2,0:T(8,128)(2,1)} %gather_fusion) | data formatting | bytes 5529600 | tf_op jit(solution)/shard_map/gather | solution.py:15
  37.3 0.0 copy-start.1
  37.4 5.4 %fusion.8 = f32[30,18,128]{2,0,1:T(8,128)S(1)} fusion(bf16[5,18,4,128,128]{4,3,2,1,0:T(8,128)(2,1)} %bitcast.85, bf16[30,5,18,4,128]{4,3,2,1,0:T(4,128)(2,1)S(1)} %bitcast.77), kind=kOutput, calls=%fused_computation.18 | convolution fusion | flops 353894400 | bytes 14837760 | tf_op jit(solution)/shard_map/mkcnd,kcnde->mce/dot_general | solution.py:16
  42.8 0.1 copy.85
  43.0 1.2 scatter_custom_fusion
  44.2 0.7 convert_bitcast_fusion.5
  44.9 14.5 %all-to-all-start.2 = ((bf16[30,64,8]{0,2,1:T(8,128)(2,1)}), bf16[30,64,8]{0,2,1:T(8,128)(2,1)S(1)}, u32[]{:S(2)}, u32[]{:S(2)}) async-start(bf16[30,64,8]{0,2,1:T(8,128)(2,1)} %convert_bitcast_fusion.5), calls=%async_computation.2 | async-start | bytes 262144 | tf_op jit(solution)/shard_map/all_to_all | solution.py:32
  59.3 0.0 copy-done.1
  59.4 0.4 copy.105
  59.8 10.0 %all-to-all-done.2 = bf16[30,64,8]{0,2,1:T(8,128)(2,1)S(1)} async-done(((bf16[30,64,8]{0,2,1:T(8,128)(2,1)}), bf16[30,64,8]{0,2,1:T(8,128)(2,1)S(1)}, u32[]{:S(2)}, u32[]{:S(2)}) %all-to-all-start.2) | async-done | bytes 30752 | tf_op jit(solution)/shard_map/all_to_all | solution.py:32
  69.7 3.7 %scatter_custom_fusion.1 = f32[30,2048]{0,1:T(8,128)S(1)} fusion(f32[30,2048]{0,1:T(8,128)S(1)} %bitcast.74, s32[512]{0:T(512)S(1)} %compare_select_fusion, bf16[30,64,8]{0,2,1:T(8,128)(2,1)S(1)} %all-to-all-done.2), kind=kCustom, calls=%fused_computation.23 | custom fusion | flops 30720 | bytes 376832 | tf_op jit(solution)/shard_map/scatter-add | solution.py:50
  73.4 0.1 convert_element_type.46
  73.5 0.2 copy.87
  73.7 7.2 %all_to_all.86 = bf16[30,4,512]{2,0,1:T(8,128)(2,1)S(1)} all-to-all(bf16[30,4,512]{2,0,1:T(8,128)(2,1)S(1)} %copy.87), channel_id=1, replica_groups=mesh['space'=64,'mode'=4] {'mode'}, dimensions={1} | all-to-all | bytes 245760 | tf_op jit(solution)/shard_map/all_to_all | solution.py:37
  81.0 0.3 fusion.7
  81.3 0.2 copy.88
  81.5 15.3 %all_to_all.87 = bf16[120,5,512]{2,1,0:T(8,128)(2,1)S(1)} all-to-all(bf16[120,5,512]{2,1,0:T(8,128)(2,1)S(1)} %copy.88), channel_id=1, replica_groups=mesh['space'=64,'mode'=4] {'mode'}, dimensions={0} | all-to-all | bytes 1228800 | tf_op jit(solution)/shard_map/all_to_all | solution.py:41
  96.8 0.5 copy.90
  97.4 0.2 reshape.47
  97.6 0.2 copy.91
  97.8 2.8 %gather_fusion.1 = bf16[72,30,5,128]{3,1,2,0:T(8,128)(2,1)} fusion(bf16[30,5,16,128]{3,0,2,1:T(8,128)(2,1)S(1)} %copy.91, s32[1024]{0:T(1024)S(1)} %pad_clamp_fusion), kind=kCustom, calls=%fused_computation.1 | custom fusion | bytes 5529888 | tf_op jit(solution)/shard_map/gather | solution.py:15
  100.5 2.9 %copy.92 = bf16[72,30,5,128]{3,0,2,1:T(8,128)(2,1)S(1)} copy(bf16[72,30,5,128]{3,1,2,0:T(8,128)(2,1)} %gather_fusion.1) | data formatting | bytes 5529600 | tf_op jit(solution)/shard_map/gather | solution.py:15
  103.4 5.4 %fusion.13 = f32[30,18,128]{2,0,1:T(8,128)S(1)} fusion(bf16[5,18,4,128,128]{4,3,2,1,0:T(8,128)(2,1)} %bitcast.86, bf16[30,5,18,4,128]{4,3,2,1,0:T(4,128)(2,1)S(1)} %bitcast.78), kind=kOutput, calls=%fused_computation.19 | convolution fusion | flops 353894400 | bytes 14837760 | tf_op jit(solution)/shard_map/mkcnd,kcnde->mce/dot_general | solution.py:16
  108.9 0.1 copy.97
  109.0 1.2 scatter_custom_fusion.2
  110.3 0.7 convert_bitcast_fusion.4
  110.9 6.8 %all-to-all-start.5 = ((bf16[30,64,8]{0,2,1:T(8,128)(2,1)}), bf16[30,64,8]{0,2,1:T(8,128)(2,1)S(1)}, u32[]{:S(2)}, u32[]{:S(2)}) async-start(bf16[30,64,8]{0,2,1:T(8,128)(2,1)} %convert_bitcast_fusion.4), calls=%async_computation.5 | async-start | bytes 262144 | tf_op jit(solution)/shard_map/all_to_all | solution.py:32
  117.8 0.9 copy.99
  118.7 0.4 copy.108
  119.1 9.1 %all-to-all-done.5 = bf16[30,64,8]{0,2,1:T(8,128)(2,1)S(1)} async-done(((bf16[30,64,8]{0,2,1:T(8,128)(2,1)}), bf16[30,64,8]{0,2,1:T(8,128)(2,1)S(1)}, u32[]{:S(2)}, u32[]{:S(2)}) %all-to-all-start.5) | async-done | bytes 30752 | tf_op jit(solution)/shard_map/all_to_all | solution.py:32
  128.1 3.7 %scatter_custom_fusion.3 = f32[30,2048]{0,1:T(8,128)S(1)} fusion(f32[30,2048]{0,1:T(8,128)S(1)} %bitcast.73, s32[512]{0:T(512)S(1)} %compare_select_fusion, bf16[30,64,8]{0,2,1:T(8,128)(2,1)S(1)} %all-to-all-done.5), kind=kCustom, calls=%fused_computation.21 | custom fusion | flops 30720 | bytes 376832 | tf_op jit(solution)/shard_map/scatter-add | solution.py:50
  131.8 0.1 convert_element_type.52
  131.9 0.9 copy.100
  (16 shorter events, 0.2 us)
Async XLA Ops:
  2.3 10.3 %all-to-all-start = ((bf16[30,4,512]{2,0,1:T(8,128)(2,1)}), bf16[30,4,512]{2,0,1:T(8,128)(2,1)S(1)}, u32[]{:S(2)}, u32[]{:S(2)}) async-start(bf16[30,4,512]{2,0,1:T(8,128)(2,1)} %copy.74), calls=%async_computation | async-start | bytes 262144 | tf_op jit(solution)/shard_map/all_to_all | solution.py:37
  8.2 10.2 %copy-start = (s32[18,4]{0,1:T(4,128)S(1)}, s32[18,4]{0,1:T(4,128)}, u32[]{:S(2)}) copy-start(s32[18,4]{0,1:T(4,128)} %param.9) | copy-start | bytes 868
  8.2 10.4 %copy-start.2 = (s32[256]{0:T(256)S(1)}, s32[256]{0:T(256)}, u32[]{:S(2)}) copy-start(s32[256]{0:T(256)} %param.10) | copy-start | bytes 3076
  14.1 16.6 %all-to-all-start.1 = ((bf16[120,5,512]{2,1,0:T(8,128)(2,1)}), bf16[120,5,512]{2,1,0:T(8,128)(2,1)S(1)}, u32[]{:S(2)}, u32[]{:S(2)}) async-start(bf16[120,5,512]{2,1,0:T(8,128)(2,1)} %copy.75), calls=%async_computation.1 | async-start | bytes 1966080 | tf_op jit(solution)/shard_map/all_to_all | solution.py:41
  37.3 22.0 %copy-start.1 = (s32[512]{0:T(512)S(1)}, s32[512]{0:T(512)}, u32[]{:S(2)}) copy-start(s32[512]{0:T(512)} %param.11) | copy-start | bytes 6148
  44.9 24.9 %all-to-all-start.2 = ((bf16[30,64,8]{0,2,1:T(8,128)(2,1)}), bf16[30,64,8]{0,2,1:T(8,128)(2,1)S(1)}, u32[]{:S(2)}, u32[]{:S(2)}) async-start(bf16[30,64,8]{0,2,1:T(8,128)(2,1)} %convert_bitcast_fusion.5), calls=%async_computation.2 | async-start | bytes 262144 | tf_op jit(solution)/shard_map/all_to_all | solution.py:32
  110.9 17.2 %all-to-all-start.5 = ((bf16[30,64,8]{0,2,1:T(8,128)(2,1)}), bf16[30,64,8]{0,2,1:T(8,128)(2,1)S(1)}, u32[]{:S(2)}, u32[]{:S(2)}) async-start(bf16[30,64,8]{0,2,1:T(8,128)(2,1)} %convert_bitcast_fusion.4), calls=%async_computation.5 | async-start | bytes 262144 | tf_op jit(solution)/shard_map/all_to_all | solution.py:32
where the time goes:
time: 133 us
  waiting for transfers between devices  31.1 us (23%)
  starting transfers between devices  30.6 us (23%)
  local copies, waits for them, and re-layouts  23.9 us (18%)
  blocking collectives  22.5 us (17%)
  other arithmetic  12.3 us (9%)
  matrix products  11.4 us (9%)
    all_to_all x2, starting transfers between devices, send_partials(): lax.all_to_all(packed.astype(jnp.bfloat16), 'space', split_axis=1, concat...  21.3 us
    all_to_all x2, waiting for transfers between devices, send_partials(): lax.all_to_all(packed.astype(jnp.bfloat16), 'space', split_axis=1, concat...  19 us
    all_to_all x1, blocking collectives, mix_field(): lax.all_to_all(mixed_all, 'mode', split_axis=0, concat_axis=2, tiled=True)  15.3 us
    all_to_all x1, waiting for transfers between devices, mix_field(): lax.all_to_all(mixed_all, 'mode', split_axis=0, concat_axis=2, tiled=True)  12.1 us
    gather x4, local copies, waits for them, and re-layouts, block_rows(): picked = field_blocks[:, :, block_cols, :]  11.3 us
    dot_general x2, matrix products, block_rows(): jnp.einsum('mkcnd,kcnde->mce', picked, stiffness, preferred_element_type=...  10.8 us
    scatter-add x2, other arithmetic, one_apply(): summed = owned_flat.at[:, recv_row].add(arrived, mode='drop')  7.39 us
    all_to_all x1, blocking collectives, mix_field(): lax.all_to_all(field_now, 'mode', split_axis=1, concat_axis=0, tiled=True)  7.22 us
  transfers between devices with their start and end apart: 4, of which 3 were waited for; matrix products, arithmetic and copies ran while one was open for 5% of the time, Pallas kernels for 0%

commit v1 on v0

v1 whole, which is shorter than its diff:
```python
import functools

import jax
import jax.numpy as jnp
from jax import lax
from jax.experimental import pallas as pl
from jax.experimental.pallas import tpu as pltpu
from jax.sharding import PartitionSpec as P

LANES = 128
PAD = 32
QUARTERS = 4

VMEM = pl.BlockSpec(memory_space=pltpu.VMEM)
SMEM = pl.BlockSpec(memory_space=pltpu.SMEM)
ANY = pl.BlockSpec(memory_space=pl.ANY)
VMEM_LIMIT = 40 * 1024 * 1024


def call(kernel, outs, ins, in_specs, flops, scratch=(), grid=None, out_specs=None):
    out_bytes = sum(o.size * o.dtype.itemsize for o in outs)
    in_bytes = sum(a.size * a.dtype.itemsize for a in ins)
    extra = {} if grid is None else {"grid": grid}
    return pl.pallas_call(
        kernel,
        out_shape=outs,
        in_specs=in_specs,
        out_specs=out_specs or [VMEM] * len(outs),
        scratch_shapes=scratch,
        compiler_params=pltpu.CompilerParams(vmem_limit_bytes=VMEM_LIMIT),
        cost_estimate=pl.CostEstimate(flops=flops, bytes_accessed=in_bytes + out_bytes, transcendentals=0),
        **extra,
    )(*ins)


def one_hot(hit):
    return jnp.where(hit, 1.0, 0.0).astype(jnp.bfloat16)


def tables_kernel(cols_ref, coef_ref, send_ref, recv_ref, recv2_ref, g_ref, s_ref, s2_ref, r_ref, r2_ref):
    lanes = lax.broadcasted_iota(jnp.int32, g_ref.shape, 1)
    total = jnp.zeros(g_ref.shape, jnp.float32)
    for slot in range(cols_ref.shape[1]):
        total += jnp.where(cols_ref[:, slot:slot + 1] == lanes, coef_ref[:, slot:slot + 1], 0.0)
    g_ref[...] = total.astype(jnp.bfloat16)
    send = send_ref[...]
    s_ref[...] = one_hot(send == lax.broadcasted_iota(jnp.int32, s_ref.shape, 0))
    width = send.shape[1]
    rows = lax.broadcasted_iota(jnp.int32, (s2_ref.shape[0], width), 0)
    for quarter in range(QUARTERS):
        s2_ref[:, quarter * width:(quarter + 1) * width] = one_hot(send == rows * QUARTERS + quarter)
    for table, recv in ((r_ref, recv_ref), (r2_ref, recv2_ref)):
        wanted = recv[...]
        step = 256
        for at in range(0, table.shape[1], step):
            target = lax.broadcasted_iota(jnp.int32, (table.shape[0], step), 1) + at
            table[:, at:at + step] = one_hot(wanted == target)


def block_row(row, rows, cols_ref, mixed_ref, stiff_ref, first):
    terms = stiff_ref.shape[0]
    stored = cols_ref.shape[1]
    total = None
    for term in range(terms):
        picked = jnp.concatenate(
            [mixed_ref[cols_ref[row, c], term * rows:(term + 1) * rows, :] for c in range(stored)], axis=1
        )
        stiff = stiff_ref[term, first:first + stored].reshape(stored * LANES, LANES)
        product = jnp.dot(picked, stiff, preferred_element_type=jnp.float32)
        total = product if total is None else total + product
    return total


def mix(mixer, field, mixed_ref, width=256):
    for at in range(0, field.shape[1], width):
        mixed = jnp.dot(mixer, field[:, at:at + width], preferred_element_type=jnp.float32).astype(jnp.bfloat16)
        for part in range(width // LANES):
            mixed_ref[at // LANES + part] = mixed[:, part * LANES:(part + 1) * LANES]


def interface_rows(rows, cols_ref, mixed_ref, stiff_ref):
    stored = cols_ref.shape[1]
    owned_blocks = mixed_ref.shape[0]
    parts = [
        block_row(row, rows, cols_ref, mixed_ref, stiff_ref, (row - owned_blocks) * stored)
        for row in range(owned_blocks, cols_ref.shape[0])
    ]
    return jnp.concatenate(parts, axis=1).astype(jnp.bfloat16)


def interface_copy(blocks_ref, stiff_ref, sem):
    count = stiff_ref.shape[1]
    return pltpu.make_async_copy(blocks_ref.at[:, pl.ds(blocks_ref.shape[1] - count, count)], stiff_ref, sem)


def first_kernel(v0, v1, v2, v3, g_ref, s_ref, cols_ref, blocks_ref, mixed_ref, packed_ref, field_ref, stiff_ref, sem):
    copy = interface_copy(blocks_ref, stiff_ref, sem)
    copy.start()
    field_ref[...] = jnp.zeros_like(field_ref)
    for slot, source in enumerate((v0, v1, v2, v3)):
        field_ref[slot * PAD:slot * PAD + source.shape[0], :] = source[...]
    mix(g_ref[...], field_ref, mixed_ref)
    copy.wait()
    rows = field_ref.shape[0]
    part = interface_rows(rows, cols_ref, mixed_ref, stiff_ref)
    packed = lax.dot_general(s_ref[...], part, (((1,), (1,)), ((), ())), preferred_element_type=jnp.float32)
    packed_ref[...] = packed.astype(jnp.bfloat16)


def own_kernel(per_step, cols_ref, mixed_ref, stiff_ref, own_ref):
    stored = cols_ref.shape[1]
    rows = own_ref.shape[0]
    step = pl.program_id(0)
    for part in range(per_step):
        own_ref[:, part * LANES:(part + 1) * LANES] = block_row(
            step * per_step + part, rows, cols_ref, mixed_ref, stiff_ref, part * stored
        )


def second_kernel(own_ref, arrived_ref, r_ref, g_ref, s2_ref, cols_ref, blocks_ref,
                  first_ref, mixed_ref, packed_ref, field_ref, spread_ref, stiff_ref, sem):
    copy = interface_copy(blocks_ref, stiff_ref, sem)
    copy.start()
    arrived = arrived_ref[...].astype(jnp.float32).T.astype(jnp.bfloat16)
    width = 256
    for at in range(0, own_ref.shape[1], width):
        added = jnp.dot(arrived, r_ref[:, at:at + width], preferred_element_type=jnp.float32)
        field_ref[:, at:at + width] = (own_ref[:, at:at + width] + added).astype(jnp.bfloat16)
    first_ref[...] = field_ref[:first_ref.shape[0], :]
    rows = own_ref.shape[0]
    terms = stiff_ref.shape[0]
    mixer = jnp.concatenate([g_ref[term * rows:term * rows + PAD, :] for term in range(terms)], axis=0)
    mix(mixer, field_ref, mixed_ref)
    spread_ref[...] = jnp.zeros_like(spread_ref)
    copy.wait()
    part = interface_rows(PAD, cols_ref, mixed_ref, stiff_ref)
    wide = part.shape[1]
    for quarter in range(QUARTERS):
        spread_ref[quarter * PAD:(quarter + 1) * PAD, quarter * wide:(quarter + 1) * wide] = part
    packed = lax.dot_general(s2_ref[...], spread_ref[...], (((1,), (1,)), ((), ())), preferred_element_type=jnp.float32)
    packed_ref[...] = packed.astype(jnp.bfloat16)


def last_kernel(own_ref, arrived_ref, r2_ref, out_ref):
    turned = arrived_ref[...].astype(jnp.float32).T.astype(jnp.bfloat16)
    arrived = jnp.concatenate([turned[quarter * PAD:(quarter + 1) * PAD, :] for quarter in range(QUARTERS)], axis=1)
    width = 256
    for at in range(0, own_ref.shape[1], width):
        added = jnp.dot(arrived, r2_ref[:, at:at + width], preferred_element_type=jnp.float32)
        total = (own_ref[:, at:at + width] + added).astype(jnp.bfloat16)
        out_ref[:, at:at + width] = total[:out_ref.shape[0], :]


def local(groups, peers, modes_in, blocks, block_cols, send_slot, recv_row, mix_cols, mix_coef):
    bf16, f32 = jnp.bfloat16, jnp.float32
    terms, all_stored, blk, _ = blocks.shape
    out_blocks, stored = block_cols.shape
    modes_dev, owned = modes_in.shape
    modes = groups * modes_dev
    owned_blocks = owned // blk
    interface = send_slot.shape[0]
    slots = recv_row.shape[0]
    cap = slots // peers
    rows = groups * PAD
    me = lax.axis_index("mode")
    Shape = jax.ShapeDtypeStruct

    others = [
        lax.ppermute(modes_in, "mode", [((to + s) % groups, to) for to in range(groups)])
        for s in (2, 1, 3)
    ]
    fields = [modes_in, others[1], others[0], others[2]]

    def own_first(table, fill):
        split = table.reshape(terms, groups, modes_dev, table.shape[-1])
        turned = lax.dynamic_slice_in_dim(jnp.concatenate([split, split], axis=1), me, groups, axis=1)
        padded = jnp.pad(turned, ((0, 0), (0, 0), (0, PAD - modes_dev), (0, 0)), constant_values=fill)
        return padded.reshape(terms * rows, table.shape[-1])

    place = (mix_cols // modes_dev - me + groups) % groups * PAD + mix_cols % modes_dev
    place = jnp.where(mix_cols < modes, place, -1)
    halves = cap // QUARTERS
    recv2 = recv_row.reshape(peers, halves, QUARTERS).transpose(2, 0, 1).reshape(slots, 1)
    g, s, s2, r, r2 = call(
        tables_kernel,
        [Shape((terms * rows, rows), bf16), Shape((slots, interface), bf16),
         Shape((slots // QUARTERS, QUARTERS * interface), bf16),
         Shape((slots, owned), bf16), Shape((slots, owned), bf16)],
        [own_first(place, -1), own_first(mix_coef, 0.0), send_slot.reshape(1, interface),
         recv_row.reshape(slots, 1), recv2],
        [VMEM] * 5, flops=10 * slots * owned,
    )
    if_stored = (out_blocks - owned_blocks) * stored
    stiff_scratch = pltpu.VMEM((terms, if_stored, blk, blk), bf16)
    mixed, packed = call(
        first_kernel,
        [Shape((owned_blocks, terms * rows, blk), bf16), Shape((slots, rows), bf16)],
        [*fields, g, s, block_cols, blocks],
        [VMEM] * 6 + [SMEM, ANY], flops=2 * terms * rows * rows * owned,
        scratch=[pltpu.VMEM((rows, owned), bf16), stiff_scratch, pltpu.SemaphoreType.DMA],
    )
    arrived = lax.all_to_all(packed.reshape(peers, cap, rows), "space", split_axis=0, concat_axis=0, tiled=True)

    def own_rows(mixed_field, count):
        per_step = 2
        return call(
            functools.partial(own_kernel, per_step),
            [Shape((count, owned), f32)], [block_cols, mixed_field, blocks],
            [SMEM, VMEM, pl.BlockSpec((terms, per_step * stored, blk, blk), lambda i: (0, i, 0, 0))],
            flops=2 * terms * stored * owned_blocks * count * blk * blk,
            grid=(owned_blocks // per_step,),
            out_specs=[pl.BlockSpec((count, per_step * blk), lambda i: (0, i))],
        )[0]

    own = own_rows(mixed, rows)
    first_apply, mixed2, packed2 = call(
        second_kernel,
        [Shape((modes_dev, owned), bf16), Shape((owned_blocks, terms * PAD, blk), bf16),
         Shape((slots // QUARTERS, QUARTERS * PAD), bf16)],
        [own, arrived.reshape(slots, rows), r, g, s2, block_cols, blocks],
        [VMEM] * 5 + [SMEM, ANY], flops=2 * slots * rows * owned,
        scratch=[pltpu.VMEM((rows, owned), bf16), pltpu.VMEM((QUARTERS * PAD, QUARTERS * interface), bf16),
                 stiff_scratch, pltpu.SemaphoreType.DMA],
    )
    arrived2 = lax.all_to_all(
        packed2.reshape(peers, halves, QUARTERS * PAD), "space", split_axis=0, concat_axis=0, tiled=True
    )
    own2 = own_rows(mixed2, PAD)
    second_apply = call(
        last_kernel, [Shape((modes_dev, owned), bf16)],
        [own2, arrived2.reshape(slots // QUARTERS, QUARTERS * PAD), r2],
        [VMEM] * 3, flops=2 * slots * PAD * owned,
    )[0]
    return (first_apply, second_apply)


def solution(mesh):
    in_specs = (
        P("mode", "space"),
        P(None, "space", None, None),
        P("space", None),
        P("space"),
        P("space"),
        P(),
        P(),
    )
    out_specs = (P("mode", "space"), P("mode", "space"))
    body = functools.partial(local, mesh.shape["mode"], mesh.shape["space"])
    return jax.shard_map(body, mesh=mesh, in_specs=in_specs, out_specs=out_specs, check_vma=False)
```

time: 133 us -> 71.6 us (0.54)
  waiting for transfers between devices: 31.1 us -> 0.36 us
  Pallas kernels: 0 us -> 23.5 us
  blocking collectives: 22.5 us -> 0 us
  other arithmetic: 12.3 us -> 0.83 us
  matrix products: 11.4 us -> 0 us
  local copies, waits for them, and re-layouts: 23.9 us -> 17 us
  starting transfers between devices: 30.6 us -> 28.3 us
    all_to_all x4 -> x2, waiting for transfers between devices: 31.1 us -> 0.36 us  [the longest x1 0.35 us: local(): lax.all_to_all(packed.reshape(peers, cap, rows), 'space', split_axis=0, c...]
    pallas_call x0 -> x6, Pallas kernels: none -> 23.5 us  [call(): pl.pallas_call(kernel, out_shape=outs, in_specs=in_specs, out_specs=out_s...]
    all_to_all x2 -> x0, blocking collectives: 22.5 us -> none  [the longest x1 15.3 us: mix_field(): lax.all_to_all(mixed_all, 'mode', split_axis=0, concat_axis=2, tiled=True)]
    dot_general x4 -> x0, matrix products: 11.4 us -> none  [the longest x2 10.8 us: block_rows(): jnp.einsum('mkcnd,kcnde->mce', picked, stiffness, preferred_element_type=...]
    gather x4 -> x0, local copies, waits for them, and re-layouts: 11.3 us -> none  [block_rows(): picked = field_blocks[:, :, block_cols, :]]
    unnamed x14 -> x25, local copies, waits for them, and re-layouts: 3.63 us -> 13.7 us
    all_to_all x4 -> x2, starting transfers between devices: 30.6 us -> 23 us  [the longest x1 13 us: local(): lax.all_to_all(packed.reshape(peers, cap, rows), 'space', split_axis=0, c...]
    scatter-add x2 -> x0, other arithmetic: 7.39 us -> none  [one_apply(): summed = owned_flat.at[:, recv_row].add(arrived, mode='drop')]
  transfers between devices with their start and end apart: 4 -> 5, of which waited for: 3 -> 1; matrix products, arithmetic and copies ran while one was open for 5% -> 8% of each run, Pallas kernels for 0% -> 21%
where the time goes in v1:
time: 71.6 us; the launch traced here: 70.9 us
  starting transfers between devices  28.3 us (40%)
  Pallas kernels  23.5 us (33%)
  local copies, waits for them, and re-layouts  17 us (24%)
  between operations  0.88 us (1%)
  other arithmetic  0.83 us (1%)
    pallas_call x6, Pallas kernels, call(): pl.pallas_call(kernel, out_shape=outs, in_specs=in_specs, out_specs=out_s...  23.5 us
    unnamed x25, local copies, waits for them, and re-layouts  13.7 us
    all_to_all x1, starting transfers between devices, local(): lax.all_to_all(packed.reshape(peers, cap, rows), 'space', split_axis=0, c...  13 us
    all_to_all x1, starting transfers between devices, local(): lax.all_to_all(packed2.reshape(peers, halves, QUARTERS * PAD), 'space', s...  9.98 us
    ppermute x3, starting transfers between devices, local(): lax.ppermute(modes_in, 'mode', [((to + s) % groups, to) for to in range(g...  5.3 us
  transfers between devices with their start and end apart: 5, of which 1 were waited for; matrix products, arithmetic and copies ran while one was open for 8% of the time, Pallas kernels for 21%

profile of v1, /device:TPU:1, one launch (start us, length us, event | category | flops | bytes accessed | tf_op | source)
XLA Modules:
  0.0 70.9 jit_solution(7044255591199270260)
XLA Ops:
  0.6 0.0 copy-start.9
  0.6 0.0 copy-start.10
  0.6 3.8 %collective-permute-start.1 = (bf16[30,2048]{1,0:T(8,128)(2,1)}, bf16[30,2048]{1,0:T(8,128)(2,1)S(1)}, u32[]{:S(2)}, u32[]{:S(2)}) collective-permute-start(bf16[30,2048]{1,0:T(8,128)(2,1)} %v0.1), channel_id=1, source_target_pairs={{2,0},{3,1},{0,2},{1,3},{6,4},{7,5},{4,6},{5,7},{10,8},{11,9},{8,1... | collective-permute-start | bytes 368648 | tf_op jit(solution)/shard_map/ppermute | solution.py:169
  4.5 0.8 %collective-permute-start = (bf16[30,2048]{1,0:T(8,128)(2,1)}, bf16[30,2048]{1,0:T(8,128)(2,1)S(1)}, u32[]{:S(2)}, u32[]{:S(2)}) collective-permute-start(bf16[30,2048]{1,0:T(8,128)(2,1)} %v0.1), channel_id=1, source_target_pairs={{1,0},{2,1},{3,2},{0,3},{5,4},{6,5},{7,6},{4,7},{9,8},{10,9},{11,1... | collective-permute-start | bytes 368648 | tf_op jit(solution)/shard_map/ppermute | solution.py:169
  5.3 0.7 collective-permute-start.2
  5.9 0.8 %fusion.7 = s32[5,120,8]{1,2,0:T(8,128)S(1)} fusion(s32[5,120,8]{1,2,0:T(8,128)} %param.12, s32[]{:T(128)S(6)} %axis_index.12), kind=kLoop, calls=%fused_computation.16 | loop fusion | flops 139200 | bytes 38404 | tf_op jit(solution)/shard_map/jit(_where)/select_n | solution.py:181
  6.7 0.8 %reshape.42 = f32[5,4,30,8]{2,1,3,0:T(4,128)S(1)} reshape(f32[5,120,8]{1,2,0:T(8,128)} %param.13) | data formatting | bytes 38400 | tf_op jit(solution)/shard_map/reshape | solution.py:175
  7.6 0.8 %copy.47.cols_ref = s32[18,4]{1,0:T(8,128)S(1)} copy(s32[18,4]{0,1:T(4,128)} %param.9) | data formatting | bytes 576 | tf_op args[2]
  8.4 0.1 reshape.40
  8.5 0.8 %reshape.46 = s32[64,2,4]{2,1,0:T(2,128)S(1)} reshape(s32[512]{0:T(512)} %param.11) | data formatting | bytes 4096 | tf_op jit(solution)/shard_map/reshape | solution.py:183
  9.3 0.6 copy.43
  9.9 0.1 reshape.52.recv2_ref
  10.0 0.2 copy.51
  10.3 0.2 copy.50
  10.5 0.8 %copy.44.recv_ref = s32[512,1]{1,0:T(8,128)S(1)} copy(s32[512,1]{0,1:T(1,128)} %bitcast.19) | data formatting | bytes 4096 | tf_op jit(solution)/shard_map/reshape | solution.py:190
  11.4 0.0 copy-done.10
  11.4 2.3 %shard_map.86 = (bf16[640,128]{1,0:T(8,128)(2,1)S(1)}, bf16[512,256]{1,0:T(8,128)(2,1)S(1)}, bf16[128,1024]{1,0:T(8,128)(2,1)S(1)}, bf16[512,2048]{1,0:T(8,128)(2,1)S(1)}, bf16[512,2048]{1,0:T(8,128)(2,1)S(1)}) custom-call(s32[640,8]{1,0:T(8,128)S(1)} %bitcast.14, f32[640,8]{1,0:T(8,128)S(1)} %bitcast.13, s32[1,256]{1,0:T(1,128)S(1)} %bitcast.17, ...), custom_call_target="tpu_custom_call" | custom-call | flops 10485760 | bytes 4928512 | tf_op jit(solution)/shard_map/pallas_call | solution.py:24
  13.7 0.0 copy-start.3
  13.7 1.3 %copy-done.3 = bf16[512,2048]{1,0:T(8,128)(2,1)} copy-done((bf16[512,2048]{1,0:T(8,128)(2,1)}, bf16[512,2048]{1,0:T(8,128)(2,1)S(1)}, u32[]{:S(2)}) %copy-start.3) | copy-done | bytes 2097176
  15.0 0.0 copy-start.7
  15.0 0.7 %copy-done.7 = bf16[128,1024]{1,0:T(8,128)(2,1)} copy-done((bf16[128,1024]{1,0:T(8,128)(2,1)}, bf16[128,1024]{1,0:T(8,128)(2,1)S(1)}, u32[]{:S(2)}) %copy-start.7) | copy-done | bytes 262168
  15.8 0.0 collective-permute-done.1.v2
  15.8 0.0 collective-permute-done.v1
  15.8 0.0 collective-permute-done.2.v3
  15.8 0.0 copy-done.9
  15.8 3.7 %shard_map.87 = (bf16[16,640,128]{2,1,0:T(8,128)(2,1)S(1)}, bf16[512,128]{1,0:T(8,128)(2,1)}) custom-call(bf16[30,2048]{1,0:T(8,128)(2,1)S(1)} %copy-done.9, bf16[30,2048]{1,0:T(8,128)(2,1)S(1)} %collective-permute-done.v1, bf16[30,2048]{1,0:T(8,128)(2,1)S(1)} %collective-permute-done.1.v2, bf16[30,2048]{1,0:T(8,128)(2,1)} %collective-permute-done.2.v3, ...), custom_call_target="tpu_custom_call" | custom-call | flops 335544320 | bytes 15466784 | tf_op jit(solution)/shard_map/pallas_call | solution.py:24
  19.5 0.0 copy-start.1
  19.5 1.5 %copy-done.1 = bf16[16,640,128]{2,1,0:T(8,128)(2,1)} copy-done((bf16[16,640,128]{2,1,0:T(8,128)(2,1)}, bf16[16,640,128]{2,1,0:T(8,128)(2,1)S(1)}, u32[]{:S(2)}) %copy-start.1) | copy-done | bytes 2621464
  21.0 13.0 %all-to-all-start = ((bf16[64,8,128]{2,1,0:T(8,128)(2,1)}), bf16[64,8,128]{2,1,0:T(8,128)(2,1)S(1)}, u32[]{:S(2)}, u32[]{:S(2)}) async-start(bf16[64,8,128]{2,1,0:T(8,128)(2,1)} %bitcast.5), calls=%async_computation | async-start | bytes 262144 | tf_op jit(solution)/shard_map/all_to_all | solution.py:202
  34.0 0.0 copy-start.2
  34.0 1.7 %copy-done.2 = bf16[16,640,128]{2,1,0:T(8,128)(2,1)S(1)} copy-done((bf16[16,640,128]{2,1,0:T(8,128)(2,1)S(1)}, bf16[16,640,128]{2,1,0:T(8,128)(2,1)}, u32[]{:S(2)}) %copy-start.2) | copy-done | bytes 2621464
  35.7 8.3 %shard_map.88.own_ref = f32[128,2048]{1,0:T(8,128)S(1)} custom-call(s32[18,4]{1,0:T(8,128)S(1)} %copy.47.cols_ref, bf16[16,640,128]{2,1,0:T(8,128)(2,1)S(1)} %copy-done.2, bf16[5,72,128,128]{3,2,1,0:T(8,128)(2,1)} %stiff_ref.3), custom_call_target="tpu_custom_call" | custom-call | flops 1342177280 | bytes 15466784 | tf_op jit(solution)/shard_map/pallas_call | solution.py:24
  44.0 0.4 all-to-all-done
  44.3 0.0 copy-start.8
  44.3 0.9 %copy-done.8 = bf16[128,1024]{1,0:T(8,128)(2,1)S(1)} copy-done((bf16[128,1024]{1,0:T(8,128)(2,1)S(1)}, bf16[128,1024]{1,0:T(8,128)(2,1)}, u32[]{:S(2)}) %copy-start.8) | copy-done | bytes 262168
  45.3 3.8 %shard_map.89 = (bf16[30,2048]{1,0:T(8,128)(2,1)}, bf16[16,160,128]{2,1,0:T(8,128)(2,1)S(1)}, bf16[128,128]{1,0:T(8,128)(2,1)}) custom-call(f32[128,2048]{1,0:T(8,128)S(1)} %shard_map.88.own_ref, bf16[512,128]{1,0:T(8,128)(2,1)S(1)} %bitcast.15, bf16[512,2048]{1,0:T(8,128)(2,1)S(1)} %get-tuple-element.16.r_ref, ...), custom_call_target="tpu_custom_call" | custom-call | flops 268435456 | bytes 16310560 | tf_op jit(solution)/shard_map/pallas_call | solution.py:24
  49.1 0.0 copy-start.5
  49.1 0.8 %copy-done.5 = bf16[16,160,128]{2,1,0:T(8,128)(2,1)} copy-done((bf16[16,160,128]{2,1,0:T(8,128)(2,1)}, bf16[16,160,128]{2,1,0:T(8,128)(2,1)S(1)}, u32[]{:S(2)}) %copy-start.5) | copy-done | bytes 655384
  49.9 10.0 %all-to-all-start.1 = ((bf16[64,2,128]{2,1,0:T(2,128)(2,1)}), bf16[64,2,128]{2,1,0:T(2,128)(2,1)S(1)}, u32[]{:S(2)}, u32[]{:S(2)}) async-start(bf16[64,2,128]{2,1,0:T(2,128)(2,1)} %bitcast.7), calls=%async_computation.1 | async-start | bytes 65536 | tf_op jit(solution)/shard_map/all_to_all | solution.py:225
  59.9 0.0 copy-start
  59.9 4.3 %copy-done = bf16[5,72,128,128]{3,2,1,0:T(8,128)(2,1)S(1)} copy-done((bf16[5,72,128,128]{3,2,1,0:T(8,128)(2,1)S(1)}, bf16[5,72,128,128]{3,2,1,0:T(8,128)(2,1)}, u32[]{:S(2)}) %copy-start) | copy-done | bytes 11796504
  64.3 0.0 copy-start.6
  64.3 1.1 %copy-done.6 = bf16[16,160,128]{2,1,0:T(8,128)(2,1)S(1)} copy-done((bf16[16,160,128]{2,1,0:T(8,128)(2,1)S(1)}, bf16[16,160,128]{2,1,0:T(8,128)(2,1)}, u32[]{:S(2)}) %copy-start.6) | copy-done | bytes 655384
  65.4 0.0 copy-start.4
  65.4 4.3 %shard_map.90.own_ref = f32[32,2048]{1,0:T(8,128)S(1)} custom-call(s32[18,4]{1,0:T(8,128)S(1)} %copy.47.cols_ref, bf16[16,160,128]{2,1,0:T(8,128)(2,1)S(1)} %copy-done.6, bf16[5,72,128,128]{3,2,1,0:T(8,128)(2,1)S(1)} %copy-done), custom_call_target="tpu_custom_call" | custom-call | flops 335544320 | bytes 12714272 | tf_op jit(solution)/shard_map/pallas_call | solution.py:24
  69.7 0.0 all-to-all-done.1
  69.7 0.0 copy-done.4
  69.7 1.2 %shard_map.91 = bf16[30,2048]{1,0:T(8,128)(2,1)} custom-call(f32[32,2048]{1,0:T(8,128)S(1)} %shard_map.90.own_ref, bf16[128,128]{1,0:T(8,128)(2,1)S(1)} %bitcast.16, bf16[512,2048]{1,0:T(8,128)(2,1)S(1)} %copy-done.4), custom_call_target="tpu_custom_call" | custom-call | flops 67108864 | bytes 2514944 | tf_op jit(solution)/shard_map/pallas_call | solution.py:24
  (6 shorter events, 0.1 us)
Async XLA Ops:
  0.6 15.1 %copy-start.9 = (bf16[30,2048]{1,0:T(8,128)(2,1)S(1)}, bf16[30,2048]{1,0:T(8,128)(2,1)}, u32[]{:S(2)}) copy-start(bf16[30,2048]{1,0:T(8,128)(2,1)} %v0.1) | copy-start | bytes 368644
  0.6 10.7 %copy-start.10 = (s32[256]{0:T(256)S(1)}, s32[256]{0:T(256)}, u32[]{:S(2)}) copy-start(s32[256]{0:T(256)} %param.10) | copy-start | bytes 3076
  0.6 15.1 %collective-permute-start.1 = (bf16[30,2048]{1,0:T(8,128)(2,1)}, bf16[30,2048]{1,0:T(8,128)(2,1)S(1)}, u32[]{:S(2)}, u32[]{:S(2)}) collective-permute-start(bf16[30,2048]{1,0:T(8,128)(2,1)} %v0.1), channel_id=1, source_target_pairs={{2,0},{3,1},{0,2},{1,3},{6,4},{7,5},{4,6},{5,7},{10,8},{11,9},{8,1... | collective-permute-start | bytes 368648 | tf_op jit(solution)/shard_map/ppermute | solution.py:169
  4.5 11.3 %collective-permute-start = (bf16[30,2048]{1,0:T(8,128)(2,1)}, bf16[30,2048]{1,0:T(8,128)(2,1)S(1)}, u32[]{:S(2)}, u32[]{:S(2)}) collective-permute-start(bf16[30,2048]{1,0:T(8,128)(2,1)} %v0.1), channel_id=1, source_target_pairs={{1,0},{2,1},{3,2},{0,3},{5,4},{6,5},{7,6},{4,7},{9,8},{10,9},{11,1... | collective-permute-start | bytes 368648 | tf_op jit(solution)/shard_map/ppermute | solution.py:169
  5.3 10.5 %collective-permute-start.2 = (bf16[30,2048]{1,0:T(8,128)(2,1)}, bf16[30,2048]{1,0:T(8,128)(2,1)}, u32[]{:S(2)}, u32[]{:S(2)}) collective-permute-start(bf16[30,2048]{1,0:T(8,128)(2,1)} %v0.1), channel_id=1, source_target_pairs={{3,0},{0,1},{1,2},{2,3},{7,4},{4,5},{5,6},{6,7},{11,8},{8,9},{9,10... | collective-permute-start | bytes 368648 | tf_op jit(solution)/shard_map/ppermute | solution.py:169
  13.7 1.3 %copy-start.3 = (bf16[512,2048]{1,0:T(8,128)(2,1)}, bf16[512,2048]{1,0:T(8,128)(2,1)S(1)}, u32[]{:S(2)}) copy-start(bf16[512,2048]{1,0:T(8,128)(2,1)S(1)} %get-tuple-element.21.r2_ref) | copy-start | bytes 6291460
  15.0 0.7 %copy-start.7 = (bf16[128,1024]{1,0:T(8,128)(2,1)}, bf16[128,1024]{1,0:T(8,128)(2,1)S(1)}, u32[]{:S(2)}) copy-start(bf16[128,1024]{1,0:T(8,128)(2,1)S(1)} %get-tuple-element.17.s2_ref) | copy-start | bytes 786436
  19.5 1.5 %copy-start.1 = (bf16[16,640,128]{2,1,0:T(8,128)(2,1)}, bf16[16,640,128]{2,1,0:T(8,128)(2,1)S(1)}, u32[]{:S(2)}) copy-start(bf16[16,640,128]{2,1,0:T(8,128)(2,1)S(1)} %get-tuple-element.14.mixed_ref) | copy-start | bytes 7864324
  21.0 23.4 %all-to-all-start = ((bf16[64,8,128]{2,1,0:T(8,128)(2,1)}), bf16[64,8,128]{2,1,0:T(8,128)(2,1)S(1)}, u32[]{:S(2)}, u32[]{:S(2)}) async-start(bf16[64,8,128]{2,1,0:T(8,128)(2,1)} %bitcast.5), calls=%async_computation | async-start | bytes 262144 | tf_op jit(solution)/shard_map/all_to_all | solution.py:202
  34.0 1.7 %copy-start.2 = (bf16[16,640,128]{2,1,0:T(8,128)(2,1)S(1)}, bf16[16,640,128]{2,1,0:T(8,128)(2,1)}, u32[]{:S(2)}) copy-start(bf16[16,640,128]{2,1,0:T(8,128)(2,1)} %copy-done.1) | copy-start | bytes 7864324
  44.3 1.0 %copy-start.8 = (bf16[128,1024]{1,0:T(8,128)(2,1)S(1)}, bf16[128,1024]{1,0:T(8,128)(2,1)}, u32[]{:S(2)}) copy-start(bf16[128,1024]{1,0:T(8,128)(2,1)} %copy-done.7) | copy-start | bytes 786436
  49.1 0.8 %copy-start.5 = (bf16[16,160,128]{2,1,0:T(8,128)(2,1)}, bf16[16,160,128]{2,1,0:T(8,128)(2,1)S(1)}, u32[]{:S(2)}) copy-start(bf16[16,160,128]{2,1,0:T(8,128)(2,1)S(1)} %get-tuple-element.19.mixed_ref) | copy-start | bytes 1966084
  49.9 19.7 %all-to-all-start.1 = ((bf16[64,2,128]{2,1,0:T(2,128)(2,1)}), bf16[64,2,128]{2,1,0:T(2,128)(2,1)S(1)}, u32[]{:S(2)}, u32[]{:S(2)}) async-start(bf16[64,2,128]{2,1,0:T(2,128)(2,1)} %bitcast.7), calls=%async_computation.1 | async-start | bytes 65536 | tf_op jit(solution)/shard_map/all_to_all | solution.py:225
  59.9 4.4 %copy-start = (bf16[5,72,128,128]{3,2,1,0:T(8,128)(2,1)S(1)}, bf16[5,72,128,128]{3,2,1,0:T(8,128)(2,1)}, u32[]{:S(2)}) copy-start(bf16[5,72,128,128]{3,2,1,0:T(8,128)(2,1)} %stiff_ref.3) | copy-start | bytes 35389444
  64.3 1.1 %copy-start.6 = (bf16[16,160,128]{2,1,0:T(8,128)(2,1)S(1)}, bf16[16,160,128]{2,1,0:T(8,128)(2,1)}, u32[]{:S(2)}) copy-start(bf16[16,160,128]{2,1,0:T(8,128)(2,1)} %copy-done.5) | copy-start | bytes 1966084
  65.4 4.3 %copy-start.4 = (bf16[512,2048]{1,0:T(8,128)(2,1)S(1)}, bf16[512,2048]{1,0:T(8,128)(2,1)}, u32[]{:S(2)}) copy-start(bf16[512,2048]{1,0:T(8,128)(2,1)} %copy-done.3) | copy-start | bytes 6291460

commit v2 on v0

v2 whole, which is shorter than its diff:
```python
import functools

import jax
import jax.numpy as jnp
from jax import lax
from jax.experimental import pallas as pl
from jax.experimental.pallas import tpu as pltpu
from jax.sharding import PartitionSpec as P

LANES = 128
PAD = 32
QUARTERS = 4
WIDTH = 256

VMEM = pl.BlockSpec(memory_space=pltpu.VMEM)
SMEM = pl.BlockSpec(memory_space=pltpu.SMEM)
HBM = pl.BlockSpec(memory_space=pltpu.HBM)
VMEM_LIMIT = 48 * 1024 * 1024
bf16, f32, i32 = jnp.bfloat16, jnp.float32, jnp.int32


def call(kernel, outs, ins, in_specs, out_specs, flops, scratch=()):
    moved = sum(a.size * a.dtype.itemsize for a in [*outs, *ins])
    return pl.pallas_call(
        kernel,
        out_shape=outs,
        in_specs=in_specs,
        out_specs=out_specs,
        scratch_shapes=scratch,
        compiler_params=pltpu.CompilerParams(vmem_limit_bytes=VMEM_LIMIT),
        cost_estimate=pl.CostEstimate(flops=flops, bytes_accessed=moved, transcendentals=0),
    )(*ins)


def one_hot(hit):
    return jnp.where(hit, 1.0, 0.0).astype(bf16)


def dot(a, b):
    return jnp.dot(a, b, preferred_element_type=f32)


def dot_t(a, b):
    return lax.dot_general(a, b, (((1,), (1,)), ((), ())), preferred_element_type=f32)


def padded_place(modes, groups, modes_dev):
    place = modes
    for group in range(1, groups):
        place += jnp.where(modes >= group * modes_dev, PAD - modes_dev, 0)
    return place


def mixer_columns(term, groups, cols_ref, coef_ref):
    modes = cols_ref.shape[2]
    cols = cols_ref[term]
    place = jnp.where(cols < modes, padded_place(cols, groups, modes // groups), -1)
    coef = coef_ref[term]
    want = lax.broadcasted_iota(i32, (groups * PAD, modes), 0)
    total = jnp.zeros(want.shape, f32)
    for slot in range(cols.shape[0]):
        total += jnp.where(place[slot:slot + 1, :] == want, coef[slot:slot + 1, :], 0.0)
    return total.astype(bf16)


def mixer_kernel(groups, cols_ref, coef_ref, g_ref):
    modes = cols_ref.shape[2]
    rows = groups * PAD
    out_mode = lax.broadcasted_iota(i32, (rows, modes), 1)
    spread = one_hot(padded_place(out_mode, groups, modes // groups) == lax.broadcasted_iota(i32, (rows, modes), 0))
    for term in range(cols_ref.shape[0]):
        g_ref[term * rows:(term + 1) * rows, :] = dot_t(spread, mixer_columns(term, groups, cols_ref, coef_ref)).astype(bf16)


def receive_table(recv_ref, r_ref):
    slots = recv_ref.shape[1]
    turned = jnp.broadcast_to(recv_ref[...].astype(f32), (LANES, slots)).T
    wanted = turned[:, :1].astype(i32)
    for at in range(0, r_ref.shape[1], WIDTH):
        r_ref[:, at:at + WIDTH] = one_hot(wanted == lax.broadcasted_iota(i32, (slots, WIDTH), 1) + at)


def block_row(row, rows, cols_ref, mixed_ref, stiff):
    terms, stored = stiff.shape[:2]
    picked = jnp.concatenate(
        [
            mixed_ref[cols_ref[c, row], term * rows:(term + 1) * rows, :]
            for term in range(terms)
            for c in range(stored)
        ],
        axis=1,
    )
    return dot(picked, stiff.reshape(terms * stored * LANES, LANES))


def mix(mixer, field_ref, mixed_ref):
    rows = field_ref.shape[0] * field_ref.shape[1]
    for at in range(0, field_ref.shape[2], WIDTH):
        field = field_ref[:, :, at:at + WIDTH].reshape(rows, WIDTH)
        mixed = dot(mixer, field).astype(bf16)
        for part in range(WIDTH // LANES):
            mixed_ref[at // LANES + part] = mixed[:, part * LANES:(part + 1) * LANES]


def first_kernel(groups, v0, v1, v2, v3, g_ref, send_ref, cols_ref, blocks_ref,
                 packed_ref, own_out, token_ref, field_ref, mixed_ref, own_ref, sems):
    me = lax.axis_index("mode")
    rows = groups * PAD
    stored, out_blocks = cols_ref.shape
    owned_blocks = mixed_ref.shape[0]
    field_ref[...] = jnp.zeros_like(field_ref)
    for slot, source in enumerate((v0, v1, v2, v3)):
        field_ref[lax.rem(me + slot, groups), :source.shape[0], :] = source[...]
    mix(g_ref[...], field_ref, mixed_ref)

    def row_of(row):
        return block_row(row, rows, cols_ref, mixed_ref, blocks_ref[:, row * stored:(row + 1) * stored])

    copies = []
    for row in range(owned_blocks):
        own_ref[:, row * LANES:(row + 1) * LANES] = row_of(row)
        if row % 4 == 3:
            at = pl.ds((row - 3) * LANES, 4 * LANES)
            copies.append(pltpu.make_async_copy(own_ref.at[:, at], own_out.at[:, at], sems.at[row // 4]))
            copies[-1].start()
    part = jnp.concatenate([row_of(row) for row in range(owned_blocks, out_blocks)], axis=1).astype(bf16)
    slots = packed_ref.shape[0]
    place = one_hot(send_ref[...] == lax.broadcasted_iota(i32, (slots, send_ref.shape[1]), 0))
    packed_ref[...] = dot_t(place, part).astype(bf16)
    token_ref[...] = jnp.zeros_like(token_ref)
    for copy in copies:
        copy.wait()


def between_kernel(groups, token_ref, cols_ref, coef_ref, recv_ref, r_ref, g2_ref):
    me = lax.axis_index("mode")
    modes = cols_ref.shape[2]
    modes_dev = modes // groups
    row = lax.broadcasted_iota(i32, (PAD, modes), 0)
    mine = one_hot((lax.broadcasted_iota(i32, (PAD, modes), 1) == row + me * modes_dev) & (row < modes_dev))
    for term in range(cols_ref.shape[0]):
        g2_ref[term * PAD:(term + 1) * PAD, :] = dot_t(mine, mixer_columns(term, groups, cols_ref, coef_ref)).astype(bf16)
    receive_table(recv_ref, r_ref)


def second_kernel(groups, own_ref, arrived_ref, r_ref, g2_ref, send_ref, cols_ref, blocks_ref,
                  first_ref, mixed_out, packed_ref, field_ref, mixed_ref, spread_ref, stiff_ref, sem, sems):
    me = lax.axis_index("mode")
    stored, out_blocks = cols_ref.shape
    owned_blocks = mixed_ref.shape[0]
    count = stiff_ref.shape[1]
    fetch = pltpu.make_async_copy(blocks_ref.at[:, pl.ds(owned_blocks * stored, count)], stiff_ref, sem)
    fetch.start()
    arrived = arrived_ref[...].astype(f32).T.astype(bf16)
    for at in range(0, own_ref.shape[1], WIDTH):
        total = own_ref[:, at:at + WIDTH] + dot(arrived, r_ref[:, at:at + WIDTH])
        field_ref[:, :, at:at + WIDTH] = total.astype(bf16).reshape(groups, PAD, WIDTH)
    first_ref[...] = field_ref[me, :first_ref.shape[0], :]
    mix(g2_ref[...], field_ref, mixed_ref)
    keep = pltpu.make_async_copy(mixed_ref, mixed_out, sems)
    keep.start()
    spread_ref[...] = jnp.zeros_like(spread_ref)
    width = send_ref.shape[1]
    send = send_ref[...]
    lines = lax.broadcasted_iota(i32, (packed_ref.shape[0], width), 0) * QUARTERS
    place = jnp.concatenate([one_hot(send == lines + quarter) for quarter in range(QUARTERS)], axis=1)
    fetch.wait()
    part = jnp.concatenate(
        [
            block_row(row, PAD, cols_ref, mixed_ref, stiff_ref[:, (row - owned_blocks) * stored:(row - owned_blocks + 1) * stored])
            for row in range(owned_blocks, out_blocks)
        ],
        axis=1,
    ).astype(bf16)
    for quarter in range(QUARTERS):
        spread_ref[quarter * PAD:(quarter + 1) * PAD, quarter * width:(quarter + 1) * width] = part
    packed_ref[...] = dot_t(place, spread_ref[...]).astype(bf16)
    keep.wait()


def own_kernel(steps, cols_ref, recv_ref, mixed_hbm, blocks_ref, own_ref, r_ref, mixed_ref, stiff_ref, sem, sems):
    stored = cols_ref.shape[0]
    owned_blocks = mixed_ref.shape[0]
    per = owned_blocks // steps
    fetch = pltpu.make_async_copy(mixed_hbm, mixed_ref, sem)
    fetch.start()
    copies = []
    for step in range(steps):
        at = pl.ds(step * per * stored, per * stored)
        copies.append(pltpu.make_async_copy(blocks_ref.at[:, at], stiff_ref.at[:, at], sems.at[step]))
        copies[-1].start()
    receive_table(recv_ref, r_ref)
    fetch.wait()
    for step in range(steps):
        copies[step].wait()
        for row in range(step * per, (step + 1) * per):
            own_ref[:, row * LANES:(row + 1) * LANES] = block_row(
                row, PAD, cols_ref, mixed_ref, stiff_ref[:, row * stored:(row + 1) * stored]
            )


def last_kernel(own_ref, arrived_ref, r_ref, out_ref, slots_ref):
    arrived = arrived_ref[...].astype(f32)
    lines = arrived.shape[0]
    for quarter in range(QUARTERS):
        turned = pltpu.roll(arrived, (QUARTERS - quarter) % QUARTERS * PAD, 1)
        slots_ref[pl.ds(quarter, lines, stride=QUARTERS), :] = turned
    by_slot = slots_ref[...].T[:PAD, :].astype(bf16)
    for at in range(0, own_ref.shape[1], WIDTH):
        total = own_ref[:, at:at + WIDTH] + dot(by_slot, r_ref[:, at:at + WIDTH])
        out_ref[:, at:at + WIDTH] = total.astype(bf16)[:out_ref.shape[0], :]


def local(groups, peers, modes_in, blocks, block_cols, send_slot, recv_row, mix_cols, mix_coef):
    terms, all_stored, blk, _ = blocks.shape
    out_blocks, stored = block_cols.shape
    modes_dev, owned = modes_in.shape
    owned_blocks = owned // blk
    interface = send_slot.shape[0]
    slots = recv_row.shape[0]
    cap = slots // peers
    rows = groups * PAD
    lines = slots // QUARTERS
    Shape = jax.ShapeDtypeStruct
    dma = pltpu.SemaphoreType.DMA

    others = {
        s: lax.ppermute(modes_in, "mode", [((to + s) % groups, to) for to in range(groups)])
        for s in (2, 1, 3)
    }
    fields = [modes_in, others[1], others[2], others[3]]
    cols_t = block_cols.T
    mix_cols_t, mix_coef_t = mix_cols.transpose(0, 2, 1), mix_coef.transpose(0, 2, 1)
    send, recv = send_slot.reshape(1, interface), recv_row.reshape(1, slots)

    g = call(
        functools.partial(mixer_kernel, groups), [Shape((terms * rows, rows), bf16)],
        [mix_cols_t, mix_coef_t], [VMEM] * 2, [VMEM], flops=10**6,
    )[0]
    field_scratch = pltpu.VMEM((groups, PAD, owned), bf16)
    packed, own, token = call(
        functools.partial(first_kernel, groups),
        [Shape((slots, rows), bf16), Shape((rows, owned), f32), Shape((8, LANES), f32)],
        [*fields, g, send, cols_t, blocks],
        [VMEM] * 6 + [SMEM, VMEM], [VMEM, HBM, VMEM],
        flops=2 * terms * stored * out_blocks * rows * blk * blk,
        scratch=[field_scratch, pltpu.VMEM((owned_blocks, terms * rows, blk), bf16),
                 pltpu.VMEM((rows, owned), f32), dma((owned_blocks // 4,))],
    )
    arrived = lax.all_to_all(packed.reshape(peers, cap, rows), "space", split_axis=0, concat_axis=0, tiled=True)
    r, g2 = call(
        functools.partial(between_kernel, groups), [Shape((slots, owned), bf16), Shape((terms * PAD, rows), bf16)],
        [token, mix_cols_t, mix_coef_t, recv], [VMEM] * 4, [VMEM] * 2, flops=10**9,
    )
    first_apply, mixed2, packed2 = call(
        functools.partial(second_kernel, groups),
        [Shape((modes_dev, owned), bf16), Shape((owned_blocks, terms * PAD, blk), bf16), Shape((lines, QUARTERS * PAD), bf16)],
        [own, arrived.reshape(slots, rows), r, g2, send, cols_t, blocks],
        [VMEM] * 5 + [SMEM, HBM], [VMEM, HBM, VMEM], flops=2 * slots * rows * owned,
        scratch=[field_scratch, pltpu.VMEM((owned_blocks, terms * PAD, blk), bf16),
                 pltpu.VMEM((QUARTERS * PAD, QUARTERS * interface), bf16),
                 pltpu.VMEM((terms, (out_blocks - owned_blocks) * stored, blk, blk), bf16), dma, dma],
    )
    arrived2 = lax.all_to_all(
        packed2.reshape(peers, cap // QUARTERS, QUARTERS * PAD), "space", split_axis=0, concat_axis=0, tiled=True
    )
    steps = 8
    own2, r2 = call(
        functools.partial(own_kernel, steps), [Shape((PAD, owned), f32), Shape((slots, owned), bf16)],
        [cols_t, recv, mixed2, blocks], [SMEM, VMEM, HBM, HBM], [VMEM] * 2,
        flops=2 * terms * stored * owned_blocks * PAD * blk * blk,
        scratch=[pltpu.VMEM((owned_blocks, terms * PAD, blk), bf16),
                 pltpu.VMEM((terms, owned_blocks * stored, blk, blk), bf16), dma, dma((steps,))],
    )
    second_apply = call(
        last_kernel, [Shape((modes_dev, owned), bf16)],
        [own2, arrived2.reshape(lines, QUARTERS * PAD), r2], [VMEM] * 3, [VMEM],
        flops=2 * slots * PAD * owned, scratch=[pltpu.VMEM((slots, QUARTERS * PAD), f32)],
    )[0]
    return (first_apply, second_apply)


def solution(mesh):
    in_specs = (
        P("mode", "space"),
        P(None, "space", None, None),
        P("space", None),
        P("space"),
        P("space"),
        P(),
        P(),
    )
    out_specs = (P("mode", "space"), P("mode", "space"))
    body = functools.partial(local, mesh.shape["mode"], mesh.shape["space"])
    return jax.shard_map(body, mesh=mesh, in_specs=in_specs, out_specs=out_specs, check_vma=False)
```

time: 133 us -> 67.1 us (0.50)
  blocking collectives: 22.5 us -> 0 us
  Pallas kernels: 0 us -> 20.9 us
  local copies, waits for them, and re-layouts: 23.9 us -> 5.69 us
  waiting for transfers between devices: 31.1 us -> 17.4 us
  other arithmetic: 12.3 us -> 0 us
  matrix products: 11.4 us -> 0 us
  starting transfers between devices: 30.6 us -> 21.9 us
    all_to_all x2 -> x0, blocking collectives: 22.5 us -> none  [the longest x1 15.3 us: mix_field(): lax.all_to_all(mixed_all, 'mode', split_axis=0, concat_axis=2, tiled=True)]
    pallas_call x0 -> x6, Pallas kernels: none -> 20.9 us  [call(): pl.pallas_call(kernel, out_shape=outs, in_specs=in_specs, out_specs=out_s...]
    all_to_all x4 -> x2, waiting for transfers between devices: 31.1 us -> 12.6 us  [the longest x1 9.66 us: local(): lax.all_to_all(packed.reshape(peers, cap, rows), 'space', split_axis=0, c...]
    all_to_all x4 -> x2, starting transfers between devices: 30.6 us -> 16.6 us  [the longest x1 11.7 us: local(): lax.all_to_all(packed.reshape(peers, cap, rows), 'space', split_axis=0, c...]
    dot_general x4 -> x0, matrix products: 11.4 us -> none  [the longest x2 10.8 us: block_rows(): jnp.einsum('mkcnd,kcnde->mce', picked, stiffness, preferred_element_type=...]
    gather x4 -> x0, local copies, waits for them, and re-layouts: 11.3 us -> none  [block_rows(): picked = field_blocks[:, :, block_cols, :]]
    scatter-add x2 -> x0, other arithmetic: 7.39 us -> none  [one_apply(): summed = owned_flat.at[:, recv_row].add(arrived, mode='drop')]
    ppermute x0 -> x3, starting transfers between devices: none -> 5.3 us  [local(): lax.ppermute(modes_in, 'mode', [((to + s) % groups, to) for to in range(g...]
  transfers between devices with their start and end apart: 4 -> 5, of which waited for: 3 -> 4; matrix products, arithmetic and copies ran while one was open for 5% -> 0% of each run, Pallas kernels for 0% -> 9%
where the time goes in v2:
time: 67.1 us; the launch traced here: 66.7 us
  starting transfers between devices  21.9 us (33%)
  Pallas kernels  20.9 us (31%)
  waiting for transfers between devices  17.4 us (26%)
  local copies, waits for them, and re-layouts  5.69 us (8%)
  between operations  0.75 us (1%)
    pallas_call x6, Pallas kernels, call(): pl.pallas_call(kernel, out_shape=outs, in_specs=in_specs, out_specs=out_s...  20.9 us
    all_to_all x1, starting transfers between devices, local(): lax.all_to_all(packed.reshape(peers, cap, rows), 'space', split_axis=0, c...  11.7 us
    all_to_all x1, waiting for transfers between devices, local(): lax.all_to_all(packed.reshape(peers, cap, rows), 'space', split_axis=0, c...  9.66 us
    unnamed x24, local copies, waits for them, and re-layouts  5.69 us
    ppermute x3, starting transfers between devices, local(): lax.ppermute(modes_in, 'mode', [((to + s) % groups, to) for to in range(g...  5.3 us
    all_to_all x1, starting transfers between devices, local(): lax.all_to_all(packed2.reshape(peers, cap // QUARTERS, QUARTERS * PAD), '...  4.89 us
    ppermute x3, waiting for transfers between devices, local(): lax.ppermute(modes_in, 'mode', [((to + s) % groups, to) for to in range(g...  4.83 us
    all_to_all x1, waiting for transfers between devices, local(): lax.all_to_all(packed2.reshape(peers, cap // QUARTERS, QUARTERS * PAD), '...  2.9 us
  transfers between devices with their start and end apart: 5, of which 4 were waited for; matrix products, arithmetic and copies ran while one was open for 0% of the time, Pallas kernels for 9%

profile of v2, /device:TPU:1, one launch (start us, length us, event | category | flops | bytes accessed | tf_op | source)
XLA Modules:
  0.0 66.7 jit_solution(4417879581875795953)
XLA Ops:
  0.6 3.8 %collective-permute-start.1 = (bf16[30,2048]{1,0:T(8,128)(2,1)}, bf16[30,2048]{1,0:T(8,128)(2,1)S(1)}, u32[]{:S(2)}, u32[]{:S(2)}) collective-permute-start(bf16[30,2048]{1,0:T(8,128)(2,1)} %v0.1), channel_id=1, source_target_pairs={{2,0},{3,1},{0,2},{1,3},{6,4},{7,5},{4,6},{5,7},{10,8},{11,9},{8,1... | collective-permute-start | bytes 368648 | tf_op jit(solution)/shard_map/ppermute | solution.py:228
  4.5 0.8 %collective-permute-start = (bf16[30,2048]{1,0:T(8,128)(2,1)}, bf16[30,2048]{1,0:T(8,128)(2,1)S(1)}, u32[]{:S(2)}, u32[]{:S(2)}) collective-permute-start(bf16[30,2048]{1,0:T(8,128)(2,1)} %v0.1), channel_id=1, source_target_pairs={{1,0},{2,1},{3,2},{0,3},{5,4},{6,5},{7,6},{4,7},{9,8},{10,9},{11,1... | collective-permute-start | bytes 368648 | tf_op jit(solution)/shard_map/ppermute | solution.py:228
  5.2 0.7 %collective-permute-start.2 = (bf16[30,2048]{1,0:T(8,128)(2,1)}, bf16[30,2048]{1,0:T(8,128)(2,1)S(1)}, u32[]{:S(2)}, u32[]{:S(2)}) collective-permute-start(bf16[30,2048]{1,0:T(8,128)(2,1)} %v0.1), channel_id=1, source_target_pairs={{3,0},{0,1},{1,2},{2,3},{7,4},{4,5},{5,6},{6,7},{11,8},{8,9},{9,10... | collective-permute-start | bytes 368648 | tf_op jit(solution)/shard_map/ppermute | solution.py:228
  5.9 0.0 copy-start.3
  5.9 0.7 %copy-done.3 = s32[5,120,8]{1,2,0:T(8,128)S(1)} copy-done((s32[5,120,8]{1,2,0:T(8,128)S(1)}, s32[5,120,8]{1,2,0:T(8,128)}, u32[]{:S(2)}) %copy-start.3) | copy-done | bytes 19224
  6.7 0.0 copy-start.5
  6.7 0.7 %copy-done.5 = f32[5,120,8]{1,2,0:T(8,128)S(1)} copy-done((f32[5,120,8]{1,2,0:T(8,128)S(1)}, f32[5,120,8]{1,2,0:T(8,128)}, u32[]{:S(2)}) %copy-start.5) | copy-done | bytes 19224
  7.4 0.4 shard_map.86.g_ref
  7.8 0.0 collective-permute-done.1.v2
  7.8 3.0 %collective-permute-done.v1 = bf16[30,2048]{1,0:T(8,128)(2,1)S(1)} collective-permute-done((bf16[30,2048]{1,0:T(8,128)(2,1)}, bf16[30,2048]{1,0:T(8,128)(2,1)S(1)}, u32[]{:S(2)}, u32[]{:S(2)}) %collective-permute-start) | collective-permute-done | bytes 122912 | tf_op jit(solution)/shard_map/ppermute | solution.py:228
  10.8 1.8 %collective-permute-done.2.v3 = bf16[30,2048]{1,0:T(8,128)(2,1)S(1)} collective-permute-done((bf16[30,2048]{1,0:T(8,128)(2,1)}, bf16[30,2048]{1,0:T(8,128)(2,1)S(1)}, u32[]{:S(2)}, u32[]{:S(2)}) %collective-permute-start.2) | collective-permute-done | bytes 122912 | tf_op jit(solution)/shard_map/ppermute | solution.py:228
  12.6 0.0 copy-start.2
  12.6 0.9 %copy-done.2 = bf16[30,2048]{1,0:T(8,128)(2,1)S(1)} copy-done((bf16[30,2048]{1,0:T(8,128)(2,1)S(1)}, bf16[30,2048]{1,0:T(8,128)(2,1)}, u32[]{:S(2)}) %copy-start.2) | copy-done | bytes 122904
  13.6 0.0 copy-start.7
  13.6 0.7 %copy-done.7 = s32[18,4]{0,1:T(4,128)S(1)} copy-done((s32[18,4]{0,1:T(4,128)S(1)}, s32[18,4]{0,1:T(4,128)}, u32[]{:S(2)}) %copy-start.7) | copy-done | bytes 312
  14.2 0.0 copy-start.9
  14.2 0.7 %copy-done.9 = s32[256]{0:T(256)S(1)} copy-done((s32[256]{0:T(256)S(1)}, s32[256]{0:T(256)}, u32[]{:S(2)}) %copy-start.9) | copy-done | bytes 1048
  14.9 0.0 copy-start.4
  14.9 0.0 copy-start.6
  14.9 0.0 copy-start.11
  14.9 10.2 %shard_map.87 = (bf16[512,128]{1,0:T(8,128)(2,1)}, f32[128,2048]{1,0:T(8,128)S(1)}, f32[8,128]{1,0:T(8,128)S(1)}) custom-call(bf16[30,2048]{1,0:T(8,128)(2,1)S(1)} %copy-done.2, bf16[30,2048]{1,0:T(8,128)(2,1)S(1)} %collective-permute-done.v1, bf16[30,2048]{1,0:T(8,128)(2,1)S(1)} %collective-permute-done.1.v2, ...), custom_call_target="tpu_custom_call" | custom-call | flops 1509949440 | bytes 13636896 | tf_op jit(solution)/shard_map/pallas_call | solution.py:24
  25.1 0.0 copy-start.8
  25.1 0.0 copy-start.10
  25.1 11.7 %all-to-all-start = ((bf16[64,8,128]{2,1,0:T(8,128)(2,1)}), bf16[64,8,128]{2,1,0:T(8,128)(2,1)S(1)}, u32[]{:S(2)}, u32[]{:S(2)}) async-start(bf16[64,8,128]{2,1,0:T(8,128)(2,1)} %bitcast.4), calls=%async_computation | async-start | bytes 262144 | tf_op jit(solution)/shard_map/all_to_all | solution.py:250
  36.8 0.0 copy-done.4
  36.8 0.0 copy-done.6
  36.9 0.0 copy-done.11
  36.9 0.7 shard_map.88
  37.5 9.7 %all-to-all-done = bf16[64,8,128]{2,1,0:T(8,128)(2,1)S(1)} async-done(((bf16[64,8,128]{2,1,0:T(8,128)(2,1)}), bf16[64,8,128]{2,1,0:T(8,128)(2,1)S(1)}, u32[]{:S(2)}, u32[]{:S(2)}) %all-to-all-start) | async-done | bytes 131104 | tf_op jit(solution)/shard_map/all_to_all | solution.py:250
  47.2 0.0 copy-done.8
  47.2 0.0 copy-done.10
  47.2 3.2 %shard_map.89 = (bf16[30,2048]{1,0:T(8,128)(2,1)}, bf16[16,160,128]{2,1,0:T(8,128)(2,1)S(1)}, bf16[128,128]{1,0:T(8,128)(2,1)}) custom-call(f32[128,2048]{1,0:T(8,128)S(1)} %get-tuple-element.12.own_ref, bf16[512,128]{1,0:T(8,128)(2,1)S(1)} %bitcast.9, bf16[512,2048]{1,0:T(8,128)(2,1)S(1)} %get-tuple-element.15.r_ref, ...), custom_call_target="tpu_custom_call" | custom-call | flops 268435456 | bytes 15926560 | tf_op jit(solution)/shard_map/pallas_call | solution.py:24
  50.4 0.0 copy-start
  50.4 0.9 %copy-done = bf16[16,160,128]{2,1,0:T(8,128)(2,1)} copy-done((bf16[16,160,128]{2,1,0:T(8,128)(2,1)}, bf16[16,160,128]{2,1,0:T(8,128)(2,1)S(1)}, u32[]{:S(2)}) %copy-start) | copy-done | bytes 655384
  51.3 4.9 %all-to-all-start.1 = ((bf16[64,2,128]{2,1,0:T(2,128)(2,1)}), bf16[64,2,128]{2,1,0:T(2,128)(2,1)S(1)}, u32[]{:S(2)}, u32[]{:S(2)}) async-start(bf16[64,2,128]{2,1,0:T(2,128)(2,1)} %bitcast.7), calls=%async_computation.1 | async-start | bytes 65536 | tf_op jit(solution)/shard_map/all_to_all | solution.py:264
  56.2 0.0 copy-start.1
  56.2 1.1 %copy-done.1 = bf16[16,160,128]{2,1,0:T(8,128)(2,1)S(1)} copy-done((bf16[16,160,128]{2,1,0:T(8,128)(2,1)S(1)}, bf16[16,160,128]{2,1,0:T(8,128)(2,1)}, u32[]{:S(2)}) %copy-start.1) | copy-done | bytes 655384
  57.3 5.2 %shard_map.90 = (f32[32,2048]{1,0:T(8,128)S(1)}, bf16[512,2048]{1,0:T(8,128)(2,1)S(1)}) custom-call(s32[4,18]{1,0:T(4,128)S(1)} %bitcast.17, s32[1,512]{1,0:T(1,128)S(1)} %bitcast.21, bf16[16,160,128]{2,1,0:T(8,128)(2,1)S(1)} %copy-done.1, bf16[5,72,128,128]{3,2,1,0:T(8,128)(2,1)} %blocks_ref.5), custom_call_target="tpu_custom_call" | custom-call | flops 335544320 | bytes 14813472 | tf_op jit(solution)/shard_map/pallas_call | solution.py:24
  62.5 2.9 %all-to-all-done.1 = bf16[64,2,128]{2,1,0:T(2,128)(2,1)S(1)} async-done(((bf16[64,2,128]{2,1,0:T(2,128)(2,1)}), bf16[64,2,128]{2,1,0:T(2,128)(2,1)S(1)}, u32[]{:S(2)}, u32[]{:S(2)}) %all-to-all-start.1) | async-done | bytes 32800 | tf_op jit(solution)/shard_map/all_to_all | solution.py:264
  65.4 1.3 %shard_map.91 = bf16[30,2048]{1,0:T(8,128)(2,1)} custom-call(f32[32,2048]{1,0:T(8,128)S(1)} %get-tuple-element.19.own_ref, bf16[128,128]{1,0:T(8,128)(2,1)S(1)} %bitcast.10, bf16[512,2048]{1,0:T(8,128)(2,1)S(1)} %get-tuple-element.21.r_ref), custom_call_target="tpu_custom_call" | custom-call | flops 67108864 | bytes 2514944 | tf_op jit(solution)/shard_map/pallas_call | solution.py:24
Async XLA Ops:
  0.6 7.2 %collective-permute-start.1 = (bf16[30,2048]{1,0:T(8,128)(2,1)}, bf16[30,2048]{1,0:T(8,128)(2,1)S(1)}, u32[]{:S(2)}, u32[]{:S(2)}) collective-permute-start(bf16[30,2048]{1,0:T(8,128)(2,1)} %v0.1), channel_id=1, source_target_pairs={{2,0},{3,1},{0,2},{1,3},{6,4},{7,5},{4,6},{5,7},{10,8},{11,9},{8,1... | collective-permute-start | bytes 368648 | tf_op jit(solution)/shard_map/ppermute | solution.py:228
  4.5 6.3 %collective-permute-start = (bf16[30,2048]{1,0:T(8,128)(2,1)}, bf16[30,2048]{1,0:T(8,128)(2,1)S(1)}, u32[]{:S(2)}, u32[]{:S(2)}) collective-permute-start(bf16[30,2048]{1,0:T(8,128)(2,1)} %v0.1), channel_id=1, source_target_pairs={{1,0},{2,1},{3,2},{0,3},{5,4},{6,5},{7,6},{4,7},{9,8},{10,9},{11,1... | collective-permute-start | bytes 368648 | tf_op jit(solution)/shard_map/ppermute | solution.py:228
  5.2 7.4 %collective-permute-start.2 = (bf16[30,2048]{1,0:T(8,128)(2,1)}, bf16[30,2048]{1,0:T(8,128)(2,1)S(1)}, u32[]{:S(2)}, u32[]{:S(2)}) collective-permute-start(bf16[30,2048]{1,0:T(8,128)(2,1)} %v0.1), channel_id=1, source_target_pairs={{3,0},{0,1},{1,2},{2,3},{7,4},{4,5},{5,6},{6,7},{11,8},{8,9},{9,10... | collective-permute-start | bytes 368648 | tf_op jit(solution)/shard_map/ppermute | solution.py:228
  5.9 0.7 %copy-start.3 = (s32[5,120,8]{1,2,0:T(8,128)S(1)}, s32[5,120,8]{1,2,0:T(8,128)}, u32[]{:S(2)}) copy-start(s32[5,120,8]{1,2,0:T(8,128)} %param.12) | copy-start | bytes 57604
  6.7 0.7 %copy-start.5 = (f32[5,120,8]{1,2,0:T(8,128)S(1)}, f32[5,120,8]{1,2,0:T(8,128)}, u32[]{:S(2)}) copy-start(f32[5,120,8]{1,2,0:T(8,128)} %param.13) | copy-start | bytes 57604
  12.6 0.9 %copy-start.2 = (bf16[30,2048]{1,0:T(8,128)(2,1)S(1)}, bf16[30,2048]{1,0:T(8,128)(2,1)}, u32[]{:S(2)}) copy-start(bf16[30,2048]{1,0:T(8,128)(2,1)} %v0.1) | copy-start | bytes 368644
  13.6 0.7 %copy-start.7 = (s32[18,4]{0,1:T(4,128)S(1)}, s32[18,4]{0,1:T(4,128)}, u32[]{:S(2)}) copy-start(s32[18,4]{0,1:T(4,128)} %param.9) | copy-start | bytes 868
  14.2 0.7 %copy-start.9 = (s32[256]{0:T(256)S(1)}, s32[256]{0:T(256)}, u32[]{:S(2)}) copy-start(s32[256]{0:T(256)} %param.10) | copy-start | bytes 3076
  14.9 21.9 %copy-start.4 = (s32[5,120,8]{1,2,0:T(8,128)S(1)}, s32[5,120,8]{1,2,0:T(8,128)}, u32[]{:S(2)}) copy-start(s32[5,120,8]{1,2,0:T(8,128)} %param.12) | copy-start | bytes 57604
  14.9 21.9 %copy-start.6 = (f32[5,120,8]{1,2,0:T(8,128)S(1)}, f32[5,120,8]{1,2,0:T(8,128)}, u32[]{:S(2)}) copy-start(f32[5,120,8]{1,2,0:T(8,128)} %param.13) | copy-start | bytes 57604
  14.9 21.9 %copy-start.11 = (s32[512]{0:T(512)S(1)}, s32[512]{0:T(512)}, u32[]{:S(2)}) copy-start(s32[512]{0:T(512)} %param.11) | copy-start | bytes 6148
  25.1 22.1 %copy-start.8 = (s32[18,4]{0,1:T(4,128)S(1)}, s32[18,4]{0,1:T(4,128)}, u32[]{:S(2)}) copy-start(s32[18,4]{0,1:T(4,128)} %param.9) | copy-start | bytes 868
  25.1 22.1 %copy-start.10 = (s32[256]{0:T(256)S(1)}, s32[256]{0:T(256)}, u32[]{:S(2)}) copy-start(s32[256]{0:T(256)} %param.10) | copy-start | bytes 3076
  25.1 22.1 %all-to-all-start = ((bf16[64,8,128]{2,1,0:T(8,128)(2,1)}), bf16[64,8,128]{2,1,0:T(8,128)(2,1)S(1)}, u32[]{:S(2)}, u32[]{:S(2)}) async-start(bf16[64,8,128]{2,1,0:T(8,128)(2,1)} %bitcast.4), calls=%async_computation | async-start | bytes 262144 | tf_op jit(solution)/shard_map/all_to_all | solution.py:250
  50.4 0.9 %copy-start = (bf16[16,160,128]{2,1,0:T(8,128)(2,1)}, bf16[16,160,128]{2,1,0:T(8,128)(2,1)S(1)}, u32[]{:S(2)}) copy-start(bf16[16,160,128]{2,1,0:T(8,128)(2,1)S(1)} %get-tuple-element.18.mixed_hbm) | copy-start | bytes 1966084
  51.3 14.1 %all-to-all-start.1 = ((bf16[64,2,128]{2,1,0:T(2,128)(2,1)}), bf16[64,2,128]{2,1,0:T(2,128)(2,1)S(1)}, u32[]{:S(2)}, u32[]{:S(2)}) async-start(bf16[64,2,128]{2,1,0:T(2,128)(2,1)} %bitcast.7), calls=%async_computation.1 | async-start | bytes 65536 | tf_op jit(solution)/shard_map/all_to_all | solution.py:264
  56.2 1.1 %copy-start.1 = (bf16[16,160,128]{2,1,0:T(8,128)(2,1)S(1)}, bf16[16,160,128]{2,1,0:T(8,128)(2,1)}, u32[]{:S(2)}) copy-start(bf16[16,160,128]{2,1,0:T(8,128)(2,1)} %copy-done) | copy-start | bytes 1966084

commit v3 on v2

v3 whole, which is shorter than its diff:
```python
import functools
import math

import jax
import jax.numpy as jnp
from jax import lax
from jax.experimental import pallas as pl
from jax.experimental.pallas import tpu as pltpu
from jax.sharding import PartitionSpec as P

LANES = 128
PAD = 32
QUARTERS = 4
WIDTH = 256

VMEM = pl.BlockSpec(memory_space=pltpu.VMEM)
SMEM = pl.BlockSpec(memory_space=pltpu.SMEM)
HBM = pl.BlockSpec(memory_space=pltpu.HBM)
VMEM_LIMIT = 32 * 1024 * 1024
bf16, f32, i32 = jnp.bfloat16, jnp.float32, jnp.int32


def call(kernel, outs, ins, in_specs, out_specs, flops, scratch=()):
    moved = sum(math.prod(a.shape) * jnp.dtype(a.dtype).itemsize for a in [*outs, *ins])
    return pl.pallas_call(
        kernel,
        out_shape=outs,
        in_specs=in_specs,
        out_specs=out_specs,
        scratch_shapes=scratch,
        compiler_params=pltpu.CompilerParams(vmem_limit_bytes=VMEM_LIMIT),
        cost_estimate=pl.CostEstimate(flops=flops, bytes_accessed=moved, transcendentals=0),
    )(*ins)


def begin(sems, *pairs):
    copies = [pltpu.make_async_copy(source, target, sems.at[at]) for at, (source, target) in enumerate(pairs)]
    for copy in copies:
        copy.start()
    return copies


def finish(copies):
    for copy in copies:
        copy.wait()


def one_hot(hit):
    return jnp.where(hit, 1.0, 0.0).astype(bf16)


def dot(a, b):
    return jnp.dot(a, b, preferred_element_type=f32)


def dot_t(a, b):
    return lax.dot_general(a, b, (((1,), (1,)), ((), ())), preferred_element_type=f32)


def padded_place(modes, groups, modes_dev):
    place = modes
    for group in range(1, groups):
        place += jnp.where(modes >= group * modes_dev, PAD - modes_dev, 0)
    return place


def mixer_columns(term, groups, cols_ref, coef_ref):
    modes = cols_ref.shape[2]
    cols = cols_ref[term]
    place = jnp.where(cols < modes, padded_place(cols, groups, modes // groups), -1)
    coef = coef_ref[term]
    want = lax.broadcasted_iota(i32, (groups * PAD, modes), 0)
    total = jnp.zeros(want.shape, f32)
    for slot in range(cols.shape[0]):
        total += jnp.where(place[slot:slot + 1, :] == want, coef[slot:slot + 1, :], 0.0)
    return total.astype(bf16)


def receive_table(recv_ref, r_ref):
    slots = recv_ref.shape[1]
    turned = jnp.broadcast_to(recv_ref[...].astype(f32), (LANES, slots)).T
    wanted = turned[:, :1].astype(i32)
    for at in range(0, r_ref.shape[1], WIDTH):
        r_ref[:, at:at + WIDTH] = one_hot(wanted == lax.broadcasted_iota(i32, (slots, WIDTH), 1) + at)


def block_row(row, rows, cols_ref, mixed_ref, stiff):
    terms, stored = stiff.shape[:2]
    picked = jnp.concatenate(
        [
            mixed_ref[cols_ref[c, row], term * rows:(term + 1) * rows, :]
            for term in range(terms)
            for c in range(stored)
        ],
        axis=1,
    )
    return dot(picked, stiff.reshape(terms * stored * LANES, LANES))


def mix(mixer, field_ref, mixed_ref, start, stop):
    rows = field_ref.shape[0] * field_ref.shape[1]
    for at in range(start, stop, WIDTH):
        field = field_ref[:, :, at:at + WIDTH].reshape(rows, WIDTH)
        mixed = dot(mixer, field).astype(bf16)
        for part in range(WIDTH // LANES):
            mixed_ref[at // LANES + part] = mixed[:, part * LANES:(part + 1) * LANES]


def interface_part(rows, cols_ref, mixed_ref, stiff_ref):
    stored, out_blocks = cols_ref.shape
    owned_blocks = mixed_ref.shape[0]
    parts = [
        block_row(row, rows, cols_ref, mixed_ref, stiff_ref[:, (row - owned_blocks) * stored:(row - owned_blocks + 1) * stored])
        for row in range(owned_blocks, out_blocks)
    ]
    return jnp.concatenate(parts, axis=1).astype(bf16)


def last_stored(blocks_ref, stiff_ref):
    count = stiff_ref.shape[1]
    return blocks_ref.at[:, pl.ds(blocks_ref.shape[1] - count, count)]


def setup_kernel(groups, cols_hbm, coef_hbm, send_hbm, own_hbm, blocks_ref,
                 g_ref, place_ref, own_ref, stiff_ref, cols_ref, coef_ref, send_ref, sems):
    copies = begin(
        sems, (cols_hbm, cols_ref), (coef_hbm, coef_ref), (send_hbm, send_ref), (own_hbm, own_ref),
        (last_stored(blocks_ref, stiff_ref), stiff_ref),
    )
    modes = cols_ref.shape[2]
    rows = groups * PAD
    out_mode = lax.broadcasted_iota(i32, (rows, modes), 1)
    spread = one_hot(padded_place(out_mode, groups, modes // groups) == lax.broadcasted_iota(i32, (rows, modes), 0))
    finish(copies[:3])
    for term in range(cols_ref.shape[0]):
        g_ref[term * rows:(term + 1) * rows, :] = dot_t(spread, mixer_columns(term, groups, cols_ref, coef_ref)).astype(bf16)
    place_ref[...] = one_hot(send_ref[...] == lax.broadcasted_iota(i32, place_ref.shape, 0))
    finish(copies[3:])


def first_kernel(groups, v0, v1, v2, v3, g_ref, place_ref, cols_hbm, stiff_ref,
                 packed_ref, mixed_hbm, field_ref, mixed_ref, cols_ref, sems):
    cols_copy = begin(sems, (cols_hbm, cols_ref))
    me = lax.axis_index("mode")
    modes_dev, owned = v0.shape
    field_ref[:, modes_dev:, :] = jnp.zeros_like(field_ref[:, modes_dev:, :])
    for slot, source in enumerate((v0, v1, v2, v3)):
        field_ref[lax.rem(me + slot, groups), :modes_dev, :] = source[...]
    mixer = g_ref[...]
    pieces = 2
    width = owned // pieces
    keeps = []
    for piece in range(pieces):
        mix(mixer, field_ref, mixed_ref, piece * width, (piece + 1) * width)
        at = pl.ds(piece * width // LANES, width // LANES)
        keeps += begin(sems.at[pl.ds(1 + piece, 1)], (mixed_ref.at[at], mixed_hbm.at[at]))
    finish(cols_copy)
    part = interface_part(groups * PAD, cols_ref, mixed_ref, stiff_ref)
    packed_ref[...] = dot_t(place_ref[...], part).astype(bf16)
    finish(keeps)


def own_fetch(steps, stored, blocks_ref, stiff_ref, sems):
    count = stiff_ref.shape[1] // steps
    return begin(
        sems, *((blocks_ref.at[:, pl.ds(step * count, count)], stiff_ref.at[:, pl.ds(step * count, count)]) for step in range(steps))
    )


def own_rows(rows, cols_ref, mixed_ref, stiff_ref, copies, own_ref):
    stored = cols_ref.shape[0]
    per = mixed_ref.shape[0] // len(copies)
    for step, copy in enumerate(copies):
        copy.wait()
        for row in range(step * per, (step + 1) * per):
            own_ref[:, row * LANES:(row + 1) * LANES] = block_row(
                row, rows, cols_ref, mixed_ref, stiff_ref[:, row * stored:(row + 1) * stored]
            )


def between_kernel(groups, steps, mixed_hbm, cols_hbm, coef_hbm, recv_hbm, where_hbm, blocks_ref,
                   own_ref, r_ref, g2_ref, mixed_ref, stiff_ref, cols_ref, coef_ref, recv_ref, where_ref, sems):
    small = begin(
        sems, (cols_hbm, cols_ref), (coef_hbm, coef_ref), (recv_hbm, recv_ref), (where_hbm, where_ref), (mixed_hbm, mixed_ref)
    )
    copies = own_fetch(steps, where_ref.shape[0], blocks_ref, stiff_ref, sems.at[pl.ds(len(small), steps)])
    me = lax.axis_index("mode")
    modes = cols_ref.shape[2]
    modes_dev = modes // groups
    row = lax.broadcasted_iota(i32, (PAD, modes), 0)
    mine = one_hot((lax.broadcasted_iota(i32, (PAD, modes), 1) == row + me * modes_dev) & (row < modes_dev))
    finish(small[:3])
    for term in range(cols_ref.shape[0]):
        g2_ref[term * PAD:(term + 1) * PAD, :] = dot_t(mine, mixer_columns(term, groups, cols_ref, coef_ref)).astype(bf16)
    receive_table(recv_ref, r_ref)
    finish(small[3:])
    own_rows(groups * PAD, where_ref, mixed_ref, stiff_ref, copies, own_ref)


def second_kernel(groups, own_ref, arrived_ref, r_ref, g2_ref, send_hbm, where_hbm, blocks_ref,
                  first_ref, mixed_hbm, packed_ref, field_ref, mixed_ref, spread_ref, stiff_ref, send_ref, where_ref, sems):
    small = begin(sems, (send_hbm, send_ref), (where_hbm, where_ref), (last_stored(blocks_ref, stiff_ref), stiff_ref))
    me = lax.axis_index("mode")
    owned = own_ref.shape[1]
    arrived = arrived_ref[...].astype(f32).T.astype(bf16)
    for at in range(0, owned, WIDTH):
        total = own_ref[:, at:at + WIDTH] + dot(arrived, r_ref[:, at:at + WIDTH])
        field_ref[:, :, at:at + WIDTH] = total.astype(bf16).reshape(groups, PAD, WIDTH)
    first_ref[...] = field_ref[me, :first_ref.shape[0], :]
    mix(g2_ref[...], field_ref, mixed_ref, 0, owned)
    keeps = begin(sems.at[pl.ds(len(small), 1)], (mixed_ref, mixed_hbm))
    spread_ref[...] = jnp.zeros_like(spread_ref)
    width = send_ref.shape[1]
    finish(small)
    send = send_ref[...]
    lines = lax.broadcasted_iota(i32, (packed_ref.shape[0], width), 0) * QUARTERS
    place = jnp.concatenate([one_hot(send == lines + quarter) for quarter in range(QUARTERS)], axis=1)
    part = interface_part(PAD, where_ref, mixed_ref, stiff_ref)
    for quarter in range(QUARTERS):
        spread_ref[quarter * PAD:(quarter + 1) * PAD, quarter * width:(quarter + 1) * width] = part
    packed_ref[...] = dot_t(place, spread_ref[...]).astype(bf16)
    finish(keeps)


def own_kernel(steps, where_hbm, recv_hbm, mixed_hbm, blocks_ref, own_ref, r_ref,
               mixed_ref, stiff_ref, recv_ref, where_ref, sems):
    small = begin(sems, (recv_hbm, recv_ref), (where_hbm, where_ref), (mixed_hbm, mixed_ref))
    copies = own_fetch(steps, where_ref.shape[0], blocks_ref, stiff_ref, sems.at[pl.ds(len(small), steps)])
    finish(small[:1])
    receive_table(recv_ref, r_ref)
    finish(small[1:])
    own_rows(PAD, where_ref, mixed_ref, stiff_ref, copies, own_ref)


def last_kernel(own_ref, arrived_ref, r_ref, out_ref, slots_ref):
    arrived = arrived_ref[...].astype(f32)
    lines = arrived.shape[0]
    for quarter in range(QUARTERS):
        turned = pltpu.roll(arrived, (QUARTERS - quarter) % QUARTERS * PAD, 1)
        slots_ref[pl.ds(quarter, lines, stride=QUARTERS), :] = turned
    by_slot = slots_ref[...].T[:PAD, :].astype(bf16)
    for at in range(0, own_ref.shape[1], WIDTH):
        total = own_ref[:, at:at + WIDTH] + dot(by_slot, r_ref[:, at:at + WIDTH])
        out_ref[:, at:at + WIDTH] = total.astype(bf16)[:out_ref.shape[0], :]


def local(groups, peers, modes_in, blocks, block_cols, send_slot, recv_row, mix_cols, mix_coef):
    terms, all_stored, blk, _ = blocks.shape
    out_blocks, stored = block_cols.shape
    modes_dev, owned = modes_in.shape
    owned_blocks = owned // blk
    interface = send_slot.shape[0]
    slots = recv_row.shape[0]
    cap = slots // peers
    rows = groups * PAD
    lines = slots // QUARTERS
    Shape, dma = jax.ShapeDtypeStruct, pltpu.SemaphoreType.DMA

    def pin(x):
        return pltpu.with_memory_space_constraint(x, pltpu.HBM)

    others = {
        s: lax.ppermute(modes_in, "mode", [((to + s) % groups, to) for to in range(groups)])
        for s in (2, 1, 3)
    }
    blocks = pin(blocks)
    where = pin(block_cols.T)
    mix_cols, mix_coef = pin(mix_cols.transpose(0, 2, 1)), pin(mix_coef.transpose(0, 2, 1))
    send, recv = pin(send_slot.reshape(1, interface)), pin(recv_row.reshape(1, slots))
    tables = [pltpu.VMEM(mix_cols.shape, i32), pltpu.VMEM(mix_coef.shape, f32)]
    where_scratch = pltpu.SMEM(where.shape, i32)
    send_scratch, recv_scratch = pltpu.VMEM(send.shape, i32), pltpu.VMEM(recv.shape, i32)
    if_blocks = (terms, (out_blocks - owned_blocks) * stored, blk, blk)
    own_scratch = pltpu.VMEM((terms, owned_blocks * stored, blk, blk), bf16)
    field_scratch = pltpu.VMEM((groups, PAD, owned), bf16)
    block_flops = 2 * terms * stored * blk * blk
    wide, narrow = (owned_blocks, terms * rows, blk), (owned_blocks, terms * PAD, blk)

    g, place, own_field, stiff = call(
        functools.partial(setup_kernel, groups),
        [Shape((terms * rows, rows), bf16), Shape((slots, interface), bf16), Shape((modes_dev, owned), bf16), Shape(if_blocks, bf16)],
        [mix_cols, mix_coef, send, pin(modes_in), blocks], [HBM] * 5, [VMEM] * 4, flops=10**6,
        scratch=[*tables, send_scratch, dma((5,))],
    )
    packed, mixed = call(
        functools.partial(first_kernel, groups),
        [Shape((slots, rows), bf16), pltpu.HBM(wide, bf16)],
        [own_field, others[1], others[2], others[3], g, place, where, stiff],
        [VMEM] * 6 + [HBM, VMEM], [VMEM, HBM],
        flops=block_flops * (out_blocks - owned_blocks) * rows,
        scratch=[field_scratch, pltpu.VMEM(wide, bf16), where_scratch, dma((3,))],
    )
    arrived = lax.all_to_all(packed.reshape(peers, cap, rows), "space", split_axis=0, concat_axis=0, tiled=True)
    steps = 8
    own, r, g2 = call(
        functools.partial(between_kernel, groups, steps),
        [Shape((rows, owned), f32), Shape((slots, owned), bf16), Shape((terms * PAD, rows), bf16)],
        [pin(mixed), mix_cols, mix_coef, recv, where, blocks], [HBM] * 6, [VMEM] * 3,
        flops=block_flops * owned_blocks * rows,
        scratch=[pltpu.VMEM(wide, bf16), own_scratch, *tables, recv_scratch, where_scratch, dma((5 + steps,))],
    )
    first_apply, mixed2, packed2 = call(
        functools.partial(second_kernel, groups),
        [Shape((modes_dev, owned), bf16), pltpu.HBM(narrow, bf16), Shape((lines, QUARTERS * PAD), bf16)],
        [own, arrived.reshape(slots, rows), r, g2, send, where, blocks],
        [VMEM] * 4 + [HBM] * 3, [VMEM, HBM, VMEM], flops=2 * slots * rows * owned,
        scratch=[field_scratch, pltpu.VMEM(narrow, bf16), pltpu.VMEM((QUARTERS * PAD, QUARTERS * interface), bf16),
                 pltpu.VMEM(if_blocks, bf16), send_scratch, where_scratch, dma((4,))],
    )
    arrived2 = lax.all_to_all(
        packed2.reshape(peers, cap // QUARTERS, QUARTERS * PAD), "space", split_axis=0, concat_axis=0, tiled=True
    )
    own2, r2 = call(
        functools.partial(own_kernel, steps), [Shape((PAD, owned), f32), Shape((slots, owned), bf16)],
        [where, recv, pin(mixed2), blocks], [HBM] * 4, [VMEM] * 2, flops=block_flops * owned_blocks * PAD,
        scratch=[pltpu.VMEM(narrow, bf16), own_scratch, recv_scratch, where_scratch, dma((3 + steps,))],
    )
    second_apply = call(
        last_kernel, [Shape((modes_dev, owned), bf16)],
        [own2, arrived2.reshape(lines, QUARTERS * PAD), r2], [VMEM] * 3, [VMEM],
        flops=2 * slots * PAD * owned, scratch=[pltpu.VMEM((slots, QUARTERS * PAD), f32)],
    )[0]
    return (first_apply, second_apply)


def solution(mesh):
    in_specs = (
        P("mode", "space"),
        P(None, "space", None, None),
        P("space", None),
        P("space"),
        P("space"),
        P(),
        P(),
    )
    out_specs = (P("mode", "space"), P("mode", "space"))
    body = functools.partial(local, mesh.shape["mode"], mesh.shape["space"])
    return jax.shard_map(body, mesh=mesh, in_specs=in_specs, out_specs=out_specs, check_vma=False)
```

time: 67.1 us -> 59.5 us (0.89)
  local copies, waits for them, and re-layouts: 5.69 us -> 0 us
  waiting for transfers between devices: 17.4 us -> 14.3 us
  starting transfers between devices: 21.9 us -> 24.4 us
  Pallas kernels: 20.9 us -> 19.9 us
    unnamed x24 -> x0, local copies, waits for them, and re-layouts: 5.69 us -> none
    all_to_all x1, waiting for transfers between devices: 9.66 us -> 4.1 us  [local(): lax.all_to_all(packed.reshape(peers, cap, rows), 'space', split_axis=0, c...]
    all_to_all x1, waiting for transfers between devices: 2.9 us -> 4.54 us  [local(): lax.all_to_all(packed2.reshape(peers, cap // QUARTERS, QUARTERS * PAD), '...]
    all_to_all x1, starting transfers between devices: 4.89 us -> 6.26 us  [local(): lax.all_to_all(packed2.reshape(peers, cap // QUARTERS, QUARTERS * PAD), '...]
    all_to_all x1, starting transfers between devices: 11.7 us -> 12.8 us  [local(): lax.all_to_all(packed.reshape(peers, cap, rows), 'space', split_axis=0, c...]
    pallas_call x6, Pallas kernels: 20.9 us -> 19.9 us  [call(): pl.pallas_call(kernel, out_shape=outs, in_specs=in_specs, out_specs=out_s...]
    ppermute x3, waiting for transfers between devices: 4.83 us -> 5.69 us  [local(): lax.ppermute(modes_in, 'mode', [((to + s) % groups, to) for to in range(g...]
  transfers between devices with their start and end apart: 5 -> 5, of which waited for: 4 -> 3; matrix products, arithmetic and copies ran while one was open for 0% -> 0% of each run, Pallas kernels for 9% -> 21%
where the time goes in v3:
time: 59.5 us; the launch traced here: 59.3 us
  starting transfers between devices  24.4 us (41%)
  Pallas kernels  19.9 us (33%)
  waiting for transfers between devices  14.3 us (24%)
  between operations  0.7 us (1%)
    pallas_call x6, Pallas kernels, call(): pl.pallas_call(kernel, out_shape=outs, in_specs=in_specs, out_specs=out_s...  19.9 us
    all_to_all x1, starting transfers between devices, local(): lax.all_to_all(packed.reshape(peers, cap, rows), 'space', split_axis=0, c...  12.8 us
    all_to_all x1, starting transfers between devices, local(): lax.all_to_all(packed2.reshape(peers, cap // QUARTERS, QUARTERS * PAD), '...  6.26 us
    ppermute x3, waiting for transfers between devices, local(): lax.ppermute(modes_in, 'mode', [((to + s) % groups, to) for to in range(g...  5.69 us
    ppermute x3, starting transfers between devices, local(): lax.ppermute(modes_in, 'mode', [((to + s) % groups, to) for to in range(g...  5.29 us
    all_to_all x1, waiting for transfers between devices, local(): lax.all_to_all(packed2.reshape(peers, cap // QUARTERS, QUARTERS * PAD), '...  4.54 us
    all_to_all x1, waiting for transfers between devices, local(): lax.all_to_all(packed.reshape(peers, cap, rows), 'space', split_axis=0, c...  4.1 us
  transfers between devices with their start and end apart: 5, of which 3 were waited for; matrix products, arithmetic and copies ran while one was open for 0% of the time, Pallas kernels for 21%

profile of v3, /device:TPU:1, one launch (start us, length us, event | category | flops | bytes accessed | tf_op | source)
XLA Modules:
  0.0 59.3 jit_solution(10883998568122706285)
XLA Ops:
  0.6 3.6 %collective-permute-start = (bf16[30,2048]{1,0:T(8,128)(2,1)}, bf16[30,2048]{1,0:T(8,128)(2,1)S(1)}, u32[]{:S(2)}, u32[]{:S(2)}) collective-permute-start(bf16[30,2048]{1,0:T(8,128)(2,1)} %own_hbm.1), channel_id=1, source_target_pairs={{1,0},{2,1},{3,2},{0,3},{5,4},{6,5},{7,6},{4,7},{9,8},{10,9},{11,1... | collective-permute-start | bytes 368648 | tf_op jit(solution)/shard_map/ppermute | solution.py:263
  4.3 0.0 collective-permute-start.2
  4.3 1.6 %collective-permute-start.1 = (bf16[30,2048]{1,0:T(8,128)(2,1)}, bf16[30,2048]{1,0:T(8,128)(2,1)S(1)}, u32[]{:S(2)}, u32[]{:S(2)}) collective-permute-start(bf16[30,2048]{1,0:T(8,128)(2,1)} %own_hbm.1), channel_id=1, source_target_pairs={{2,0},{3,1},{0,2},{1,3},{6,4},{7,5},{4,6},{5,7},{10,8},{11,9},{8,1... | collective-permute-start | bytes 368648 | tf_op jit(solution)/shard_map/ppermute | solution.py:263
  5.9 1.5 %shard_map.86 = (bf16[640,128]{1,0:T(8,128)(2,1)S(1)}, bf16[512,256]{1,0:T(8,128)(2,1)S(1)}, bf16[30,2048]{1,0:T(8,128)(2,1)S(1)}, bf16[5,8,128,128]{3,2,1,0:T(8,128)(2,1)S(1)}) custom-call(s32[5,8,120]{2,1,0:T(8,128)} %bitcast.11, f32[5,8,120]{2,1,0:T(8,128)} %bitcast.13, s32[1,256]{1,0:T(1,128)} %bitcast.21, bf16[30,2048]{1,0:T(8,128)(2,1)} %own_hbm.1, ...), custom_call_target="tpu_custom_call" | custom-call | flops 1000000 | bytes 13818368 | tf_op jit(solution)/shard_map/pallas_call | solution.py:25
  7.4 0.0 collective-permute-done.v1
  7.4 5.7 %collective-permute-done.2.v3 = bf16[30,2048]{1,0:T(8,128)(2,1)S(1)} collective-permute-done((bf16[30,2048]{1,0:T(8,128)(2,1)}, bf16[30,2048]{1,0:T(8,128)(2,1)S(1)}, u32[]{:S(2)}, u32[]{:S(2)}) %collective-permute-start.2) | collective-permute-done | bytes 122912 | tf_op jit(solution)/shard_map/ppermute | solution.py:263
  13.1 0.0 collective-permute-done.1.v2
  13.1 2.8 %shard_map.87 = (bf16[512,128]{1,0:T(8,128)(2,1)}, bf16[16,640,128]{2,1,0:T(8,128)(2,1)}) custom-call(bf16[30,2048]{1,0:T(8,128)(2,1)S(1)} %get-tuple-element.16.v0, bf16[30,2048]{1,0:T(8,128)(2,1)S(1)} %collective-permute-done.v1, bf16[30,2048]{1,0:T(8,128)(2,1)S(1)} %collective-permute-done.1.v2, bf16[30,2048]{1,0:T(8,128)(2,1)S(1)} %collective-permute-done.2.v3, ...), custom_call_target="tpu_custom_call" | custom-call | flops 167772160 | bytes 4981024 | tf_op jit(solution)/shard_map/pallas_call | solution.py:25
  15.9 12.8 %all-to-all-start = ((bf16[64,8,128]{2,1,0:T(8,128)(2,1)}), bf16[64,8,128]{2,1,0:T(8,128)(2,1)S(1)}, u32[]{:S(2)}, u32[]{:S(2)}) async-start(bf16[64,8,128]{2,1,0:T(8,128)(2,1)} %bitcast.5), calls=%async_computation | async-start | bytes 262144 | tf_op jit(solution)/shard_map/all_to_all | solution.py:293
  28.7 6.3 %shard_map.88 = (f32[128,2048]{1,0:T(8,128)S(1)}, bf16[512,2048]{1,0:T(8,128)(2,1)S(1)}, bf16[160,128]{1,0:T(8,128)(2,1)S(1)}) custom-call(bf16[16,640,128]{2,1,0:T(8,128)(2,1)} %get-tuple-element.20.mixed_hbm, s32[5,8,120]{2,1,0:T(8,128)} %bitcast.12, f32[5,8,120]{2,1,0:T(8,128)} %bitcast.14, s32[1,512]{1,0:T(1,128)} %bitcast.19, s32[4,18]{1,0:T(4,128)} %bitcast.16, ...), custom_call_target="tpu_custom_call" | custom-call | flops 1342177280 | bytes 17645344 | tf_op jit(solution)/shard_map/pallas_call | solution.py:25
  35.0 4.1 %all-to-all-done = bf16[64,8,128]{2,1,0:T(8,128)(2,1)S(1)} async-done(((bf16[64,8,128]{2,1,0:T(8,128)(2,1)}), bf16[64,8,128]{2,1,0:T(8,128)(2,1)S(1)}, u32[]{:S(2)}, u32[]{:S(2)}) %all-to-all-start) | async-done | bytes 131104 | tf_op jit(solution)/shard_map/all_to_all | solution.py:293
  39.1 3.5 %shard_map.89 = (bf16[30,2048]{1,0:T(8,128)(2,1)}, bf16[16,160,128]{2,1,0:T(8,128)(2,1)}, bf16[128,128]{1,0:T(8,128)(2,1)}) custom-call(f32[128,2048]{1,0:T(8,128)S(1)} %get-tuple-element.21.own_ref, bf16[512,128]{1,0:T(8,128)(2,1)S(1)} %bitcast.9, bf16[512,2048]{1,0:T(8,128)(2,1)S(1)} %get-tuple-element.23.r_ref, ...), custom_call_target="tpu_custom_call" | custom-call | flops 268435456 | bytes 15926560 | tf_op jit(solution)/shard_map/pallas_call | solution.py:25
  42.6 6.3 %all-to-all-start.1 = ((bf16[64,2,128]{2,1,0:T(2,128)(2,1)}), bf16[64,2,128]{2,1,0:T(2,128)(2,1)S(1)}, u32[]{:S(2)}, u32[]{:S(2)}) async-start(bf16[64,2,128]{2,1,0:T(2,128)(2,1)} %bitcast.7), calls=%async_computation.1 | async-start | bytes 65536 | tf_op jit(solution)/shard_map/all_to_all | solution.py:310
  48.8 4.7 %shard_map.90 = (f32[32,2048]{1,0:T(8,128)S(1)}, bf16[512,2048]{1,0:T(8,128)(2,1)S(1)}) custom-call(s32[4,18]{1,0:T(4,128)} %bitcast.18, s32[1,512]{1,0:T(1,128)} %bitcast.20, bf16[16,160,128]{2,1,0:T(8,128)(2,1)} %get-tuple-element.26.mixed_hbm, bf16[5,72,128,128]{3,2,1,0:T(8,128)(2,1)} %blocks_ref.7), custom_call_target="tpu_custom_call" | custom-call | flops 335544320 | bytes 14813472 | tf_op jit(solution)/shard_map/pallas_call | solution.py:25
  53.5 4.5 %all-to-all-done.1 = bf16[64,2,128]{2,1,0:T(2,128)(2,1)S(1)} async-done(((bf16[64,2,128]{2,1,0:T(2,128)(2,1)}), bf16[64,2,128]{2,1,0:T(2,128)(2,1)S(1)}, u32[]{:S(2)}, u32[]{:S(2)}) %all-to-all-start.1) | async-done | bytes 32800 | tf_op jit(solution)/shard_map/all_to_all | solution.py:310
  58.0 1.3 %shard_map.91 = bf16[30,2048]{1,0:T(8,128)(2,1)} custom-call(f32[32,2048]{1,0:T(8,128)S(1)} %get-tuple-element.27.own_ref, bf16[128,128]{1,0:T(8,128)(2,1)S(1)} %bitcast.10, bf16[512,2048]{1,0:T(8,128)(2,1)S(1)} %get-tuple-element.29.r_ref), custom_call_target="tpu_custom_call" | custom-call | flops 67108864 | bytes 2514944 | tf_op jit(solution)/shard_map/pallas_call | solution.py:25
Async XLA Ops:
  0.6 6.8 %collective-permute-start = (bf16[30,2048]{1,0:T(8,128)(2,1)}, bf16[30,2048]{1,0:T(8,128)(2,1)S(1)}, u32[]{:S(2)}, u32[]{:S(2)}) collective-permute-start(bf16[30,2048]{1,0:T(8,128)(2,1)} %own_hbm.1), channel_id=1, source_target_pairs={{1,0},{2,1},{3,2},{0,3},{5,4},{6,5},{7,6},{4,7},{9,8},{10,9},{11,1... | collective-permute-start | bytes 368648 | tf_op jit(solution)/shard_map/ppermute | solution.py:263
  4.3 8.8 %collective-permute-start.2 = (bf16[30,2048]{1,0:T(8,128)(2,1)}, bf16[30,2048]{1,0:T(8,128)(2,1)S(1)}, u32[]{:S(2)}, u32[]{:S(2)}) collective-permute-start(bf16[30,2048]{1,0:T(8,128)(2,1)} %own_hbm.1), channel_id=1, source_target_pairs={{3,0},{0,1},{1,2},{2,3},{7,4},{4,5},{5,6},{6,7},{11,8},{8,9},{9,10... | collective-permute-start | bytes 368648 | tf_op jit(solution)/shard_map/ppermute | solution.py:263
  4.3 8.8 %collective-permute-start.1 = (bf16[30,2048]{1,0:T(8,128)(2,1)}, bf16[30,2048]{1,0:T(8,128)(2,1)S(1)}, u32[]{:S(2)}, u32[]{:S(2)}) collective-permute-start(bf16[30,2048]{1,0:T(8,128)(2,1)} %own_hbm.1), channel_id=1, source_target_pairs={{2,0},{3,1},{0,2},{1,3},{6,4},{7,5},{4,6},{5,7},{10,8},{11,9},{8,1... | collective-permute-start | bytes 368648 | tf_op jit(solution)/shard_map/ppermute | solution.py:263
  15.9 23.2 %all-to-all-start = ((bf16[64,8,128]{2,1,0:T(8,128)(2,1)}), bf16[64,8,128]{2,1,0:T(8,128)(2,1)S(1)}, u32[]{:S(2)}, u32[]{:S(2)}) async-start(bf16[64,8,128]{2,1,0:T(8,128)(2,1)} %bitcast.5), calls=%async_computation | async-start | bytes 262144 | tf_op jit(solution)/shard_map/all_to_all | solution.py:293
  42.6 15.5 %all-to-all-start.1 = ((bf16[64,2,128]{2,1,0:T(2,128)(2,1)}), bf16[64,2,128]{2,1,0:T(2,128)(2,1)S(1)}, u32[]{:S(2)}, u32[]{:S(2)}) async-start(bf16[64,2,128]{2,1,0:T(2,128)(2,1)} %bitcast.7), calls=%async_computation.1 | async-start | bytes 65536 | tf_op jit(solution)/shard_map/all_to_all | solution.py:310

commit v4 on v3

v4 whole, which is shorter than its diff:
```python
import functools
import math

import jax
import jax.numpy as jnp
from jax import lax
from jax.experimental import pallas as pl
from jax.experimental.pallas import tpu as pltpu
from jax.sharding import PartitionSpec as P

LANES = 128
PAD = 32
QUARTERS = 4
WIDTH = 256

VMEM = pl.BlockSpec(memory_space=pltpu.VMEM)
SMEM = pl.BlockSpec(memory_space=pltpu.SMEM)
HBM = pl.BlockSpec(memory_space=pltpu.HBM)
VMEM_LIMIT = 32 * 1024 * 1024
bf16, f32, i32 = jnp.bfloat16, jnp.float32, jnp.int32


def call(kernel, outs, ins, in_specs, out_specs, flops, scratch=()):
    moved = sum(math.prod(a.shape) * jnp.dtype(a.dtype).itemsize for a in [*outs, *ins])
    return pl.pallas_call(
        kernel,
        out_shape=outs,
        in_specs=in_specs,
        out_specs=out_specs,
        scratch_shapes=scratch,
        compiler_params=pltpu.CompilerParams(vmem_limit_bytes=VMEM_LIMIT),
        cost_estimate=pl.CostEstimate(flops=flops, bytes_accessed=moved, transcendentals=0),
    )(*ins)


def begin(sems, *pairs):
    copies = [pltpu.make_async_copy(source, target, sems.at[at]) for at, (source, target) in enumerate(pairs)]
    for copy in copies:
        copy.start()
    return copies


def finish(copies):
    for copy in copies:
        copy.wait()


def one_hot(hit):
    return jnp.where(hit, 1.0, 0.0).astype(bf16)


def dot(a, b):
    return jnp.dot(a, b, preferred_element_type=f32)


def dot_t(a, b):
    return lax.dot_general(a, b, (((1,), (1,)), ((), ())), preferred_element_type=f32)


def padded_place(modes, groups, modes_dev):
    place = modes
    for group in range(1, groups):
        place += jnp.where(modes >= group * modes_dev, PAD - modes_dev, 0)
    return place


def mixer_columns(term, groups, cols_ref, coef_ref):
    modes = cols_ref.shape[2]
    cols = cols_ref[term]
    place = jnp.where(cols < modes, padded_place(cols, groups, modes // groups), -1)
    coef = coef_ref[term]
    want = lax.broadcasted_iota(i32, (groups * PAD, modes), 0)
    total = jnp.zeros(want.shape, f32)
    for slot in range(cols.shape[0]):
        total += jnp.where(place[slot:slot + 1, :] == want, coef[slot:slot + 1, :], 0.0)
    return total.astype(bf16)


def block_row(row, rows, cols_ref, mixed_ref, stiff):
    terms, stored = stiff.shape[:2]
    picked = jnp.concatenate(
        [
            mixed_ref[cols_ref[c, row], term * rows:(term + 1) * rows, :]
            for term in range(terms)
            for c in range(stored)
        ],
        axis=1,
    )
    return dot(picked, stiff.reshape(terms * stored * LANES, LANES))


def last_stored(blocks_ref, stiff_ref):
    count = stiff_ref.shape[1]
    return blocks_ref.at[:, pl.ds(blocks_ref.shape[1] - count, count)]


def by_quarter(rows_ref, quarter):
    return rows_ref[pl.ds(quarter, rows_ref.shape[0] // QUARTERS, stride=QUARTERS), :]


def receive_table(recv_ref, r_ref, turned_ref):
    slots = recv_ref.shape[1]
    turned_ref[...] = jnp.broadcast_to(recv_ref[...].astype(f32), (LANES, slots)).T
    lanes = lax.broadcasted_iota(i32, (slots // QUARTERS, LANES), 1)
    for quarter in range(QUARTERS):
        offset = by_quarter(turned_ref, quarter).astype(i32) - lanes
        at = slice(quarter * slots // QUARTERS, (quarter + 1) * slots // QUARTERS)
        for block in range(r_ref.shape[0]):
            r_ref[block, at, :] = one_hot(offset == block * LANES)


def mixed_row(picked, stiff, mixer):
    terms, stored = stiff.shape[:2]
    wide = jnp.concatenate([stiff[term].reshape(stored * LANES, LANES) for term in range(terms)], axis=1)
    product = dot(picked, wide).astype(bf16)
    return dot(mixer, jnp.concatenate([product[:, term * LANES:(term + 1) * LANES] for term in range(terms)], axis=0))


def setup_kernel(groups, cols_hbm, coef_hbm, send_hbm, own_hbm, blocks_ref,
                 g_ref, place_ref, own_ref, stiff_ref, cols_ref, coef_ref, send_ref, sems):
    copies = begin(
        sems, (cols_hbm, cols_ref), (coef_hbm, coef_ref), (send_hbm, send_ref), (own_hbm, own_ref),
        (last_stored(blocks_ref, stiff_ref), stiff_ref),
    )
    modes = cols_ref.shape[2]
    rows = groups * PAD
    out_mode = lax.broadcasted_iota(i32, (rows, modes), 1)
    spread = one_hot(padded_place(out_mode, groups, modes // groups) == lax.broadcasted_iota(i32, (rows, modes), 0))
    finish(copies[:3])
    for term in range(cols_ref.shape[0]):
        g_ref[:, term * rows:(term + 1) * rows] = dot_t(spread, mixer_columns(term, groups, cols_ref, coef_ref)).astype(bf16)
    place_ref[...] = one_hot(send_ref[...] == lax.broadcasted_iota(i32, place_ref.shape, 0))
    finish(copies[3:])


def first_kernel(groups, v0, v1, v2, v3, g_ref, place_ref, where_hbm, stiff_ref,
                 packed_ref, field_hbm, g_hbm, field_ref, where_ref, sems):
    copies = begin(sems, (where_hbm, where_ref), (g_ref, g_hbm))
    me = lax.axis_index("mode")
    owned_blocks, _, _, lanes = field_ref.shape
    modes_dev = v0.shape[0]
    field_ref[:, :, modes_dev:, :] = jnp.zeros_like(field_ref[:, :, modes_dev:, :])
    for slot, source in enumerate((v0, v1, v2, v3)):
        group = lax.rem(me + slot, groups)
        for block in range(owned_blocks):
            field_ref[block, group, :modes_dev, :] = source[:, block * lanes:(block + 1) * lanes]
    copies += begin(sems.at[pl.ds(2, 1)], (field_ref, field_hbm))
    copies[0].wait()
    mixer = g_ref[...]
    stored, out_blocks = where_ref.shape
    parts = []
    for row in range(owned_blocks, out_blocks):
        picked = jnp.concatenate(
            [field_ref[where_ref[c, row]].reshape(groups * PAD, lanes) for c in range(stored)], axis=1
        )
        at = (row - owned_blocks) * stored
        parts.append(mixed_row(picked, stiff_ref[:, at:at + stored], mixer))
    part = jnp.concatenate(parts, axis=1).astype(bf16)
    packed_ref[...] = dot_t(place_ref[...], part).astype(bf16)
    finish(copies[1:])


def own_fetch(steps, stored, blocks_ref, stiff_ref, sems):
    count = stiff_ref.shape[1] // steps
    return begin(
        sems, *((blocks_ref.at[:, pl.ds(step * count, count)], stiff_ref.at[:, pl.ds(step * count, count)]) for step in range(steps))
    )


def between_kernel(groups, steps, field_hbm, g_hbm, cols_hbm, coef_hbm, recv_hbm, where_hbm, blocks_ref,
                   own_ref, own_hbm, r_ref, g2_ref, g2_hbm,
                   field_ref, g_ref, stiff_ref, cols_ref, coef_ref, recv_ref, where_ref, turned_ref, sems):
    small = begin(
        sems, (cols_hbm, cols_ref), (coef_hbm, coef_ref), (recv_hbm, recv_ref), (where_hbm, where_ref),
        (g_hbm, g_ref), (field_hbm, field_ref),
    )
    used = len(small)
    copies = own_fetch(steps, where_ref.shape[0], blocks_ref, stiff_ref, sems.at[pl.ds(used, steps)])
    me = lax.axis_index("mode")
    terms, _, modes = cols_ref.shape
    modes_dev = modes // groups
    rows = groups * PAD
    row = lax.broadcasted_iota(i32, (PAD, modes), 0)
    mine = one_hot((lax.broadcasted_iota(i32, (PAD, modes), 1) == row + me * modes_dev) & (row < modes_dev))
    finish(small[:3])
    for term in range(terms):
        g2_ref[:, term * rows:(term + 1) * rows] = dot_t(mine, mixer_columns(term, groups, cols_ref, coef_ref)).astype(bf16)
    keeps = begin(sems.at[pl.ds(used + steps, 1)], (g2_ref, g2_hbm))
    receive_table(recv_ref, r_ref, turned_ref)
    finish(small[3:])
    mixer = g_ref[...]
    stored = where_ref.shape[0]
    owned_blocks = own_ref.shape[0]
    per = owned_blocks // steps
    for step in range(steps):
        copies[step].wait()
        for block in range(step * per, (step + 1) * per):
            picked = jnp.concatenate(
                [field_ref[where_ref[c, block]].reshape(rows, LANES) for c in range(stored)], axis=1
            )
            own_ref[block] = mixed_row(picked, stiff_ref[:, block * stored:(block + 1) * stored], mixer)
        at = pl.ds(step * per, per)
        keeps += begin(sems.at[pl.ds(used + steps + 1 + step, 1)], (own_ref.at[at], own_hbm.at[at]))
    finish(keeps)


def second_kernel(groups, own_ref, arrived_ref, r_ref, g2_ref, send_hbm, where_hbm, blocks_ref,
                  packed_ref, turned_hbm, turned_ref, lines_ref, spread_ref, stiff_ref, send_ref, where_ref, sems):
    small = begin(sems, (where_hbm, where_ref), (send_hbm, send_ref), (last_stored(blocks_ref, stiff_ref), stiff_ref))
    lines_ref[...] = arrived_ref[...].astype(f32)
    turned_ref[...] = jnp.concatenate(
        [by_quarter(lines_ref, quarter).T.astype(bf16) for quarter in range(QUARTERS)], axis=1
    )
    keeps = begin(sems.at[pl.ds(len(small), 1)], (turned_ref, turned_hbm))
    turned = turned_ref[...]
    width = send_ref.shape[1]
    finish(small[:2])
    lines = lax.broadcasted_iota(i32, (packed_ref.shape[0], width), 0) * QUARTERS
    place = jnp.concatenate([one_hot(send_ref[...] == lines + quarter) for quarter in range(QUARTERS)], axis=1)
    spread_ref[...] = jnp.zeros_like(spread_ref)
    stored, out_blocks = where_ref.shape
    owned_blocks = own_ref.shape[0]
    picks = []
    for row in range(owned_blocks, out_blocks):
        columns = [where_ref[c, row] for c in range(stored)]
        base = jnp.concatenate([own_ref[column] for column in columns], axis=1)
        table = jnp.concatenate([r_ref[column] for column in columns], axis=1)
        picks.append((base + dot(turned, table)).astype(bf16))
    small[2].wait()
    mixer = g2_ref[...]
    part = jnp.concatenate(
        [mixed_row(picked, stiff_ref[:, at * stored:(at + 1) * stored], mixer) for at, picked in enumerate(picks)], axis=1
    ).astype(bf16)
    for quarter in range(QUARTERS):
        spread_ref[quarter * PAD:(quarter + 1) * PAD, quarter * width:(quarter + 1) * width] = part
    packed_ref[...] = dot_t(place, spread_ref[...]).astype(bf16)
    finish(keeps)


def own_kernel(groups, steps, where_hbm, recv_hbm, g2_hbm, turned_hbm, own_hbm, blocks_ref,
               first_ref, own2_ref, r_ref,
               own_ref, field_ref, mixed_ref, stiff_ref, recv_ref, where_ref, g2_ref, turned_ref, rows_ref, sems):
    small = begin(
        sems, (recv_hbm, recv_ref), (where_hbm, where_ref), (g2_hbm, g2_ref), (turned_hbm, turned_ref), (own_hbm, own_ref)
    )
    copies = own_fetch(steps, where_ref.shape[0], blocks_ref, stiff_ref, sems.at[pl.ds(len(small), steps)])
    me = lax.axis_index("mode")
    small[0].wait()
    receive_table(recv_ref, r_ref, rows_ref)
    finish(small[1:])
    owned_blocks, rows, lanes = own_ref.shape
    terms, stored = stiff_ref.shape[0], where_ref.shape[0]
    modes_dev = first_ref.shape[0]
    turned = turned_ref[...]
    mixer = jnp.concatenate([g2_ref[:, term * rows:(term + 1) * rows] for term in range(terms)], axis=0)
    for block in range(0, owned_blocks, 2):
        table = jnp.concatenate([r_ref[block], r_ref[block + 1]], axis=1)
        base = jnp.concatenate([own_ref[block], own_ref[block + 1]], axis=1)
        field = (base + dot(turned, table)).astype(bf16)
        mixed = dot(mixer, field).astype(bf16)
        for part in range(2):
            field_ref[block + part] = field[:, part * lanes:(part + 1) * lanes].reshape(groups, PAD, lanes)
            mixed_ref[block + part] = mixed[:, part * lanes:(part + 1) * lanes]
            first_ref[:, (block + part) * lanes:(block + part + 1) * lanes] = field_ref[block + part, me, :modes_dev, :]
    per = owned_blocks // steps
    for step in range(steps):
        copies[step].wait()
        for block in range(step * per, (step + 1) * per):
            own2_ref[:, block * lanes:(block + 1) * lanes] = block_row(
                block, PAD, where_ref, mixed_ref, stiff_ref[:, block * stored:(block + 1) * stored]
            )


def last_kernel(own_ref, arrived_ref, r_ref, out_ref):
    turned = arrived_ref[...].astype(f32).T.astype(bf16)
    by_slot = jnp.concatenate([turned[quarter * PAD:(quarter + 1) * PAD, :] for quarter in range(QUARTERS)], axis=1)
    for block in range(0, r_ref.shape[0], 2):
        at = slice(block * LANES, (block + 2) * LANES)
        table = jnp.concatenate([r_ref[block], r_ref[block + 1]], axis=1)
        total = own_ref[:, at] + dot(by_slot, table)
        out_ref[:, at] = total.astype(bf16)[:out_ref.shape[0], :]


def local(groups, peers, modes_in, blocks, block_cols, send_slot, recv_row, mix_cols, mix_coef):
    terms, all_stored, blk, _ = blocks.shape
    out_blocks, stored = block_cols.shape
    modes_dev, owned = modes_in.shape
    owned_blocks = owned // blk
    interface = send_slot.shape[0]
    slots = recv_row.shape[0]
    cap = slots // peers
    rows = groups * PAD
    lines = slots // QUARTERS
    Shape, dma = jax.ShapeDtypeStruct, pltpu.SemaphoreType.DMA

    def pin(x):
        return pltpu.with_memory_space_constraint(x, pltpu.HBM)

    others = {
        s: lax.ppermute(modes_in, "mode", [((to + s) % groups, to) for to in range(groups)])
        for s in (2, 1, 3)
    }
    blocks = pin(blocks)
    where = pin(block_cols.T)
    mix_cols, mix_coef = pin(mix_cols.transpose(0, 2, 1)), pin(mix_coef.transpose(0, 2, 1))
    send, recv = pin(send_slot.reshape(1, interface)), pin(recv_row.reshape(1, slots))
    tables = [pltpu.VMEM(mix_cols.shape, i32), pltpu.VMEM(mix_coef.shape, f32)]
    where_scratch = pltpu.SMEM(where.shape, i32)
    send_scratch, recv_scratch = pltpu.VMEM(send.shape, i32), pltpu.VMEM(recv.shape, i32)
    if_blocks = (terms, (out_blocks - owned_blocks) * stored, blk, blk)
    own_scratch = pltpu.VMEM((terms, owned_blocks * stored, blk, blk), bf16)
    field_shape = (owned_blocks, groups, PAD, blk)
    field_scratch = pltpu.VMEM(field_shape, bf16)
    own_shape, table_shape = (owned_blocks, rows, blk), (owned_blocks, slots, blk)
    turned_scratch = pltpu.VMEM((slots, LANES), f32)
    block_flops = 2 * terms * stored * blk * blk

    g, place, own_field, stiff = call(
        functools.partial(setup_kernel, groups),
        [Shape((rows, terms * rows), bf16), Shape((slots, interface), bf16), Shape((modes_dev, owned), bf16), Shape(if_blocks, bf16)],
        [mix_cols, mix_coef, send, pin(modes_in), blocks], [HBM] * 5, [VMEM] * 4, flops=10**6,
        scratch=[*tables, send_scratch, dma((5,))],
    )
    packed, field, g_kept = call(
        functools.partial(first_kernel, groups),
        [Shape((slots, rows), bf16), pltpu.HBM(field_shape, bf16), pltpu.HBM((rows, terms * rows), bf16)],
        [own_field, others[1], others[2], others[3], g, place, where, stiff],
        [VMEM] * 6 + [HBM, VMEM], [VMEM, HBM, HBM],
        flops=block_flops * (out_blocks - owned_blocks) * rows,
        scratch=[field_scratch, where_scratch, dma((3,))],
    )
    arrived = lax.all_to_all(packed.reshape(peers, cap, rows), "space", split_axis=0, concat_axis=0, tiled=True)
    steps = 16
    own, own_kept, r, g2, g2_kept = call(
        functools.partial(between_kernel, groups, steps),
        [Shape(own_shape, f32), pltpu.HBM(own_shape, f32), Shape(table_shape, bf16),
         Shape((PAD, terms * rows), bf16), pltpu.HBM((PAD, terms * rows), bf16)],
        [pin(field), pin(g_kept), mix_cols, mix_coef, recv, where, blocks], [HBM] * 7, [VMEM, HBM, VMEM, VMEM, HBM],
        flops=block_flops * owned_blocks * rows,
        scratch=[field_scratch, pltpu.VMEM((rows, terms * rows), bf16), own_scratch, *tables, recv_scratch, where_scratch,
                 turned_scratch, dma((7 + 2 * steps,))],
    )
    packed2, turned = call(
        functools.partial(second_kernel, groups),
        [Shape((lines, QUARTERS * PAD), bf16), pltpu.HBM((rows, slots), bf16)],
        [own, arrived.reshape(slots, rows), r, g2, send, where, blocks],
        [VMEM] * 4 + [HBM] * 3, [VMEM, HBM], flops=2 * slots * rows * owned,
        scratch=[pltpu.VMEM((rows, slots), bf16), turned_scratch, pltpu.VMEM((QUARTERS * PAD, QUARTERS * interface), bf16),
                 pltpu.VMEM(if_blocks, bf16), send_scratch, where_scratch, dma((4,))],
    )
    arrived2 = lax.all_to_all(
        packed2.reshape(peers, cap // QUARTERS, QUARTERS * PAD), "space", split_axis=0, concat_axis=0, tiled=True
    )
    first_apply, own2, r2 = call(
        functools.partial(own_kernel, groups, steps),
        [Shape((modes_dev, owned), bf16), Shape((PAD, owned), f32), Shape(table_shape, bf16)],
        [where, recv, pin(g2_kept), pin(turned), pin(own_kept), blocks], [HBM] * 6, [VMEM] * 3,
        flops=block_flops * owned_blocks * PAD,
        scratch=[pltpu.VMEM(own_shape, f32), field_scratch, pltpu.VMEM((owned_blocks, terms * PAD, blk), bf16), own_scratch,
                 recv_scratch, where_scratch, pltpu.VMEM((PAD, terms * rows), bf16), pltpu.VMEM((rows, slots), bf16),
                 turned_scratch, dma((5 + steps,))],
    )
    second_apply = call(
        last_kernel, [Shape((modes_dev, owned), bf16)],
        [own2, arrived2.reshape(lines, QUARTERS * PAD), r2], [VMEM] * 3, [VMEM], flops=2 * slots * PAD * owned,
    )[0]
    return (first_apply, second_apply)


def solution(mesh):
    in_specs = (
        P("mode", "space"),
        P(None, "space", None, None),
        P("space", None),
        P("space"),
        P("space"),
        P(),
        P(),
    )
    out_specs = (P("mode", "space"), P("mode", "space"))
    body = functools.partial(local, mesh.shape["mode"], mesh.shape["space"])
    return jax.shard_map(body, mesh=mesh, in_specs=in_specs, out_specs=out_specs, check_vma=False)
```

time: 59.5 us -> 61.6 us (1.035)
  waiting for transfers between devices: 14.3 us -> 8.62 us
  Pallas kernels: 19.9 us -> 24.7 us
  starting transfers between devices: 24.4 us -> 27.3 us
    pallas_call x6, Pallas kernels: 19.9 us -> 24.7 us  [call(): pl.pallas_call(kernel, out_shape=outs, in_specs=in_specs, out_specs=out_s...]
    all_to_all x1, waiting for transfers between devices: 4.1 us -> 1.11 us  [local(): lax.all_to_all(packed.reshape(peers, cap, rows), 'space', split_axis=0, c...]
    all_to_all x1, starting transfers between devices: 6.26 us -> 9.24 us  [local(): lax.all_to_all(packed2.reshape(peers, cap // QUARTERS, QUARTERS * PAD), '...]
    all_to_all x1, waiting for transfers between devices: 4.54 us -> 1.82 us  [local(): lax.all_to_all(packed2.reshape(peers, cap // QUARTERS, QUARTERS * PAD), '...]
  transfers between devices with their start and end apart: 5 -> 5, of which waited for: 3 -> 3; matrix products, arithmetic and copies ran while one was open for 0% -> 0% of each run, Pallas kernels for 21% -> 30%
where the time goes in v4:
time: 61.6 us; the launch traced here: 61.4 us
  starting transfers between devices  27.3 us (44%)
  Pallas kernels  24.7 us (40%)
  waiting for transfers between devices  8.62 us (14%)
  between operations  0.7 us (1%)
    pallas_call x6, Pallas kernels, call(): pl.pallas_call(kernel, out_shape=outs, in_specs=in_specs, out_specs=out_s...  24.7 us
    all_to_all x1, starting transfers between devices, local(): lax.all_to_all(packed.reshape(peers, cap, rows), 'space', split_axis=0, c...  12.8 us
    all_to_all x1, starting transfers between devices, local(): lax.all_to_all(packed2.reshape(peers, cap // QUARTERS, QUARTERS * PAD), '...  9.24 us
    ppermute x3, waiting for transfers between devices, local(): lax.ppermute(modes_in, 'mode', [((to + s) % groups, to) for to in range(g...  5.69 us
    ppermute x3, starting transfers between devices, local(): lax.ppermute(modes_in, 'mode', [((to + s) % groups, to) for to in range(g...  5.29 us
    all_to_all x1, waiting for transfers between devices, local(): lax.all_to_all(packed2.reshape(peers, cap // QUARTERS, QUARTERS * PAD), '...  1.82 us
  transfers between devices with their start and end apart: 5, of which 3 were waited for; matrix products, arithmetic and copies ran while one was open for 0% of the time, Pallas kernels for 30%

profile of v4, /device:TPU:1, one launch (start us, length us, event | category | flops | bytes accessed | tf_op | source)
XLA Modules:
  0.0 61.4 jit_solution(7800364641333553099)
XLA Ops:
  0.6 3.6 %collective-permute-start = (bf16[30,2048]{1,0:T(8,128)(2,1)}, bf16[30,2048]{1,0:T(8,128)(2,1)S(1)}, u32[]{:S(2)}, u32[]{:S(2)}) collective-permute-start(bf16[30,2048]{1,0:T(8,128)(2,1)} %own_hbm.1), channel_id=1, source_target_pairs={{1,0},{2,1},{3,2},{0,3},{5,4},{6,5},{7,6},{4,7},{9,8},{10,9},{11,1... | collective-permute-start | bytes 368648 | tf_op jit(solution)/shard_map/ppermute | solution.py:300
  4.3 0.0 collective-permute-start.2
  4.3 1.6 %collective-permute-start.1 = (bf16[30,2048]{1,0:T(8,128)(2,1)}, bf16[30,2048]{1,0:T(8,128)(2,1)S(1)}, u32[]{:S(2)}, u32[]{:S(2)}) collective-permute-start(bf16[30,2048]{1,0:T(8,128)(2,1)} %own_hbm.1), channel_id=1, source_target_pairs={{2,0},{3,1},{0,2},{1,3},{6,4},{7,5},{4,6},{5,7},{10,8},{11,9},{8,1... | collective-permute-start | bytes 368648 | tf_op jit(solution)/shard_map/ppermute | solution.py:300
  5.9 1.5 %shard_map.86 = (bf16[128,640]{1,0:T(8,128)(2,1)S(1)}, bf16[512,256]{1,0:T(8,128)(2,1)S(1)}, bf16[30,2048]{1,0:T(8,128)(2,1)S(1)}, bf16[5,8,128,128]{3,2,1,0:T(8,128)(2,1)S(1)}) custom-call(s32[5,8,120]{2,1,0:T(8,128)} %bitcast.11, f32[5,8,120]{2,1,0:T(8,128)} %bitcast.13, s32[1,256]{1,0:T(1,128)} %bitcast.21, bf16[30,2048]{1,0:T(8,128)(2,1)} %own_hbm.1, ...), custom_call_target="tpu_custom_call" | custom-call | flops 1000000 | bytes 13818368 | tf_op jit(solution)/shard_map/pallas_call | solution.py:25
  7.4 0.0 collective-permute-done.v1
  7.4 5.7 %collective-permute-done.2.v3 = bf16[30,2048]{1,0:T(8,128)(2,1)S(1)} collective-permute-done((bf16[30,2048]{1,0:T(8,128)(2,1)}, bf16[30,2048]{1,0:T(8,128)(2,1)S(1)}, u32[]{:S(2)}, u32[]{:S(2)}) %collective-permute-start.2) | collective-permute-done | bytes 122912 | tf_op jit(solution)/shard_map/ppermute | solution.py:300
  13.1 0.0 collective-permute-done.1.v2
  13.1 2.4 %shard_map.87 = (bf16[512,128]{1,0:T(8,128)(2,1)}, bf16[16,4,32,128]{3,2,1,0:T(8,128)(2,1)}, bf16[128,640]{1,0:T(8,128)(2,1)}) custom-call(bf16[30,2048]{1,0:T(8,128)(2,1)S(1)} %get-tuple-element.19.v0, bf16[30,2048]{1,0:T(8,128)(2,1)S(1)} %collective-permute-done.v1, bf16[30,2048]{1,0:T(8,128)(2,1)S(1)} %collective-permute-done.1.v2, ...), custom_call_target="tpu_custom_call" | custom-call | flops 167772160 | bytes 3047712 | tf_op jit(solution)/shard_map/pallas_call | solution.py:25
  15.5 12.8 %all-to-all-start = ((bf16[64,8,128]{2,1,0:T(8,128)(2,1)}), bf16[64,8,128]{2,1,0:T(8,128)(2,1)S(1)}, u32[]{:S(2)}, u32[]{:S(2)}) async-start(bf16[64,8,128]{2,1,0:T(8,128)(2,1)} %bitcast.5), calls=%async_computation | async-start | bytes 262144 | tf_op jit(solution)/shard_map/all_to_all | solution.py:332
  28.3 9.2 %shard_map.88 = (f32[16,128,128]{2,1,0:T(8,128)S(1)}, f32[16,128,128]{2,1,0:T(8,128)}, bf16[16,512,128]{2,1,0:T(8,128)(2,1)S(1)}, bf16[32,640]{1,0:T(8,128)(2,1)S(1)}, bf16[32,640]{1,0:T(8,128)(2,1)}) custom-call(bf16[16,4,32,128]{3,2,1,0:T(8,128)(2,1)} %get-tuple-element.23.field_hbm, bf16[128,640]{1,0:T(8,128)(2,1)} %get-tuple-element.24.g_hbm, ...), custom_call_target="tpu_custom_call" | custom-call | flops 1342177280 | bytes 16801568 | tf_op jit(solution)/shard_map/pallas_call | solution.py:25
  37.6 1.1 %all-to-all-done = bf16[64,8,128]{2,1,0:T(8,128)(2,1)S(1)} async-done(((bf16[64,8,128]{2,1,0:T(8,128)(2,1)}), bf16[64,8,128]{2,1,0:T(8,128)(2,1)S(1)}, u32[]{:S(2)}, u32[]{:S(2)}) %all-to-all-start) | async-done | bytes 131104 | tf_op jit(solution)/shard_map/all_to_all | solution.py:332
  38.7 3.0 %shard_map.89 = (bf16[128,128]{1,0:T(8,128)(2,1)}, bf16[128,512]{1,0:T(8,128)(2,1)}) custom-call(f32[16,128,128]{2,1,0:T(8,128)S(1)} %get-tuple-element.26.own_ref, bf16[512,128]{1,0:T(8,128)(2,1)S(1)} %bitcast.9, bf16[16,512,128]{2,1,0:T(8,128)(2,1)S(1)} %get-tuple-element.28.r_ref, bf16[32,640]{1,0:T(8,128)(2,1)S(1)} %get-tuple-element.29.g2_ref, ...), custom_call_target="tpu_custom_call" | custom-call | flops 268435456 | bytes 15279392 | tf_op jit(solution)/shard_map/pallas_call | solution.py:25
  41.7 9.2 %all-to-all-start.1 = ((bf16[64,2,128]{2,1,0:T(2,128)(2,1)}), bf16[64,2,128]{2,1,0:T(2,128)(2,1)S(1)}, u32[]{:S(2)}, u32[]{:S(2)}) async-start(bf16[64,2,128]{2,1,0:T(2,128)(2,1)} %bitcast.7), calls=%async_computation.1 | async-start | bytes 65536 | tf_op jit(solution)/shard_map/all_to_all | solution.py:351
  50.9 7.4 %shard_map.90 = (bf16[30,2048]{1,0:T(8,128)(2,1)}, f32[32,2048]{1,0:T(8,128)S(1)}, bf16[16,512,128]{2,1,0:T(8,128)(2,1)S(1)}) custom-call(s32[4,18]{1,0:T(4,128)} %bitcast.18, s32[1,512]{1,0:T(1,128)} %bitcast.20, bf16[32,640]{1,0:T(8,128)(2,1)} %get-tuple-element.25.g2_hbm, bf16[128,512]{1,0:T(8,128)(2,1)} %get-tuple-element.30.turned_hbm, ...), custom_call_target="tpu_custom_call" | custom-call | flops 335544320 | bytes 15501600 | tf_op jit(solution)/shard_map/pallas_call | solution.py:25
  58.4 1.8 %all-to-all-done.1 = bf16[64,2,128]{2,1,0:T(2,128)(2,1)S(1)} async-done(((bf16[64,2,128]{2,1,0:T(2,128)(2,1)}), bf16[64,2,128]{2,1,0:T(2,128)(2,1)S(1)}, u32[]{:S(2)}, u32[]{:S(2)}) %all-to-all-start.1) | async-done | bytes 32800 | tf_op jit(solution)/shard_map/all_to_all | solution.py:351
  60.2 1.2 %shard_map.91 = bf16[30,2048]{1,0:T(8,128)(2,1)} custom-call(f32[32,2048]{1,0:T(8,128)S(1)} %get-tuple-element.33.own_ref, bf16[128,128]{1,0:T(8,128)(2,1)S(1)} %bitcast.10, bf16[16,512,128]{2,1,0:T(8,128)(2,1)S(1)} %get-tuple-element.35.r_ref), custom_call_target="tpu_custom_call" | custom-call | flops 67108864 | bytes 2514944 | tf_op jit(solution)/shard_map/pallas_call | solution.py:25
Async XLA Ops:
  0.6 6.8 %collective-permute-start = (bf16[30,2048]{1,0:T(8,128)(2,1)}, bf16[30,2048]{1,0:T(8,128)(2,1)S(1)}, u32[]{:S(2)}, u32[]{:S(2)}) collective-permute-start(bf16[30,2048]{1,0:T(8,128)(2,1)} %own_hbm.1), channel_id=1, source_target_pairs={{1,0},{2,1},{3,2},{0,3},{5,4},{6,5},{7,6},{4,7},{9,8},{10,9},{11,1... | collective-permute-start | bytes 368648 | tf_op jit(solution)/shard_map/ppermute | solution.py:300
  4.3 8.8 %collective-permute-start.2 = (bf16[30,2048]{1,0:T(8,128)(2,1)}, bf16[30,2048]{1,0:T(8,128)(2,1)S(1)}, u32[]{:S(2)}, u32[]{:S(2)}) collective-permute-start(bf16[30,2048]{1,0:T(8,128)(2,1)} %own_hbm.1), channel_id=1, source_target_pairs={{3,0},{0,1},{1,2},{2,3},{7,4},{4,5},{5,6},{6,7},{11,8},{8,9},{9,10... | collective-permute-start | bytes 368648 | tf_op jit(solution)/shard_map/ppermute | solution.py:300
  4.3 8.8 %collective-permute-start.1 = (bf16[30,2048]{1,0:T(8,128)(2,1)}, bf16[30,2048]{1,0:T(8,128)(2,1)S(1)}, u32[]{:S(2)}, u32[]{:S(2)}) collective-permute-start(bf16[30,2048]{1,0:T(8,128)(2,1)} %own_hbm.1), channel_id=1, source_target_pairs={{2,0},{3,1},{0,2},{1,3},{6,4},{7,5},{4,6},{5,7},{10,8},{11,9},{8,1... | collective-permute-start | bytes 368648 | tf_op jit(solution)/shard_map/ppermute | solution.py:300
  15.5 23.2 %all-to-all-start = ((bf16[64,8,128]{2,1,0:T(8,128)(2,1)}), bf16[64,8,128]{2,1,0:T(8,128)(2,1)S(1)}, u32[]{:S(2)}, u32[]{:S(2)}) async-start(bf16[64,8,128]{2,1,0:T(8,128)(2,1)} %bitcast.5), calls=%async_computation | async-start | bytes 262144 | tf_op jit(solution)/shard_map/all_to_all | solution.py:332
  41.7 18.5 %all-to-all-start.1 = ((bf16[64,2,128]{2,1,0:T(2,128)(2,1)}), bf16[64,2,128]{2,1,0:T(2,128)(2,1)S(1)}, u32[]{:S(2)}, u32[]{:S(2)}) async-start(bf16[64,2,128]{2,1,0:T(2,128)(2,1)} %bitcast.7), calls=%async_computation.1 | async-start | bytes 65536 | tf_op jit(solution)/shard_map/all_to_all | solution.py:351

commit v5 on v3

--- a/solution.py
+++ b/solution.py
@@ -97,13 +97,17 @@
     return dot(picked, stiff.reshape(terms * stored * LANES, LANES))
 
 
-def mix(mixer, field_ref, mixed_ref, start, stop):
-    rows = field_ref.shape[0] * field_ref.shape[1]
-    for at in range(start, stop, WIDTH):
-        field = field_ref[:, :, at:at + WIDTH].reshape(rows, WIDTH)
-        mixed = dot(mixer, field).astype(bf16)
-        for part in range(WIDTH // LANES):
-            mixed_ref[at // LANES + part] = mixed[:, part * LANES:(part + 1) * LANES]
+def mix(mixer, field_ref, mixed_ref):
+    blocks, groups, pad, lanes = field_ref.shape
+    for block in range(0, blocks, 2):
+        pair = [field_ref[block + part].reshape(groups * pad, lanes) for part in range(2)]
+        mixed = dot(mixer, jnp.concatenate(pair, axis=1)).astype(bf16)
+        for part in range(2):
+            mixed_ref[block + part] = mixed[:, part * lanes:(part + 1) * lanes]
+
+
+def stacked(wide):
+    return jnp.concatenate([wide[:, at:at + LANES] for at in range(0, wide.shape[1], LANES)], axis=0)
 
 
 def interface_part(rows, cols_ref, mixed_ref, stiff_ref):
@@ -121,11 +125,18 @@
     return blocks_ref.at[:, pl.ds(blocks_ref.shape[1] - count, count)]
 
 
-def setup_kernel(groups, cols_hbm, coef_hbm, send_hbm, own_hbm, blocks_ref,
-                 g_ref, place_ref, own_ref, stiff_ref, cols_ref, coef_ref, send_ref, sems):
+def mixed_row(picked, stiff, mixer):
+    terms, stored = stiff.shape[:2]
+    wide = jnp.concatenate([stiff[term].reshape(stored * LANES, LANES) for term in range(terms)], axis=1)
+    product = dot(picked, wide).astype(bf16)
+    return dot(mixer, jnp.concatenate([product[:, term * LANES:(term + 1) * LANES] for term in range(terms)], axis=0))
+
+
+def setup_kernel(groups, cols_hbm, coef_hbm, send_hbm, own_hbm, where_hbm, blocks_ref,
+                 g_ref, place_ref, own_ref, where_ref, stiff_ref, cols_ref, coef_ref, send_ref, sems):
     copies = begin(
         sems, (cols_hbm, cols_ref), (coef_hbm, coef_ref), (send_hbm, send_ref), (own_hbm, own_ref),
-        (last_stored(blocks_ref, stiff_ref), stiff_ref),
+        (where_hbm, where_ref), (last_stored(blocks_ref, stiff_ref), stiff_ref),
     )
     modes = cols_ref.shape[2]
     rows = groups * PAD
@@ -133,31 +144,35 @@
     spread = one_hot(padded_place(out_mode, groups, modes // groups) == lax.broadcasted_iota(i32, (rows, modes), 0))
     finish(copies[:3])
     for term in range(cols_ref.shape[0]):
-        g_ref[term * rows:(term + 1) * rows, :] = dot_t(spread, mixer_columns(term, groups, cols_ref, coef_ref)).astype(bf16)
+        g_ref[:, term * rows:(term + 1) * rows] = dot_t(spread, mixer_columns(term, groups, cols_ref, coef_ref)).astype(bf16)
     place_ref[...] = one_hot(send_ref[...] == lax.broadcasted_iota(i32, place_ref.shape, 0))
     finish(copies[3:])
 
 
-def first_kernel(groups, v0, v1, v2, v3, g_ref, place_ref, cols_hbm, stiff_ref,
-                 packed_ref, mixed_hbm, field_ref, mixed_ref, cols_ref, sems):
-    cols_copy = begin(sems, (cols_hbm, cols_ref))
+def first_kernel(groups, v0, v1, v2, v3, g_ref, place_ref, where_ref, stiff_ref,
+                 packed_ref, field_hbm, g_hbm, field_ref, sems):
+    copies = begin(sems, (g_ref, g_hbm))
     me = lax.axis_index("mode")
-    modes_dev, owned = v0.shape
-    field_ref[:, modes_dev:, :] = jnp.zeros_like(field_ref[:, modes_dev:, :])
+    owned_blocks, _, _, lanes = field_ref.shape
+    modes_dev = v0.shape[0]
+    field_ref[:, :, modes_dev:, :] = jnp.zeros_like(field_ref[:, :, modes_dev:, :])
     for slot, source in enumerate((v0, v1, v2, v3)):
-        field_ref[lax.rem(me + slot, groups), :modes_dev, :] = source[...]
+        group = lax.rem(me + slot, groups)
+        for block in range(owned_blocks):
+            field_ref[block, group, :modes_dev, :] = source[:, block * lanes:(block + 1) * lanes]
+    copies += begin(sems.at[pl.ds(1, 1)], (field_ref, field_hbm))
     mixer = g_ref[...]
-    pieces = 2
-    width = owned // pieces
-    keeps = []
-    for piece in range(pieces):
-        mix(mixer, field_ref, mixed_ref, piece * width, (piece + 1) * width)
-        at = pl.ds(piece * width // LANES, width // LANES)
-        keeps += begin(sems.at[pl.ds(1 + piece, 1)], (mixed_ref.at[at], mixed_hbm.at[at]))
-    finish(cols_copy)
-    part = interface_part(groups * PAD, cols_ref, mixed_ref, stiff_ref)
+    stored, out_blocks = where_ref.shape
+    parts = []
+    for row in range(owned_blocks, out_blocks):
+        picked = jnp.concatenate(
+            [field_ref[where_ref[c, row]].reshape(groups * PAD, lanes) for c in range(stored)], axis=1
+        )
+        at = (row - owned_blocks) * stored
+        parts.append(mixed_row(picked, stiff_ref[:, at:at + stored], mixer))
+    part = jnp.concatenate(parts, axis=1).astype(bf16)
     packed_ref[...] = dot_t(place_ref[...], part).astype(bf16)
-    finish(keeps)
+    finish(copies)
 
 
 def own_fetch(steps, stored, blocks_ref, stiff_ref, sems):
@@ -178,47 +193,53 @@
             )
 
 
-def between_kernel(groups, steps, mixed_hbm, cols_hbm, coef_hbm, recv_hbm, where_hbm, blocks_ref,
-                   own_ref, r_ref, g2_ref, mixed_ref, stiff_ref, cols_ref, coef_ref, recv_ref, where_ref, sems):
+def between_kernel(groups, steps, field_hbm, g_hbm, cols_hbm, coef_hbm, recv_hbm, send_hbm, where_hbm, blocks_ref,
+                   own_ref, r_ref, g2_ref, where_out, send_out, field_ref, g_ref, mixed_ref, stiff_ref,
+                   cols_ref, coef_ref, recv_ref, where_ref, sems):
     small = begin(
-        sems, (cols_hbm, cols_ref), (coef_hbm, coef_ref), (recv_hbm, recv_ref), (where_hbm, where_ref), (mixed_hbm, mixed_ref)
+        sems, (cols_hbm, cols_ref), (coef_hbm, coef_ref), (recv_hbm, recv_ref), (where_hbm, where_ref),
+        (g_hbm, g_ref), (field_hbm, field_ref), (where_hbm, where_out), (send_hbm, send_out),
     )
     copies = own_fetch(steps, where_ref.shape[0], blocks_ref, stiff_ref, sems.at[pl.ds(len(small), steps)])
     me = lax.axis_index("mode")
-    modes = cols_ref.shape[2]
+    terms, _, modes = cols_ref.shape
     modes_dev = modes // groups
     row = lax.broadcasted_iota(i32, (PAD, modes), 0)
     mine = one_hot((lax.broadcasted_iota(i32, (PAD, modes), 1) == row + me * modes_dev) & (row < modes_dev))
     finish(small[:3])
-    for term in range(cols_ref.shape[0]):
+    for term in range(terms):
         g2_ref[term * PAD:(term + 1) * PAD, :] = dot_t(mine, mixer_columns(term, groups, cols_ref, coef_ref)).astype(bf16)
     receive_table(recv_ref, r_ref)
     finish(small[3:])
+    mix(stacked(g_ref[...]), field_ref, mixed_ref)
     own_rows(groups * PAD, where_ref, mixed_ref, stiff_ref, copies, own_ref)
 
 
-def second_kernel(groups, own_ref, arrived_ref, r_ref, g2_ref, send_hbm, where_hbm, blocks_ref,
-                  first_ref, mixed_hbm, packed_ref, field_ref, mixed_ref, spread_ref, stiff_ref, send_ref, where_ref, sems):
-    small = begin(sems, (send_hbm, send_ref), (where_hbm, where_ref), (last_stored(blocks_ref, stiff_ref), stiff_ref))
+def second_kernel(groups, own_ref, arrived_ref, r_ref, g2_ref, send_ref, where_ref, blocks_ref,
+                  first_ref, mixed_hbm, packed_ref, field_ref, mixed_ref, spread_ref, stiff_ref, sems):
+    small = begin(sems, (last_stored(blocks_ref, stiff_ref), stiff_ref))
     me = lax.axis_index("mode")
     owned = own_ref.shape[1]
     arrived = arrived_ref[...].astype(f32).T.astype(bf16)
     for at in range(0, owned, WIDTH):
         total = own_ref[:, at:at + WIDTH] + dot(arrived, r_ref[:, at:at + WIDTH])
-        field_ref[:, :, at:at + WIDTH] = total.astype(bf16).reshape(groups, PAD, WIDTH)
-    first_ref[...] = field_ref[me, :first_ref.shape[0], :]
-    mix(g2_ref[...], field_ref, mixed_ref, 0, owned)
+        total = total.astype(bf16)
+        for part in range(0, WIDTH, LANES):
+            field_ref[(at + part) // LANES] = total[:, part:part + LANES].reshape(groups, PAD, LANES)
+    mix(g2_ref[...], field_ref, mixed_ref)
     keeps = begin(sems.at[pl.ds(len(small), 1)], (mixed_ref, mixed_hbm))
     spread_ref[...] = jnp.zeros_like(spread_ref)
     width = send_ref.shape[1]
-    finish(small)
     send = send_ref[...]
     lines = lax.broadcasted_iota(i32, (packed_ref.shape[0], width), 0) * QUARTERS
     place = jnp.concatenate([one_hot(send == lines + quarter) for quarter in range(QUARTERS)], axis=1)
+    finish(small)
     part = interface_part(PAD, where_ref, mixed_ref, stiff_ref)
     for quarter in range(QUARTERS):
         spread_ref[quarter * PAD:(quarter + 1) * PAD, quarter * width:(quarter + 1) * width] = part
     packed_ref[...] = dot_t(place, spread_ref[...]).astype(bf16)
+    for block in range(field_ref.shape[0]):
+        first_ref[:, block * LANES:(block + 1) * LANES] = field_ref[block, me, :first_ref.shape[0], :]
     finish(keeps)
 
 
@@ -272,40 +293,44 @@
     send_scratch, recv_scratch = pltpu.VMEM(send.shape, i32), pltpu.VMEM(recv.shape, i32)
     if_blocks = (terms, (out_blocks - owned_blocks) * stored, blk, blk)
     own_scratch = pltpu.VMEM((terms, owned_blocks * stored, blk, blk), bf16)
-    field_scratch = pltpu.VMEM((groups, PAD, owned), bf16)
+    field_shape, mixer_shape = (owned_blocks, groups, PAD, blk), (rows, terms * rows)
+    field_scratch = pltpu.VMEM(field_shape, bf16)
     block_flops = 2 * terms * stored * blk * blk
     wide, narrow = (owned_blocks, terms * rows, blk), (owned_blocks, terms * PAD, blk)
 
-    g, place, own_field, stiff = call(
+    g, place, own_field, where_near, stiff = call(
         functools.partial(setup_kernel, groups),
-        [Shape((terms * rows, rows), bf16), Shape((slots, interface), bf16), Shape((modes_dev, owned), bf16), Shape(if_blocks, bf16)],
-        [mix_cols, mix_coef, send, pin(modes_in), blocks], [HBM] * 5, [VMEM] * 4, flops=10**6,
-        scratch=[*tables, send_scratch, dma((5,))],
-    )
-    packed, mixed = call(
+        [Shape(mixer_shape, bf16), Shape((slots, interface), bf16), Shape((modes_dev, owned), bf16),
+         Shape(where.shape, i32), Shape(if_blocks, bf16)],
+        [mix_cols, mix_coef, send, pin(modes_in), where, blocks], [HBM] * 6, [VMEM] * 5, flops=10**6,
+        scratch=[*tables, send_scratch, dma((6,))],
+    )
+    packed, field, g_kept = call(
         functools.partial(first_kernel, groups),
-        [Shape((slots, rows), bf16), pltpu.HBM(wide, bf16)],
-        [own_field, others[1], others[2], others[3], g, place, where, stiff],
-        [VMEM] * 6 + [HBM, VMEM], [VMEM, HBM],
+        [Shape((slots, rows), bf16), pltpu.HBM(field_shape, bf16), pltpu.HBM(mixer_shape, bf16)],
+        [own_field, others[1], others[2], others[3], g, place, where_near, stiff],
+        [VMEM] * 6 + [SMEM, VMEM], [VMEM, HBM, HBM],
         flops=block_flops * (out_blocks - owned_blocks) * rows,
-        scratch=[field_scratch, pltpu.VMEM(wide, bf16), where_scratch, dma((3,))],
+        scratch=[field_scratch, dma((2,))],
     )
     arrived = lax.all_to_all(packed.reshape(peers, cap, rows), "space", split_axis=0, concat_axis=0, tiled=True)
     steps = 8
-    own, r, g2 = call(
+    own, r, g2, where_near, send_near = call(
         functools.partial(between_kernel, groups, steps),
-        [Shape((rows, owned), f32), Shape((slots, owned), bf16), Shape((terms * PAD, rows), bf16)],
-        [pin(mixed), mix_cols, mix_coef, recv, where, blocks], [HBM] * 6, [VMEM] * 3,
+        [Shape((rows, owned), f32), Shape((slots, owned), bf16), Shape((terms * PAD, rows), bf16),
+         Shape(where.shape, i32), Shape(send.shape, i32)],
+        [pin(field), pin(g_kept), mix_cols, mix_coef, recv, send, where, blocks], [HBM] * 8, [VMEM] * 5,
         flops=block_flops * owned_blocks * rows,
-        scratch=[pltpu.VMEM(wide, bf16), own_scratch, *tables, recv_scratch, where_scratch, dma((5 + steps,))],
+        scratch=[field_scratch, pltpu.VMEM(mixer_shape, bf16), pltpu.VMEM(wide, bf16), own_scratch, *tables, recv_scratch,
+                 where_scratch, dma((8 + steps,))],
     )
     first_apply, mixed2, packed2 = call(
         functools.partial(second_kernel, groups),
         [Shape((modes_dev, owned), bf16), pltpu.HBM(narrow, bf16), Shape((lines, QUARTERS * PAD), bf16)],
-        [own, arrived.reshape(slots, rows), r, g2, send, where, blocks],
-        [VMEM] * 4 + [HBM] * 3, [VMEM, HBM, VMEM], flops=2 * slots * rows * owned,
+        [own, arrived.reshape(slots, rows), r, g2, send_near, where_near, blocks],
+        [VMEM] * 5 + [SMEM, HBM], [VMEM, HBM, VMEM], flops=2 * slots * rows * owned,
         scratch=[field_scratch, pltpu.VMEM(narrow, bf16), pltpu.VMEM((QUARTERS * PAD, QUARTERS * interface), bf16),
-                 pltpu.VMEM(if_blocks, bf16), send_scratch, where_scratch, dma((4,))],
+                 pltpu.VMEM(if_blocks, bf16), dma((2,))],
     )
     arrived2 = lax.all_to_all(
         packed2.reshape(peers, cap // QUARTERS, QUARTERS * PAD), "space", split_axis=0, concat_axis=0, tiled=True

time: 59.5 us -> 58.9 us (0.990)
  Pallas kernels: 19.9 us -> 19.3 us
    pallas_call x6, Pallas kernels: 19.9 us -> 19.3 us  [call(): pl.pallas_call(kernel, out_shape=outs, in_specs=in_specs, out_specs=out_s...]
where the time goes in v5:
time: 58.9 us; the launch traced here: 58.6 us
  starting transfers between devices  24.5 us (42%)
  Pallas kernels  19.3 us (33%)
  waiting for transfers between devices  14.2 us (24%)
  between operations  0.7 us (1%)
    pallas_call x6, Pallas kernels, call(): pl.pallas_call(kernel, out_shape=outs, in_specs=in_specs, out_specs=out_s...  19.3 us
    all_to_all x1, starting transfers between devices, local(): lax.all_to_all(packed.reshape(peers, cap, rows), 'space', split_axis=0, c...  12.8 us
    all_to_all x1, starting transfers between devices, local(): lax.all_to_all(packed2.reshape(peers, cap // QUARTERS, QUARTERS * PAD), '...  6.36 us
    ppermute x3, waiting for transfers between devices, local(): lax.ppermute(modes_in, 'mode', [((to + s) % groups, to) for to in range(g...  5.66 us
    ppermute x3, starting transfers between devices, local(): lax.ppermute(modes_in, 'mode', [((to + s) % groups, to) for to in range(g...  5.29 us
    all_to_all x1, waiting for transfers between devices, local(): lax.all_to_all(packed2.reshape(peers, cap // QUARTERS, QUARTERS * PAD), '...  4.53 us
    all_to_all x1, waiting for transfers between devices, local(): lax.all_to_all(packed.reshape(peers, cap, rows), 'space', split_axis=0, c...  3.99 us
  transfers between devices with their start and end apart: 5, of which 3 were waited for; matrix products, arithmetic and copies ran while one was open for 0% of the time, Pallas kernels for 21%

profile of v5, /device:TPU:1, one launch (start us, length us, event | category | flops | bytes accessed | tf_op | source)
XLA Modules:
  0.0 58.6 jit_solution(5809656240408565799)
XLA Ops:
  0.6 3.6 %collective-permute-start = (bf16[30,2048]{1,0:T(8,128)(2,1)}, bf16[30,2048]{1,0:T(8,128)(2,1)S(1)}, u32[]{:S(2)}, u32[]{:S(2)}) collective-permute-start(bf16[30,2048]{1,0:T(8,128)(2,1)} %own_hbm.1), channel_id=1, source_target_pairs={{1,0},{2,1},{3,2},{0,3},{5,4},{6,5},{7,6},{4,7},{9,8},{10,9},{11,1... | collective-permute-start | bytes 368648 | tf_op jit(solution)/shard_map/ppermute | solution.py:284
  4.3 0.0 collective-permute-start.2
  4.3 1.6 %collective-permute-start.1 = (bf16[30,2048]{1,0:T(8,128)(2,1)}, bf16[30,2048]{1,0:T(8,128)(2,1)S(1)}, u32[]{:S(2)}, u32[]{:S(2)}) collective-permute-start(bf16[30,2048]{1,0:T(8,128)(2,1)} %own_hbm.1), channel_id=1, source_target_pairs={{2,0},{3,1},{0,2},{1,3},{6,4},{7,5},{4,6},{5,7},{10,8},{11,9},{8,1... | collective-permute-start | bytes 368648 | tf_op jit(solution)/shard_map/ppermute | solution.py:284
  5.9 1.5 %shard_map.86 = (bf16[128,640]{1,0:T(8,128)(2,1)S(1)}, bf16[512,256]{1,0:T(8,128)(2,1)S(1)}, bf16[30,2048]{1,0:T(8,128)(2,1)S(1)}, s32[4,18]{1,0:T(4,128)S(1)}, bf16[5,8,128,128]{3,2,1,0:T(8,128)(2,1)S(1)}) custom-call(s32[5,8,120]{2,1,0:T(8,128)} %bitcast.11, f32[5,8,120]{2,1,0:T(8,128)} %bitcast.13, s32[1,256]{1,0:T(1,128)} %bitcast.20, ...), custom_call_target="tpu_custom_call" | custom-call | flops 1000000 | bytes 13818944 | tf_op jit(solution)/shard_map/pallas_call | solution.py:25
  7.4 0.0 collective-permute-done.v1
  7.4 5.7 %collective-permute-done.2.v3 = bf16[30,2048]{1,0:T(8,128)(2,1)S(1)} collective-permute-done((bf16[30,2048]{1,0:T(8,128)(2,1)}, bf16[30,2048]{1,0:T(8,128)(2,1)S(1)}, u32[]{:S(2)}, u32[]{:S(2)}) %collective-permute-start.2) | collective-permute-done | bytes 122912 | tf_op jit(solution)/shard_map/ppermute | solution.py:284
  13.1 0.0 collective-permute-done.1.v2
  13.1 2.2 %shard_map.87 = (bf16[512,128]{1,0:T(8,128)(2,1)}, bf16[16,4,32,128]{3,2,1,0:T(8,128)(2,1)}, bf16[128,640]{1,0:T(8,128)(2,1)}) custom-call(bf16[30,2048]{1,0:T(8,128)(2,1)S(1)} %get-tuple-element.20.v0, bf16[30,2048]{1,0:T(8,128)(2,1)S(1)} %collective-permute-done.v1, bf16[30,2048]{1,0:T(8,128)(2,1)S(1)} %collective-permute-done.1.v2, ...), custom_call_target="tpu_custom_call" | custom-call | flops 167772160 | bytes 3047712 | tf_op jit(solution)/shard_map/pallas_call | solution.py:25
  15.3 12.8 %all-to-all-start = ((bf16[64,8,128]{2,1,0:T(8,128)(2,1)}), bf16[64,8,128]{2,1,0:T(8,128)(2,1)S(1)}, u32[]{:S(2)}, u32[]{:S(2)}) async-start(bf16[64,8,128]{2,1,0:T(8,128)(2,1)} %bitcast.5), calls=%async_computation | async-start | bytes 262144 | tf_op jit(solution)/shard_map/all_to_all | solution.py:316
  28.2 6.4 %shard_map.88 = (f32[128,2048]{1,0:T(8,128)S(1)}, bf16[512,2048]{1,0:T(8,128)(2,1)S(1)}, bf16[160,128]{1,0:T(8,128)(2,1)S(1)}, s32[4,18]{1,0:T(4,128)S(1)}, s32[1,256]{1,0:T(1,128)S(1)}) custom-call(bf16[16,4,32,128]{3,2,1,0:T(8,128)(2,1)} %get-tuple-element.25.field_hbm, bf16[128,640]{1,0:T(8,128)(2,1)} %get-tuple-element.26.g_hbm, s32[5,8,120]{2,1,0:T(8,128)} %bitcast.12, ...), custom_call_target="tpu_custom_call" | custom-call | flops 1342177280 | bytes 15714368 | tf_op jit(solution)/shard_map/pallas_call | solution.py:25
  34.5 4.0 %all-to-all-done = bf16[64,8,128]{2,1,0:T(8,128)(2,1)S(1)} async-done(((bf16[64,8,128]{2,1,0:T(8,128)(2,1)}), bf16[64,8,128]{2,1,0:T(8,128)(2,1)S(1)}, u32[]{:S(2)}, u32[]{:S(2)}) %all-to-all-start) | async-done | bytes 131104 | tf_op jit(solution)/shard_map/all_to_all | solution.py:316
  38.5 3.2 %shard_map.89 = (bf16[30,2048]{1,0:T(8,128)(2,1)}, bf16[16,160,128]{2,1,0:T(8,128)(2,1)}, bf16[128,128]{1,0:T(8,128)(2,1)}) custom-call(f32[128,2048]{1,0:T(8,128)S(1)} %get-tuple-element.27.own_ref, bf16[512,128]{1,0:T(8,128)(2,1)S(1)} %bitcast.9, bf16[512,2048]{1,0:T(8,128)(2,1)S(1)} %get-tuple-element.29.r_ref, ...), custom_call_target="tpu_custom_call" | custom-call | flops 268435456 | bytes 15926560 | tf_op jit(solution)/shard_map/pallas_call | solution.py:25
  41.8 6.4 %all-to-all-start.1 = ((bf16[64,2,128]{2,1,0:T(2,128)(2,1)}), bf16[64,2,128]{2,1,0:T(2,128)(2,1)S(1)}, u32[]{:S(2)}, u32[]{:S(2)}) async-start(bf16[64,2,128]{2,1,0:T(2,128)(2,1)} %bitcast.7), calls=%async_computation.1 | async-start | bytes 65536 | tf_op jit(solution)/shard_map/all_to_all | solution.py:335
  48.1 4.7 %shard_map.90 = (f32[32,2048]{1,0:T(8,128)S(1)}, bf16[512,2048]{1,0:T(8,128)(2,1)S(1)}) custom-call(s32[4,18]{1,0:T(4,128)} %bitcast.17, s32[1,512]{1,0:T(1,128)} %bitcast.19, bf16[16,160,128]{2,1,0:T(8,128)(2,1)} %get-tuple-element.34.mixed_hbm, bf16[5,72,128,128]{3,2,1,0:T(8,128)(2,1)} %blocks_ref.7), custom_call_target="tpu_custom_call" | custom-call | flops 335544320 | bytes 14813472 | tf_op jit(solution)/shard_map/pallas_call | solution.py:25
  52.8 4.5 %all-to-all-done.1 = bf16[64,2,128]{2,1,0:T(2,128)(2,1)S(1)} async-done(((bf16[64,2,128]{2,1,0:T(2,128)(2,1)}), bf16[64,2,128]{2,1,0:T(2,128)(2,1)S(1)}, u32[]{:S(2)}, u32[]{:S(2)}) %all-to-all-start.1) | async-done | bytes 32800 | tf_op jit(solution)/shard_map/all_to_all | solution.py:335
  57.4 1.3 %shard_map.91 = bf16[30,2048]{1,0:T(8,128)(2,1)} custom-call(f32[32,2048]{1,0:T(8,128)S(1)} %get-tuple-element.35.own_ref, bf16[128,128]{1,0:T(8,128)(2,1)S(1)} %bitcast.10, bf16[512,2048]{1,0:T(8,128)(2,1)S(1)} %get-tuple-element.37.r_ref), custom_call_target="tpu_custom_call" | custom-call | flops 67108864 | bytes 2514944 | tf_op jit(solution)/shard_map/pallas_call | solution.py:25
Async XLA Ops:
  0.6 6.8 %collective-permute-start = (bf16[30,2048]{1,0:T(8,128)(2,1)}, bf16[30,2048]{1,0:T(8,128)(2,1)S(1)}, u32[]{:S(2)}, u32[]{:S(2)}) collective-permute-start(bf16[30,2048]{1,0:T(8,128)(2,1)} %own_hbm.1), channel_id=1, source_target_pairs={{1,0},{2,1},{3,2},{0,3},{5,4},{6,5},{7,6},{4,7},{9,8},{10,9},{11,1... | collective-permute-start | bytes 368648 | tf_op jit(solution)/shard_map/ppermute | solution.py:284
  4.3 8.8 %collective-permute-start.2 = (bf16[30,2048]{1,0:T(8,128)(2,1)}, bf16[30,2048]{1,0:T(8,128)(2,1)S(1)}, u32[]{:S(2)}, u32[]{:S(2)}) collective-permute-start(bf16[30,2048]{1,0:T(8,128)(2,1)} %own_hbm.1), channel_id=1, source_target_pairs={{3,0},{0,1},{1,2},{2,3},{7,4},{4,5},{5,6},{6,7},{11,8},{8,9},{9,10... | collective-permute-start | bytes 368648 | tf_op jit(solution)/shard_map/ppermute | solution.py:284
  4.3 8.8 %collective-permute-start.1 = (bf16[30,2048]{1,0:T(8,128)(2,1)}, bf16[30,2048]{1,0:T(8,128)(2,1)S(1)}, u32[]{:S(2)}, u32[]{:S(2)}) collective-permute-start(bf16[30,2048]{1,0:T(8,128)(2,1)} %own_hbm.1), channel_id=1, source_target_pairs={{2,0},{3,1},{0,2},{1,3},{6,4},{7,5},{4,6},{5,7},{10,8},{11,9},{8,1... | collective-permute-start | bytes 368648 | tf_op jit(solution)/shard_map/ppermute | solution.py:284
  15.3 23.2 %all-to-all-start = ((bf16[64,8,128]{2,1,0:T(8,128)(2,1)}), bf16[64,8,128]{2,1,0:T(8,128)(2,1)S(1)}, u32[]{:S(2)}, u32[]{:S(2)}) async-start(bf16[64,8,128]{2,1,0:T(8,128)(2,1)} %bitcast.5), calls=%async_computation | async-start | bytes 262144 | tf_op jit(solution)/shard_map/all_to_all | solution.py:316
  41.8 15.6 %all-to-all-start.1 = ((bf16[64,2,128]{2,1,0:T(2,128)(2,1)}), bf16[64,2,128]{2,1,0:T(2,128)(2,1)S(1)}, u32[]{:S(2)}, u32[]{:S(2)}) async-start(bf16[64,2,128]{2,1,0:T(2,128)(2,1)} %bitcast.7), calls=%async_computation.1 | async-start | bytes 65536 | tf_op jit(solution)/shard_map/all_to_all | solution.py:335

commit v6 on v5

--- a/solution.py
+++ b/solution.py
@@ -132,26 +132,31 @@
     return dot(mixer, jnp.concatenate([product[:, term * LANES:(term + 1) * LANES] for term in range(terms)], axis=0))
 
 
-def setup_kernel(groups, cols_hbm, coef_hbm, send_hbm, own_hbm, where_hbm, blocks_ref,
-                 g_ref, place_ref, own_ref, where_ref, stiff_ref, cols_ref, coef_ref, send_ref, sems):
+def setup_kernel(groups, cols_hbm, coef_hbm, send_hbm, recv_hbm, own_hbm, where_hbm, blocks_ref,
+                 g_ref, g2_ref, place_ref, send_ref, recv_ref, own_ref, where_ref, stiff_ref, cols_ref, coef_ref, sems):
     copies = begin(
         sems, (cols_hbm, cols_ref), (coef_hbm, coef_ref), (send_hbm, send_ref), (own_hbm, own_ref),
-        (where_hbm, where_ref), (last_stored(blocks_ref, stiff_ref), stiff_ref),
-    )
+        (where_hbm, where_ref), (recv_hbm, recv_ref), (last_stored(blocks_ref, stiff_ref), stiff_ref),
+    )
+    me = lax.axis_index("mode")
     modes = cols_ref.shape[2]
     rows = groups * PAD
     out_mode = lax.broadcasted_iota(i32, (rows, modes), 1)
     spread = one_hot(padded_place(out_mode, groups, modes // groups) == lax.broadcasted_iota(i32, (rows, modes), 0))
     finish(copies[:3])
+    modes_dev = modes // groups
+    row = lax.broadcasted_iota(i32, (PAD, modes), 0)
+    mine = one_hot((lax.broadcasted_iota(i32, (PAD, modes), 1) == row + me * modes_dev) & (row < modes_dev))
     for term in range(cols_ref.shape[0]):
-        g_ref[:, term * rows:(term + 1) * rows] = dot_t(spread, mixer_columns(term, groups, cols_ref, coef_ref)).astype(bf16)
+        columns = mixer_columns(term, groups, cols_ref, coef_ref)
+        g_ref[:, term * rows:(term + 1) * rows] = dot_t(spread, columns).astype(bf16)
+        g2_ref[term * PAD:(term + 1) * PAD, :] = dot_t(mine, columns).astype(bf16)
     place_ref[...] = one_hot(send_ref[...] == lax.broadcasted_iota(i32, place_ref.shape, 0))
     finish(copies[3:])
 
 
 def first_kernel(groups, v0, v1, v2, v3, g_ref, place_ref, where_ref, stiff_ref,
-                 packed_ref, field_hbm, g_hbm, field_ref, sems):
-    copies = begin(sems, (g_ref, g_hbm))
+                 packed_ref, field_ref):
     me = lax.axis_index("mode")
     owned_blocks, _, _, lanes = field_ref.shape
     modes_dev = v0.shape[0]
@@ -160,7 +165,6 @@
         group = lax.rem(me + slot, groups)
         for block in range(owned_blocks):
             field_ref[block, group, :modes_dev, :] = source[:, block * lanes:(block + 1) * lanes]
-    copies += begin(sems.at[pl.ds(1, 1)], (field_ref, field_hbm))
     mixer = g_ref[...]
     stored, out_blocks = where_ref.shape
     parts = []
@@ -172,54 +176,38 @@
         parts.append(mixed_row(picked, stiff_ref[:, at:at + stored], mixer))
     part = jnp.concatenate(parts, axis=1).astype(bf16)
     packed_ref[...] = dot_t(place_ref[...], part).astype(bf16)
-    finish(copies)
-
-
-def own_fetch(steps, stored, blocks_ref, stiff_ref, sems):
-    count = stiff_ref.shape[1] // steps
-    return begin(
-        sems, *((blocks_ref.at[:, pl.ds(step * count, count)], stiff_ref.at[:, pl.ds(step * count, count)]) for step in range(steps))
-    )
-
-
-def own_rows(rows, cols_ref, mixed_ref, stiff_ref, copies, own_ref):
+
+
+def own_rows(rows, sizes, cols_ref, mixed_ref, stiff_ref, copies, own_ref):
     stored = cols_ref.shape[0]
-    per = mixed_ref.shape[0] // len(copies)
-    for step, copy in enumerate(copies):
+    row = 0
+    for size, copy in zip(sizes, copies):
         copy.wait()
-        for row in range(step * per, (step + 1) * per):
+        for row in range(row, row + size):
             own_ref[:, row * LANES:(row + 1) * LANES] = block_row(
                 row, rows, cols_ref, mixed_ref, stiff_ref[:, row * stored:(row + 1) * stored]
             )
-
-
-def between_kernel(groups, steps, field_hbm, g_hbm, cols_hbm, coef_hbm, recv_hbm, send_hbm, where_hbm, blocks_ref,
-                   own_ref, r_ref, g2_ref, where_out, send_out, field_ref, g_ref, mixed_ref, stiff_ref,
-                   cols_ref, coef_ref, recv_ref, where_ref, sems):
-    small = begin(
-        sems, (cols_hbm, cols_ref), (coef_hbm, coef_ref), (recv_hbm, recv_ref), (where_hbm, where_ref),
-        (g_hbm, g_ref), (field_hbm, field_ref), (where_hbm, where_out), (send_hbm, send_out),
-    )
-    copies = own_fetch(steps, where_ref.shape[0], blocks_ref, stiff_ref, sems.at[pl.ds(len(small), steps)])
-    me = lax.axis_index("mode")
-    terms, _, modes = cols_ref.shape
-    modes_dev = modes // groups
-    row = lax.broadcasted_iota(i32, (PAD, modes), 0)
-    mine = one_hot((lax.broadcasted_iota(i32, (PAD, modes), 1) == row + me * modes_dev) & (row < modes_dev))
-    finish(small[:3])
-    for term in range(terms):
-        g2_ref[term * PAD:(term + 1) * PAD, :] = dot_t(mine, mixer_columns(term, groups, cols_ref, coef_ref)).astype(bf16)
-    receive_table(recv_ref, r_ref)
-    finish(small[3:])
+        row += 1
+
+
+def own_fetch(sizes, stored, blocks_ref, stiff_ref, sems):
+    starts = [sum(sizes[:at]) for at in range(len(sizes))]
+    parts = [pl.ds(start * stored, size * stored) for start, size in zip(starts, sizes)]
+    return begin(sems, *((blocks_ref.at[:, part], stiff_ref.at[:, part]) for part in parts))
+
+
+def between_kernel(sizes, field_ref, g_ref, where_ref, blocks_ref, own_ref, mixed_ref, stiff_ref, sems):
+    copies = own_fetch(sizes, where_ref.shape[0], blocks_ref, stiff_ref, sems)
     mix(stacked(g_ref[...]), field_ref, mixed_ref)
-    own_rows(groups * PAD, where_ref, mixed_ref, stiff_ref, copies, own_ref)
-
-
-def second_kernel(groups, own_ref, arrived_ref, r_ref, g2_ref, send_ref, where_ref, blocks_ref,
-                  first_ref, mixed_hbm, packed_ref, field_ref, mixed_ref, spread_ref, stiff_ref, sems):
+    own_rows(g_ref.shape[0], sizes, where_ref, mixed_ref, stiff_ref, copies, own_ref)
+
+
+def second_kernel(groups, own_ref, arrived_ref, g2_ref, send_ref, recv_ref, where_ref, blocks_ref,
+                  first_ref, mixed_ref, packed_ref, field_ref, r_ref, spread_ref, stiff_ref, sems):
     small = begin(sems, (last_stored(blocks_ref, stiff_ref), stiff_ref))
     me = lax.axis_index("mode")
     owned = own_ref.shape[1]
+    receive_table(recv_ref, r_ref)
     arrived = arrived_ref[...].astype(f32).T.astype(bf16)
     for at in range(0, owned, WIDTH):
         total = own_ref[:, at:at + WIDTH] + dot(arrived, r_ref[:, at:at + WIDTH])
@@ -227,7 +215,6 @@
         for part in range(0, WIDTH, LANES):
             field_ref[(at + part) // LANES] = total[:, part:part + LANES].reshape(groups, PAD, LANES)
     mix(g2_ref[...], field_ref, mixed_ref)
-    keeps = begin(sems.at[pl.ds(len(small), 1)], (mixed_ref, mixed_hbm))
     spread_ref[...] = jnp.zeros_like(spread_ref)
     width = send_ref.shape[1]
     send = send_ref[...]
@@ -240,20 +227,15 @@
     packed_ref[...] = dot_t(place, spread_ref[...]).astype(bf16)
     for block in range(field_ref.shape[0]):
         first_ref[:, block * LANES:(block + 1) * LANES] = field_ref[block, me, :first_ref.shape[0], :]
-    finish(keeps)
-
-
-def own_kernel(steps, where_hbm, recv_hbm, mixed_hbm, blocks_ref, own_ref, r_ref,
-               mixed_ref, stiff_ref, recv_ref, where_ref, sems):
-    small = begin(sems, (recv_hbm, recv_ref), (where_hbm, where_ref), (mixed_hbm, mixed_ref))
-    copies = own_fetch(steps, where_ref.shape[0], blocks_ref, stiff_ref, sems.at[pl.ds(len(small), steps)])
-    finish(small[:1])
+
+
+def own_kernel(sizes, where_ref, mixed_ref, blocks_ref, own_ref, stiff_ref, sems):
+    copies = own_fetch(sizes, where_ref.shape[0], blocks_ref, stiff_ref, sems)
+    own_rows(PAD, sizes, where_ref, mixed_ref, stiff_ref, copies, own_ref)
+
+
+def last_kernel(own_ref, arrived_ref, recv_ref, out_ref, slots_ref, r_ref):
     receive_table(recv_ref, r_ref)
-    finish(small[1:])
-    own_rows(PAD, where_ref, mixed_ref, stiff_ref, copies, own_ref)
-
-
-def last_kernel(own_ref, arrived_ref, r_ref, out_ref, slots_ref):
     arrived = arrived_ref[...].astype(f32)
     lines = arrived.shape[0]
     for quarter in range(QUARTERS):
@@ -263,6 +245,12 @@
     for at in range(0, own_ref.shape[1], WIDTH):
         total = own_ref[:, at:at + WIDTH] + dot(by_slot, r_ref[:, at:at + WIDTH])
         out_ref[:, at:at + WIDTH] = total.astype(bf16)[:out_ref.shape[0], :]
+
+
+def uneven(rows):
+    last, rest = rows // 8, rows - rows // 8
+    third = -(-rest // 3)
+    return tuple(size for size in (third, third, rest - 2 * third, last) if size)
 
 
 def local(groups, peers, modes_in, blocks, block_cols, send_slot, recv_row, mix_cols, mix_coef):
@@ -289,8 +277,6 @@
     mix_cols, mix_coef = pin(mix_cols.transpose(0, 2, 1)), pin(mix_coef.transpose(0, 2, 1))
     send, recv = pin(send_slot.reshape(1, interface)), pin(recv_row.reshape(1, slots))
     tables = [pltpu.VMEM(mix_cols.shape, i32), pltpu.VMEM(mix_coef.shape, f32)]
-    where_scratch = pltpu.SMEM(where.shape, i32)
-    send_scratch, recv_scratch = pltpu.VMEM(send.shape, i32), pltpu.VMEM(recv.shape, i32)
     if_blocks = (terms, (out_blocks - owned_blocks) * stored, blk, blk)
     own_scratch = pltpu.VMEM((terms, owned_blocks * stored, blk, blk), bf16)
     field_shape, mixer_shape = (owned_blocks, groups, PAD, blk), (rows, terms * rows)
@@ -298,52 +284,46 @@
     block_flops = 2 * terms * stored * blk * blk
     wide, narrow = (owned_blocks, terms * rows, blk), (owned_blocks, terms * PAD, blk)
 
-    g, place, own_field, where_near, stiff = call(
+    g, g2, place, send, recv, own_field, where, stiff = call(
         functools.partial(setup_kernel, groups),
-        [Shape(mixer_shape, bf16), Shape((slots, interface), bf16), Shape((modes_dev, owned), bf16),
-         Shape(where.shape, i32), Shape(if_blocks, bf16)],
-        [mix_cols, mix_coef, send, pin(modes_in), where, blocks], [HBM] * 6, [VMEM] * 5, flops=10**6,
-        scratch=[*tables, send_scratch, dma((6,))],
-    )
-    packed, field, g_kept = call(
+        [Shape(mixer_shape, bf16), Shape((terms * PAD, rows), bf16), Shape((slots, interface), bf16), Shape(send.shape, i32),
+         Shape(recv.shape, i32), Shape((modes_dev, owned), bf16), Shape(where.shape, i32), Shape(if_blocks, bf16)],
+        [mix_cols, mix_coef, send, recv, pin(modes_in), where, blocks], [HBM] * 7, [VMEM] * 8, flops=10**6,
+        scratch=[*tables, dma((7,))],
+    )
+    packed, field = call(
         functools.partial(first_kernel, groups),
-        [Shape((slots, rows), bf16), pltpu.HBM(field_shape, bf16), pltpu.HBM(mixer_shape, bf16)],
-        [own_field, others[1], others[2], others[3], g, place, where_near, stiff],
-        [VMEM] * 6 + [SMEM, VMEM], [VMEM, HBM, HBM],
-        flops=block_flops * (out_blocks - owned_blocks) * rows,
-        scratch=[field_scratch, dma((2,))],
+        [Shape((slots, rows), bf16), Shape(field_shape, bf16)],
+        [own_field, others[1], others[2], others[3], g, place, where, stiff],
+        [VMEM] * 6 + [SMEM, VMEM], [VMEM] * 2, flops=block_flops * (out_blocks - owned_blocks) * rows,
     )
     arrived = lax.all_to_all(packed.reshape(peers, cap, rows), "space", split_axis=0, concat_axis=0, tiled=True)
-    steps = 8
-    own, r, g2, where_near, send_near = call(
-        functools.partial(between_kernel, groups, steps),
-        [Shape((rows, owned), f32), Shape((slots, owned), bf16), Shape((terms * PAD, rows), bf16),
-         Shape(where.shape, i32), Shape(send.shape, i32)],
-        [pin(field), pin(g_kept), mix_cols, mix_coef, recv, send, where, blocks], [HBM] * 8, [VMEM] * 5,
-        flops=block_flops * owned_blocks * rows,
-        scratch=[field_scratch, pltpu.VMEM(mixer_shape, bf16), pltpu.VMEM(wide, bf16), own_scratch, *tables, recv_scratch,
-                 where_scratch, dma((8 + steps,))],
-    )
+    sizes = uneven(owned_blocks)
+    own = call(
+        functools.partial(between_kernel, sizes), [Shape((rows, owned), f32)],
+        [field, g, where, blocks], [VMEM] * 2 + [SMEM, HBM], [VMEM], flops=block_flops * owned_blocks * rows,
+        scratch=[pltpu.VMEM(wide, bf16), own_scratch, dma((len(sizes),))],
+    )[0]
     first_apply, mixed2, packed2 = call(
         functools.partial(second_kernel, groups),
-        [Shape((modes_dev, owned), bf16), pltpu.HBM(narrow, bf16), Shape((lines, QUARTERS * PAD), bf16)],
-        [own, arrived.reshape(slots, rows), r, g2, send_near, where_near, blocks],
-        [VMEM] * 5 + [SMEM, HBM], [VMEM, HBM, VMEM], flops=2 * slots * rows * owned,
-        scratch=[field_scratch, pltpu.VMEM(narrow, bf16), pltpu.VMEM((QUARTERS * PAD, QUARTERS * interface), bf16),
-                 pltpu.VMEM(if_blocks, bf16), dma((2,))],
+        [Shape((modes_dev, owned), bf16), Shape(narrow, bf16), Shape((lines, QUARTERS * PAD), bf16)],
+        [own, arrived.reshape(slots, rows), g2, send, recv, where, blocks],
+        [VMEM] * 5 + [SMEM, HBM], [VMEM] * 3, flops=2 * slots * rows * owned,
+        scratch=[field_scratch, pltpu.VMEM((slots, owned), bf16), pltpu.VMEM((QUARTERS * PAD, QUARTERS * interface), bf16),
+                 pltpu.VMEM(if_blocks, bf16), dma((1,))],
     )
     arrived2 = lax.all_to_all(
         packed2.reshape(peers, cap // QUARTERS, QUARTERS * PAD), "space", split_axis=0, concat_axis=0, tiled=True
     )
-    own2, r2 = call(
-        functools.partial(own_kernel, steps), [Shape((PAD, owned), f32), Shape((slots, owned), bf16)],
-        [where, recv, pin(mixed2), blocks], [HBM] * 4, [VMEM] * 2, flops=block_flops * owned_blocks * PAD,
-        scratch=[pltpu.VMEM(narrow, bf16), own_scratch, recv_scratch, where_scratch, dma((3 + steps,))],
-    )
+    own2 = call(
+        functools.partial(own_kernel, sizes), [Shape((PAD, owned), f32)],
+        [where, mixed2, blocks], [SMEM, VMEM, HBM], [VMEM], flops=block_flops * owned_blocks * PAD,
+        scratch=[own_scratch, dma((len(sizes),))],
+    )[0]
     second_apply = call(
         last_kernel, [Shape((modes_dev, owned), bf16)],
-        [own2, arrived2.reshape(lines, QUARTERS * PAD), r2], [VMEM] * 3, [VMEM],
-        flops=2 * slots * PAD * owned, scratch=[pltpu.VMEM((slots, QUARTERS * PAD), f32)],
+        [own2, arrived2.reshape(lines, QUARTERS * PAD), recv], [VMEM] * 3, [VMEM], flops=2 * slots * PAD * owned,
+        scratch=[pltpu.VMEM((slots, QUARTERS * PAD), f32), pltpu.VMEM((slots, owned), bf16)],
     )[0]
     return (first_apply, second_apply)
 

time: 58.9 us -> 59.9 us (1.017)
  Pallas kernels: 19.3 us -> 20.9 us
  waiting for transfers between devices: 14.2 us -> 13.4 us
    pallas_call x6, Pallas kernels: 19.3 us -> 20.9 us  [call(): pl.pallas_call(kernel, out_shape=outs, in_specs=in_specs, out_specs=out_s...]
  transfers between devices with their start and end apart: 5 -> 5, of which waited for: 3 -> 3; matrix products, arithmetic and copies ran while one was open for 0% -> 0% of each run, Pallas kernels for 21% -> 22%
where the time goes in v6:
time: 59.9 us; the launch traced here: 59.7 us
  starting transfers between devices  24.7 us (41%)
  Pallas kernels  20.9 us (35%)
  waiting for transfers between devices  13.4 us (22%)
  between operations  0.69 us (1%)
    pallas_call x6, Pallas kernels, call(): pl.pallas_call(kernel, out_shape=outs, in_specs=in_specs, out_specs=out_s...  20.9 us
    all_to_all x1, starting transfers between devices, local(): lax.all_to_all(packed.reshape(peers, cap, rows), 'space', split_axis=0, c...  12.8 us
    all_to_all x1, starting transfers between devices, local(): lax.all_to_all(packed2.reshape(peers, cap // QUARTERS, QUARTERS * PAD), '...  6.56 us
    ppermute x3, waiting for transfers between devices, local(): lax.ppermute(modes_in, 'mode', [((to + s) % groups, to) for to in range(g...  5.64 us
    ppermute x3, starting transfers between devices, local(): lax.ppermute(modes_in, 'mode', [((to + s) % groups, to) for to in range(g...  5.29 us
    all_to_all x1, waiting for transfers between devices, local(): lax.all_to_all(packed2.reshape(peers, cap // QUARTERS, QUARTERS * PAD), '...  4.02 us
    all_to_all x1, waiting for transfers between devices, local(): lax.all_to_all(packed.reshape(peers, cap, rows), 'space', split_axis=0, c...  3.78 us
  transfers between devices with their start and end apart: 5, of which 3 were waited for; matrix products, arithmetic and copies ran while one was open for 0% of the time, Pallas kernels for 22%

profile of v6, /device:TPU:1, one launch (start us, length us, event | category | flops | bytes accessed | tf_op | source)
XLA Modules:
  0.0 59.7 jit_solution(5776561933326454694)
XLA Ops:
  0.6 3.6 %collective-permute-start = (bf16[30,2048]{1,0:T(8,128)(2,1)}, bf16[30,2048]{1,0:T(8,128)(2,1)S(1)}, u32[]{:S(2)}, u32[]{:S(2)}) collective-permute-start(bf16[30,2048]{1,0:T(8,128)(2,1)} %own_hbm.1), channel_id=1, source_target_pairs={{1,0},{2,1},{3,2},{0,3},{5,4},{6,5},{7,6},{4,7},{9,8},{10,9},{11,1... | collective-permute-start | bytes 368648 | tf_op jit(solution)/shard_map/ppermute | solution.py:272
  4.3 0.0 collective-permute-start.2
  4.3 1.6 %collective-permute-start.1 = (bf16[30,2048]{1,0:T(8,128)(2,1)}, bf16[30,2048]{1,0:T(8,128)(2,1)S(1)}, u32[]{:S(2)}, u32[]{:S(2)}) collective-permute-start(bf16[30,2048]{1,0:T(8,128)(2,1)} %own_hbm.1), channel_id=1, source_target_pairs={{2,0},{3,1},{0,2},{1,3},{6,4},{7,5},{4,6},{5,7},{10,8},{11,9},{8,1... | collective-permute-start | bytes 368648 | tf_op jit(solution)/shard_map/ppermute | solution.py:272
  5.9 1.5 %shard_map.86 = (bf16[128,640]{1,0:T(8,128)(2,1)S(1)}, bf16[160,128]{1,0:T(8,128)(2,1)S(1)}, bf16[512,256]{1,0:T(8,128)(2,1)S(1)}, s32[1,256]{1,0:T(1,128)S(1)},...) custom-call(s32[5,8,120]{2,1,0:T(8,128)} %bitcast.11, ...), custom_call_target="tpu_custom_call" | custom-call | flops 1000000 | bytes 13865024 | tf_op jit(solution)/shard_map/pallas_call | solution.py:25
  7.5 0.0 collective-permute-done.v1
  7.5 5.6 %collective-permute-done.2.v3 = bf16[30,2048]{1,0:T(8,128)(2,1)S(1)} collective-permute-done((bf16[30,2048]{1,0:T(8,128)(2,1)}, bf16[30,2048]{1,0:T(8,128)(2,1)S(1)}, u32[]{:S(2)}, u32[]{:S(2)}) %collective-permute-start.2) | collective-permute-done | bytes 122912 | tf_op jit(solution)/shard_map/ppermute | solution.py:272
  13.1 0.0 collective-permute-done.1.v2
  13.1 2.2 %shard_map.87 = (bf16[512,128]{1,0:T(8,128)(2,1)}, bf16[16,4,32,128]{3,2,1,0:T(8,128)(2,1)S(1)}) custom-call(bf16[30,2048]{1,0:T(8,128)(2,1)S(1)} %get-tuple-element.15.v0, bf16[30,2048]{1,0:T(8,128)(2,1)S(1)} %collective-permute-done.v1, bf16[30,2048]{1,0:T(8,128)(2,1)S(1)} %collective-permute-done.1.v2, bf16[30,2048]{1,0:T(8,128)(2,1)S(1)} %collective-permute-done.2.v3, ...), custom_call_target="tpu_custom_call" | custom-call | flops 167772160 | bytes 2883872 | tf_op jit(solution)/shard_map/pallas_call | solution.py:25
  15.3 12.8 %all-to-all-start = ((bf16[64,8,128]{2,1,0:T(8,128)(2,1)}), bf16[64,8,128]{2,1,0:T(8,128)(2,1)S(1)}, u32[]{:S(2)}, u32[]{:S(2)}) async-start(bf16[64,8,128]{2,1,0:T(8,128)(2,1)} %bitcast.5), calls=%async_computation | async-start | bytes 262144 | tf_op jit(solution)/shard_map/all_to_all | solution.py:300
  28.1 6.6 %shard_map.88.own_ref = f32[128,2048]{1,0:T(8,128)S(1)} custom-call(bf16[16,4,32,128]{3,2,1,0:T(8,128)(2,1)S(1)} %get-tuple-element.20.field_ref, bf16[128,640]{1,0:T(8,128)(2,1)S(1)} %get-tuple-element.16.g_ref, s32[4,18]{1,0:T(4,128)S(1)} %get-tuple-element.18.where_ref, bf16[5,72,128,128]{3,2,1,0:T(8,128)(2,1)} %blocks_ref.7), custom_call_target="tpu_custom_call" | custom-call | flops 1342177280 | bytes 13533472 | tf_op jit(solution)/shard_map/pallas_call | solution.py:25
  34.7 3.8 %all-to-all-done = bf16[64,8,128]{2,1,0:T(8,128)(2,1)S(1)} async-done(((bf16[64,8,128]{2,1,0:T(8,128)(2,1)}), bf16[64,8,128]{2,1,0:T(8,128)(2,1)S(1)}, u32[]{:S(2)}, u32[]{:S(2)}) %all-to-all-start) | async-done | bytes 131104 | tf_op jit(solution)/shard_map/all_to_all | solution.py:300
  38.5 4.0 %shard_map.89 = (bf16[30,2048]{1,0:T(8,128)(2,1)}, bf16[16,160,128]{2,1,0:T(8,128)(2,1)S(1)}, bf16[128,128]{1,0:T(8,128)(2,1)}) custom-call(f32[128,2048]{1,0:T(8,128)S(1)} %shard_map.88.own_ref, bf16[512,128]{1,0:T(8,128)(2,1)S(1)} %bitcast.9, bf16[160,128]{1,0:T(8,128)(2,1)S(1)} %get-tuple-element.22.g2_ref, s32[1,256]{1,0:T(1,128)S(1)} %get-tuple-element.23.send_ref, ...), custom_call_target="tpu_custom_call" | custom-call | flops 268435456 | bytes 13831456 | tf_op jit(solution)/shard_map/pallas_call | solution.py:25
  42.5 6.6 %all-to-all-start.1 = ((bf16[64,2,128]{2,1,0:T(2,128)(2,1)}), bf16[64,2,128]{2,1,0:T(2,128)(2,1)S(1)}, u32[]{:S(2)}, u32[]{:S(2)}) async-start(bf16[64,2,128]{2,1,0:T(2,128)(2,1)} %bitcast.7), calls=%async_computation.1 | async-start | bytes 65536 | tf_op jit(solution)/shard_map/all_to_all | solution.py:315
  49.1 5.2 %shard_map.90.own_ref = f32[32,2048]{1,0:T(8,128)S(1)} custom-call(s32[4,18]{1,0:T(4,128)S(1)} %get-tuple-element.18.where_ref, bf16[16,160,128]{2,1,0:T(8,128)(2,1)S(1)} %get-tuple-element.26.mixed_ref, bf16[5,72,128,128]{3,2,1,0:T(8,128)(2,1)} %blocks_ref.7), custom_call_target="tpu_custom_call" | custom-call | flops 335544320 | bytes 12714272 | tf_op jit(solution)/shard_map/pallas_call | solution.py:25
  54.3 4.0 %all-to-all-done.1 = bf16[64,2,128]{2,1,0:T(2,128)(2,1)S(1)} async-done(((bf16[64,2,128]{2,1,0:T(2,128)(2,1)}), bf16[64,2,128]{2,1,0:T(2,128)(2,1)S(1)}, u32[]{:S(2)}, u32[]{:S(2)}) %all-to-all-start.1) | async-done | bytes 32800 | tf_op jit(solution)/shard_map/all_to_all | solution.py:315
  58.3 1.4 %shard_map.91 = bf16[30,2048]{1,0:T(8,128)(2,1)} custom-call(f32[32,2048]{1,0:T(8,128)S(1)} %shard_map.90.own_ref, bf16[128,128]{1,0:T(8,128)(2,1)S(1)} %bitcast.10, s32[1,512]{1,0:T(1,128)S(1)} %get-tuple-element.24.recv_ref), custom_call_target="tpu_custom_call" | custom-call | flops 67108864 | bytes 419840 | tf_op jit(solution)/shard_map/pallas_call | solution.py:25
Async XLA Ops:
  0.6 6.8 %collective-permute-start = (bf16[30,2048]{1,0:T(8,128)(2,1)}, bf16[30,2048]{1,0:T(8,128)(2,1)S(1)}, u32[]{:S(2)}, u32[]{:S(2)}) collective-permute-start(bf16[30,2048]{1,0:T(8,128)(2,1)} %own_hbm.1), channel_id=1, source_target_pairs={{1,0},{2,1},{3,2},{0,3},{5,4},{6,5},{7,6},{4,7},{9,8},{10,9},{11,1... | collective-permute-start | bytes 368648 | tf_op jit(solution)/shard_map/ppermute | solution.py:272
  4.3 8.8 %collective-permute-start.2 = (bf16[30,2048]{1,0:T(8,128)(2,1)}, bf16[30,2048]{1,0:T(8,128)(2,1)S(1)}, u32[]{:S(2)}, u32[]{:S(2)}) collective-permute-start(bf16[30,2048]{1,0:T(8,128)(2,1)} %own_hbm.1), channel_id=1, source_target_pairs={{3,0},{0,1},{1,2},{2,3},{7,4},{4,5},{5,6},{6,7},{11,8},{8,9},{9,10... | collective-permute-start | bytes 368648 | tf_op jit(solution)/shard_map/ppermute | solution.py:272
  4.3 8.8 %collective-permute-start.1 = (bf16[30,2048]{1,0:T(8,128)(2,1)}, bf16[30,2048]{1,0:T(8,128)(2,1)S(1)}, u32[]{:S(2)}, u32[]{:S(2)}) collective-permute-start(bf16[30,2048]{1,0:T(8,128)(2,1)} %own_hbm.1), channel_id=1, source_target_pairs={{2,0},{3,1},{0,2},{1,3},{6,4},{7,5},{4,6},{5,7},{10,8},{11,9},{8,1... | collective-permute-start | bytes 368648 | tf_op jit(solution)/shard_map/ppermute | solution.py:272
  15.3 23.2 %all-to-all-start = ((bf16[64,8,128]{2,1,0:T(8,128)(2,1)}), bf16[64,8,128]{2,1,0:T(8,128)(2,1)S(1)}, u32[]{:S(2)}, u32[]{:S(2)}) async-start(bf16[64,8,128]{2,1,0:T(8,128)(2,1)} %bitcast.5), calls=%async_computation | async-start | bytes 262144 | tf_op jit(solution)/shard_map/all_to_all | solution.py:300
  42.5 15.8 %all-to-all-start.1 = ((bf16[64,2,128]{2,1,0:T(2,128)(2,1)}), bf16[64,2,128]{2,1,0:T(2,128)(2,1)S(1)}, u32[]{:S(2)}, u32[]{:S(2)}) async-start(bf16[64,2,128]{2,1,0:T(2,128)(2,1)} %bitcast.7), calls=%async_computation.1 | async-start | bytes 65536 | tf_op jit(solution)/shard_map/all_to_all | solution.py:315

commit v7 on v6

--- a/solution.py
+++ b/solution.py
@@ -76,12 +76,19 @@
     return total.astype(bf16)
 
 
-def receive_table(recv_ref, r_ref):
+def by_quarter(rows_ref, quarter):
+    return rows_ref[pl.ds(quarter, rows_ref.shape[0] // QUARTERS, stride=QUARTERS), :]
+
+
+def receive_table(recv_ref, r_ref, turned_ref):
     slots = recv_ref.shape[1]
-    turned = jnp.broadcast_to(recv_ref[...].astype(f32), (LANES, slots)).T
-    wanted = turned[:, :1].astype(i32)
-    for at in range(0, r_ref.shape[1], WIDTH):
-        r_ref[:, at:at + WIDTH] = one_hot(wanted == lax.broadcasted_iota(i32, (slots, WIDTH), 1) + at)
+    turned_ref[...] = jnp.broadcast_to(recv_ref[...].astype(f32), (LANES, slots)).T
+    lanes = lax.broadcasted_iota(i32, (slots // QUARTERS, LANES), 1)
+    for quarter in range(QUARTERS):
+        offset = by_quarter(turned_ref, quarter).astype(i32) - lanes
+        at = slice(quarter * slots // QUARTERS, (quarter + 1) * slots // QUARTERS)
+        for block in range(r_ref.shape[0]):
+            r_ref[block, at, :] = one_hot(offset == block * LANES)
 
 
 def block_row(row, rows, cols_ref, mixed_ref, stiff):
@@ -108,16 +115,6 @@
 
 def stacked(wide):
     return jnp.concatenate([wide[:, at:at + LANES] for at in range(0, wide.shape[1], LANES)], axis=0)
-
-
-def interface_part(rows, cols_ref, mixed_ref, stiff_ref):
-    stored, out_blocks = cols_ref.shape
-    owned_blocks = mixed_ref.shape[0]
-    parts = [
-        block_row(row, rows, cols_ref, mixed_ref, stiff_ref[:, (row - owned_blocks) * stored:(row - owned_blocks + 1) * stored])
-        for row in range(owned_blocks, out_blocks)
-    ]
-    return jnp.concatenate(parts, axis=1).astype(bf16)
 
 
 def last_stored(blocks_ref, stiff_ref):
@@ -156,7 +153,8 @@
 
 
 def first_kernel(groups, v0, v1, v2, v3, g_ref, place_ref, where_ref, stiff_ref,
-                 packed_ref, field_ref):
+                 packed_ref, field_hbm, g_hbm, field_ref, sems):
+    copies = begin(sems, (g_ref, g_hbm))
     me = lax.axis_index("mode")
     owned_blocks, _, _, lanes = field_ref.shape
     modes_dev = v0.shape[0]
@@ -165,6 +163,7 @@
         group = lax.rem(me + slot, groups)
         for block in range(owned_blocks):
             field_ref[block, group, :modes_dev, :] = source[:, block * lanes:(block + 1) * lanes]
+    copies += begin(sems.at[pl.ds(1, 1)], (field_ref, field_hbm))
     mixer = g_ref[...]
     stored, out_blocks = where_ref.shape
     parts = []
@@ -176,81 +175,103 @@
         parts.append(mixed_row(picked, stiff_ref[:, at:at + stored], mixer))
     part = jnp.concatenate(parts, axis=1).astype(bf16)
     packed_ref[...] = dot_t(place_ref[...], part).astype(bf16)
-
-
-def own_rows(rows, sizes, cols_ref, mixed_ref, stiff_ref, copies, own_ref):
-    stored = cols_ref.shape[0]
-    row = 0
-    for size, copy in zip(sizes, copies):
-        copy.wait()
-        for row in range(row, row + size):
-            own_ref[:, row * LANES:(row + 1) * LANES] = block_row(
-                row, rows, cols_ref, mixed_ref, stiff_ref[:, row * stored:(row + 1) * stored]
+    finish(copies)
+
+
+def own_fetch(steps, stored, blocks_ref, stiff_ref, sems):
+    count = stiff_ref.shape[1] // steps
+    parts = [pl.ds(step * count, count) for step in range(steps)]
+    return begin(sems, *((blocks_ref.at[:, part], stiff_ref.at[:, part]) for part in parts))
+
+
+def between_kernel(steps, field_hbm, g_hbm, recv_ref, where_ref, blocks_ref,
+                   own_ref, r_ref, field_ref, g_ref, mixed_ref, stiff_ref, turned_ref, sems):
+    near = begin(sems, (field_hbm, field_ref), (g_hbm, g_ref))
+    stored = where_ref.shape[0]
+    copies = own_fetch(steps, stored, blocks_ref, stiff_ref, sems.at[pl.ds(len(near), steps)])
+    receive_table(recv_ref, r_ref, turned_ref)
+    finish(near)
+    mix(stacked(g_ref[...]), field_ref, mixed_ref)
+    per = own_ref.shape[0] // steps
+    for step in range(steps):
+        copies[step].wait()
+        for row in range(step * per, (step + 1) * per):
+            own_ref[row] = block_row(
+                row, own_ref.shape[1], where_ref, mixed_ref, stiff_ref[:, row * stored:(row + 1) * stored]
             )
-        row += 1
-
-
-def own_fetch(sizes, stored, blocks_ref, stiff_ref, sems):
-    starts = [sum(sizes[:at]) for at in range(len(sizes))]
-    parts = [pl.ds(start * stored, size * stored) for start, size in zip(starts, sizes)]
-    return begin(sems, *((blocks_ref.at[:, part], stiff_ref.at[:, part]) for part in parts))
-
-
-def between_kernel(sizes, field_ref, g_ref, where_ref, blocks_ref, own_ref, mixed_ref, stiff_ref, sems):
-    copies = own_fetch(sizes, where_ref.shape[0], blocks_ref, stiff_ref, sems)
-    mix(stacked(g_ref[...]), field_ref, mixed_ref)
-    own_rows(g_ref.shape[0], sizes, where_ref, mixed_ref, stiff_ref, copies, own_ref)
-
-
-def second_kernel(groups, own_ref, arrived_ref, g2_ref, send_ref, recv_ref, where_ref, blocks_ref,
-                  first_ref, mixed_ref, packed_ref, field_ref, r_ref, spread_ref, stiff_ref, sems):
-    small = begin(sems, (last_stored(blocks_ref, stiff_ref), stiff_ref))
-    me = lax.axis_index("mode")
-    owned = own_ref.shape[1]
-    receive_table(recv_ref, r_ref)
-    arrived = arrived_ref[...].astype(f32).T.astype(bf16)
-    for at in range(0, owned, WIDTH):
-        total = own_ref[:, at:at + WIDTH] + dot(arrived, r_ref[:, at:at + WIDTH])
-        total = total.astype(bf16)
-        for part in range(0, WIDTH, LANES):
-            field_ref[(at + part) // LANES] = total[:, part:part + LANES].reshape(groups, PAD, LANES)
-    mix(g2_ref[...], field_ref, mixed_ref)
+
+
+def second_kernel(own_ref, arrived_ref, r_ref, g2_ref, send_ref, where_ref, blocks_ref,
+                  packed_ref, turned_hbm, turned_ref, lines_ref, spread_ref, stiff_ref, sems):
+    near = begin(sems, (last_stored(blocks_ref, stiff_ref), stiff_ref))
+    lines_ref[...] = arrived_ref[...].astype(f32)
+    turned = jnp.concatenate([by_quarter(lines_ref, quarter).T.astype(bf16) for quarter in range(QUARTERS)], axis=1)
+    turned_ref[...] = turned
+    keeps = begin(sems.at[pl.ds(len(near), 1)], (turned_ref, turned_hbm))
+    stored, out_blocks = where_ref.shape
+    owned_blocks = own_ref.shape[0]
+    terms = stiff_ref.shape[0]
+    mixer = g2_ref[...]
+    picks = []
+    for row in range(owned_blocks, out_blocks):
+        columns = [where_ref[c, row] for c in range(stored)]
+        base = jnp.concatenate([own_ref[column] for column in columns], axis=1)
+        table = jnp.concatenate([r_ref[column] for column in columns], axis=1)
+        field = (base + dot(turned, table)).astype(bf16)
+        mixed = dot(mixer, field).astype(bf16)
+        picks.append(jnp.concatenate([mixed[term * PAD:(term + 1) * PAD, :] for term in range(terms)], axis=1))
+    width = send_ref.shape[1]
+    lines = lax.broadcasted_iota(i32, (packed_ref.shape[0], width), 0) * QUARTERS
+    place = jnp.concatenate([one_hot(send_ref[...] == lines + quarter) for quarter in range(QUARTERS)], axis=1)
     spread_ref[...] = jnp.zeros_like(spread_ref)
-    width = send_ref.shape[1]
-    send = send_ref[...]
-    lines = lax.broadcasted_iota(i32, (packed_ref.shape[0], width), 0) * QUARTERS
-    place = jnp.concatenate([one_hot(send == lines + quarter) for quarter in range(QUARTERS)], axis=1)
-    finish(small)
-    part = interface_part(PAD, where_ref, mixed_ref, stiff_ref)
+    finish(near)
+    depth = terms * stored * LANES
+    part = jnp.concatenate(
+        [dot(picked, stiff_ref[:, at * stored:(at + 1) * stored].reshape(depth, LANES)) for at, picked in enumerate(picks)],
+        axis=1,
+    ).astype(bf16)
     for quarter in range(QUARTERS):
         spread_ref[quarter * PAD:(quarter + 1) * PAD, quarter * width:(quarter + 1) * width] = part
     packed_ref[...] = dot_t(place, spread_ref[...]).astype(bf16)
-    for block in range(field_ref.shape[0]):
-        first_ref[:, block * LANES:(block + 1) * LANES] = field_ref[block, me, :first_ref.shape[0], :]
-
-
-def own_kernel(sizes, where_ref, mixed_ref, blocks_ref, own_ref, stiff_ref, sems):
-    copies = own_fetch(sizes, where_ref.shape[0], blocks_ref, stiff_ref, sems)
-    own_rows(PAD, sizes, where_ref, mixed_ref, stiff_ref, copies, own_ref)
-
-
-def last_kernel(own_ref, arrived_ref, recv_ref, out_ref, slots_ref, r_ref):
-    receive_table(recv_ref, r_ref)
-    arrived = arrived_ref[...].astype(f32)
-    lines = arrived.shape[0]
-    for quarter in range(QUARTERS):
-        turned = pltpu.roll(arrived, (QUARTERS - quarter) % QUARTERS * PAD, 1)
-        slots_ref[pl.ds(quarter, lines, stride=QUARTERS), :] = turned
-    by_slot = slots_ref[...].T[:PAD, :].astype(bf16)
-    for at in range(0, own_ref.shape[1], WIDTH):
-        total = own_ref[:, at:at + WIDTH] + dot(by_slot, r_ref[:, at:at + WIDTH])
-        out_ref[:, at:at + WIDTH] = total.astype(bf16)[:out_ref.shape[0], :]
-
-
-def uneven(rows):
-    last, rest = rows // 8, rows - rows // 8
-    third = -(-rest // 3)
-    return tuple(size for size in (third, third, rest - 2 * third, last) if size)
+    finish(keeps)
+
+
+def own_kernel(groups, steps, where_ref, recv_ref, g2_ref, turned_hbm, own_ref, blocks_ref,
+               first_ref, own2_ref, r_ref, turned_ref, field_ref, mixed_ref, stiff_ref, rows_ref, sems):
+    stored = where_ref.shape[0]
+    near = begin(sems, (turned_hbm, turned_ref))
+    copies = own_fetch(steps, stored, blocks_ref, stiff_ref, sems.at[pl.ds(len(near), steps)])
+    me = lax.axis_index("mode")
+    receive_table(recv_ref, r_ref, rows_ref)
+    owned_blocks, _, lanes = own_ref.shape
+    finish(near)
+    turned = turned_ref[...]
+    for block in range(0, owned_blocks, 2):
+        table = jnp.concatenate([r_ref[block], r_ref[block + 1]], axis=1)
+        base = jnp.concatenate([own_ref[block], own_ref[block + 1]], axis=1)
+        field = (base + dot(turned, table)).astype(bf16)
+        for part in range(2):
+            field_ref[block + part] = field[:, part * lanes:(part + 1) * lanes].reshape(groups, PAD, lanes)
+    mix(g2_ref[...], field_ref, mixed_ref)
+    for block in range(owned_blocks):
+        first_ref[:, block * lanes:(block + 1) * lanes] = field_ref[block, me, :first_ref.shape[0], :]
+    per = owned_blocks // steps
+    for step in range(steps):
+        copies[step].wait()
+        for row in range(step * per, (step + 1) * per):
+            own2_ref[:, row * lanes:(row + 1) * lanes] = block_row(
+                row, PAD, where_ref, mixed_ref, stiff_ref[:, row * stored:(row + 1) * stored]
+            )
+
+
+def last_kernel(own_ref, arrived_ref, r_ref, out_ref):
+    turned = arrived_ref[...].astype(f32).T.astype(bf16)
+    by_slot = jnp.concatenate([turned[quarter * PAD:(quarter + 1) * PAD, :] for quarter in range(QUARTERS)], axis=1)
+    for block in range(0, r_ref.shape[0], 2):
+        at = slice(block * LANES, (block + 2) * LANES)
+        table = jnp.concatenate([r_ref[block], r_ref[block + 1]], axis=1)
+        total = own_ref[:, at] + dot(by_slot, table)
+        out_ref[:, at] = total.astype(bf16)[:out_ref.shape[0], :]
 
 
 def local(groups, peers, modes_in, blocks, block_cols, send_slot, recv_row, mix_cols, mix_coef):
@@ -284,6 +305,9 @@
     block_flops = 2 * terms * stored * blk * blk
     wide, narrow = (owned_blocks, terms * rows, blk), (owned_blocks, terms * PAD, blk)
 
+    own_shape, table_shape = (owned_blocks, rows, blk), (owned_blocks, slots, blk)
+    turned_scratch = pltpu.VMEM((slots, LANES), f32)
+
     g, g2, place, send, recv, own_field, where, stiff = call(
         functools.partial(setup_kernel, groups),
         [Shape(mixer_shape, bf16), Shape((terms * PAD, rows), bf16), Shape((slots, interface), bf16), Shape(send.shape, i32),
@@ -291,39 +315,42 @@
         [mix_cols, mix_coef, send, recv, pin(modes_in), where, blocks], [HBM] * 7, [VMEM] * 8, flops=10**6,
         scratch=[*tables, dma((7,))],
     )
-    packed, field = call(
+    packed, field, g_kept = call(
         functools.partial(first_kernel, groups),
-        [Shape((slots, rows), bf16), Shape(field_shape, bf16)],
+        [Shape((slots, rows), bf16), pltpu.HBM(field_shape, bf16), pltpu.HBM(mixer_shape, bf16)],
         [own_field, others[1], others[2], others[3], g, place, where, stiff],
-        [VMEM] * 6 + [SMEM, VMEM], [VMEM] * 2, flops=block_flops * (out_blocks - owned_blocks) * rows,
+        [VMEM] * 6 + [SMEM, VMEM], [VMEM, HBM, HBM],
+        flops=block_flops * (out_blocks - owned_blocks) * rows, scratch=[field_scratch, dma((2,))],
     )
     arrived = lax.all_to_all(packed.reshape(peers, cap, rows), "space", split_axis=0, concat_axis=0, tiled=True)
-    sizes = uneven(owned_blocks)
-    own = call(
-        functools.partial(between_kernel, sizes), [Shape((rows, owned), f32)],
-        [field, g, where, blocks], [VMEM] * 2 + [SMEM, HBM], [VMEM], flops=block_flops * owned_blocks * rows,
-        scratch=[pltpu.VMEM(wide, bf16), own_scratch, dma((len(sizes),))],
-    )[0]
-    first_apply, mixed2, packed2 = call(
-        functools.partial(second_kernel, groups),
-        [Shape((modes_dev, owned), bf16), Shape(narrow, bf16), Shape((lines, QUARTERS * PAD), bf16)],
-        [own, arrived.reshape(slots, rows), g2, send, recv, where, blocks],
-        [VMEM] * 5 + [SMEM, HBM], [VMEM] * 3, flops=2 * slots * rows * owned,
-        scratch=[field_scratch, pltpu.VMEM((slots, owned), bf16), pltpu.VMEM((QUARTERS * PAD, QUARTERS * interface), bf16),
-                 pltpu.VMEM(if_blocks, bf16), dma((1,))],
+    steps = owned_blocks // 2
+    own, r = call(
+        functools.partial(between_kernel, steps), [Shape(own_shape, f32), Shape(table_shape, bf16)],
+        [pin(field), pin(g_kept), recv, where, blocks], [HBM, HBM, VMEM, SMEM, HBM], [VMEM] * 2,
+        flops=block_flops * owned_blocks * rows,
+        scratch=[field_scratch, pltpu.VMEM(mixer_shape, bf16), pltpu.VMEM(wide, bf16), own_scratch, turned_scratch,
+                 dma((2 + steps,))],
+    )
+    packed2, turned = call(
+        second_kernel, [Shape((lines, QUARTERS * PAD), bf16), pltpu.HBM((rows, slots), bf16)],
+        [own, arrived.reshape(slots, rows), r, g2, send, where, blocks], [VMEM] * 5 + [SMEM, HBM], [VMEM, HBM],
+        flops=2 * slots * rows * owned,
+        scratch=[pltpu.VMEM((rows, slots), bf16), turned_scratch, pltpu.VMEM((QUARTERS * PAD, QUARTERS * interface), bf16), pltpu.VMEM(if_blocks, bf16), dma((2,))],
     )
     arrived2 = lax.all_to_all(
         packed2.reshape(peers, cap // QUARTERS, QUARTERS * PAD), "space", split_axis=0, concat_axis=0, tiled=True
     )
-    own2 = call(
-        functools.partial(own_kernel, sizes), [Shape((PAD, owned), f32)],
-        [where, mixed2, blocks], [SMEM, VMEM, HBM], [VMEM], flops=block_flops * owned_blocks * PAD,
-        scratch=[own_scratch, dma((len(sizes),))],
-    )[0]
+    first_apply, own2, r2 = call(
+        functools.partial(own_kernel, groups, steps),
+        [Shape((modes_dev, owned), bf16), Shape((PAD, owned), f32), Shape(table_shape, bf16)],
+        [where, recv, g2, pin(turned), own, blocks], [SMEM, VMEM, VMEM, HBM, VMEM, HBM], [VMEM] * 3,
+        flops=block_flops * owned_blocks * PAD,
+        scratch=[pltpu.VMEM((rows, slots), bf16), field_scratch, pltpu.VMEM(narrow, bf16), own_scratch, turned_scratch,
+                 dma((1 + steps,))],
+    )
     second_apply = call(
         last_kernel, [Shape((modes_dev, owned), bf16)],
-        [own2, arrived2.reshape(lines, QUARTERS * PAD), recv], [VMEM] * 3, [VMEM], flops=2 * slots * PAD * owned,
-        scratch=[pltpu.VMEM((slots, QUARTERS * PAD), f32), pltpu.VMEM((slots, owned), bf16)],
+        [own2, arrived2.reshape(lines, QUARTERS * PAD), r2], [VMEM] * 3, [VMEM], flops=2 * slots * PAD * owned,
     )[0]
     return (first_apply, second_apply)
 

time: 59.9 us -> 59.5 us (level)
  transfers between devices with their start and end apart: 5 -> 5, of which waited for: 3 -> 3; matrix products, arithmetic and copies ran while one was open for 0% -> 0% of each run, Pallas kernels for 22% -> 23%
where the time goes in v7:
time: 59.5 us; the launch traced here: 59.2 us
  starting transfers between devices  24.6 us (41%)
  Pallas kernels  20.6 us (35%)
  waiting for transfers between devices  13.3 us (22%)
  between operations  0.7 us (1%)
    pallas_call x6, Pallas kernels, call(): pl.pallas_call(kernel, out_shape=outs, in_specs=in_specs, out_specs=out_s...  20.6 us
    all_to_all x1, starting transfers between devices, local(): lax.all_to_all(packed.reshape(peers, cap, rows), 'space', split_axis=0, c...  12.8 us
    all_to_all x1, starting transfers between devices, local(): lax.all_to_all(packed2.reshape(peers, cap // QUARTERS, QUARTERS * PAD), '...  6.54 us
    ppermute x3, waiting for transfers between devices, local(): lax.ppermute(modes_in, 'mode', [((to + s) % groups, to) for to in range(g...  5.64 us
    ppermute x3, starting transfers between devices, local(): lax.ppermute(modes_in, 'mode', [((to + s) % groups, to) for to in range(g...  5.29 us
    all_to_all x1, waiting for transfers between devices, local(): lax.all_to_all(packed2.reshape(peers, cap // QUARTERS, QUARTERS * PAD), '...  3.88 us
    all_to_all x1, waiting for transfers between devices, local(): lax.all_to_all(packed.reshape(peers, cap, rows), 'space', split_axis=0, c...  3.82 us
  transfers between devices with their start and end apart: 5, of which 3 were waited for; matrix products, arithmetic and copies ran while one was open for 0% of the time, Pallas kernels for 23%

profile of v7, /device:TPU:1, one launch (start us, length us, event | category | flops | bytes accessed | tf_op | source)
XLA Modules:
  0.0 59.2 jit_solution(1608652062113318210)
XLA Ops:
  0.6 3.6 %collective-permute-start = (bf16[30,2048]{1,0:T(8,128)(2,1)}, bf16[30,2048]{1,0:T(8,128)(2,1)S(1)}, u32[]{:S(2)}, u32[]{:S(2)}) collective-permute-start(bf16[30,2048]{1,0:T(8,128)(2,1)} %own_hbm.1), channel_id=1, source_target_pairs={{1,0},{2,1},{3,2},{0,3},{5,4},{6,5},{7,6},{4,7},{9,8},{10,9},{11,1... | collective-permute-start | bytes 368648 | tf_op jit(solution)/shard_map/ppermute | solution.py:293
  4.3 0.0 collective-permute-start.2
  4.3 1.6 %collective-permute-start.1 = (bf16[30,2048]{1,0:T(8,128)(2,1)}, bf16[30,2048]{1,0:T(8,128)(2,1)S(1)}, u32[]{:S(2)}, u32[]{:S(2)}) collective-permute-start(bf16[30,2048]{1,0:T(8,128)(2,1)} %own_hbm.1), channel_id=1, source_target_pairs={{2,0},{3,1},{0,2},{1,3},{6,4},{7,5},{4,6},{5,7},{10,8},{11,9},{8,1... | collective-permute-start | bytes 368648 | tf_op jit(solution)/shard_map/ppermute | solution.py:293
  5.9 1.5 %shard_map.86 = (bf16[128,640]{1,0:T(8,128)(2,1)S(1)}, bf16[160,128]{1,0:T(8,128)(2,1)S(1)}, bf16[512,256]{1,0:T(8,128)(2,1)S(1)}, s32[1,256]{1,0:T(1,128)S(1)},...) custom-call(s32[5,8,120]{2,1,0:T(8,128)} %bitcast.11, ...), custom_call_target="tpu_custom_call" | custom-call | flops 1000000 | bytes 13865024 | tf_op jit(solution)/shard_map/pallas_call | solution.py:25
  7.5 0.0 collective-permute-done.v1
  7.5 5.6 %collective-permute-done.2.v3 = bf16[30,2048]{1,0:T(8,128)(2,1)S(1)} collective-permute-done((bf16[30,2048]{1,0:T(8,128)(2,1)}, bf16[30,2048]{1,0:T(8,128)(2,1)S(1)}, u32[]{:S(2)}, u32[]{:S(2)}) %collective-permute-start.2) | collective-permute-done | bytes 122912 | tf_op jit(solution)/shard_map/ppermute | solution.py:293
  13.1 0.0 collective-permute-done.1.v2
  13.1 2.2 %shard_map.87 = (bf16[512,128]{1,0:T(8,128)(2,1)}, bf16[16,4,32,128]{3,2,1,0:T(8,128)(2,1)}, bf16[128,640]{1,0:T(8,128)(2,1)}) custom-call(bf16[30,2048]{1,0:T(8,128)(2,1)S(1)} %get-tuple-element.23.v0, bf16[30,2048]{1,0:T(8,128)(2,1)S(1)} %collective-permute-done.v1, bf16[30,2048]{1,0:T(8,128)(2,1)S(1)} %collective-permute-done.1.v2, ...), custom_call_target="tpu_custom_call" | custom-call | flops 167772160 | bytes 3047712 | tf_op jit(solution)/shard_map/pallas_call | solution.py:25
  15.3 12.8 %all-to-all-start = ((bf16[64,8,128]{2,1,0:T(8,128)(2,1)}), bf16[64,8,128]{2,1,0:T(8,128)(2,1)S(1)}, u32[]{:S(2)}, u32[]{:S(2)}) async-start(bf16[64,8,128]{2,1,0:T(8,128)(2,1)} %bitcast.5), calls=%async_computation | async-start | bytes 262144 | tf_op jit(solution)/shard_map/all_to_all | solution.py:325
  28.2 6.5 %shard_map.88 = (f32[16,128,128]{2,1,0:T(8,128)S(1)}, bf16[16,512,128]{2,1,0:T(8,128)(2,1)S(1)}) custom-call(bf16[16,4,32,128]{3,2,1,0:T(8,128)(2,1)} %get-tuple-element.27.field_hbm, bf16[128,640]{1,0:T(8,128)(2,1)} %get-tuple-element.28.g_hbm, s32[1,512]{1,0:T(1,128)S(1)} %get-tuple-element.21.recv_ref, s32[4,18]{1,0:T(4,128)S(1)} %get-tuple-element.20.where_ref, ...), custom_call_target="tpu_custom_call" | custom-call | flops 1342177280 | bytes 15632672 | tf_op jit(solution)/shard_map/pallas_call | solution.py:25
  34.7 3.8 %all-to-all-done = bf16[64,8,128]{2,1,0:T(8,128)(2,1)S(1)} async-done(((bf16[64,8,128]{2,1,0:T(8,128)(2,1)}), bf16[64,8,128]{2,1,0:T(8,128)(2,1)S(1)}, u32[]{:S(2)}, u32[]{:S(2)}) %all-to-all-start) | async-done | bytes 131104 | tf_op jit(solution)/shard_map/all_to_all | solution.py:325
  38.5 3.7 %shard_map.89 = (bf16[128,128]{1,0:T(8,128)(2,1)}, bf16[128,512]{1,0:T(8,128)(2,1)}) custom-call(f32[16,128,128]{2,1,0:T(8,128)S(1)} %get-tuple-element.29.own_ref, bf16[512,128]{1,0:T(8,128)(2,1)S(1)} %bitcast.9, bf16[16,512,128]{2,1,0:T(8,128)(2,1)S(1)} %get-tuple-element.31.r_ref, bf16[160,128]{1,0:T(8,128)(2,1)S(1)} %get-tuple-element.22.g2_ref, ...), custom_call_target="tpu_custom_call" | custom-call | flops 268435456 | bytes 15279392 | tf_op jit(solution)/shard_map/pallas_call | solution.py:25
  42.2 6.5 %all-to-all-start.1 = ((bf16[64,2,128]{2,1,0:T(2,128)(2,1)}), bf16[64,2,128]{2,1,0:T(2,128)(2,1)S(1)}, u32[]{:S(2)}, u32[]{:S(2)}) async-start(bf16[64,2,128]{2,1,0:T(2,128)(2,1)} %bitcast.7), calls=%async_computation.1 | async-start | bytes 65536 | tf_op jit(solution)/shard_map/all_to_all | solution.py:340
  48.8 5.4 %shard_map.90 = (bf16[30,2048]{1,0:T(8,128)(2,1)}, f32[32,2048]{1,0:T(8,128)S(1)}, bf16[16,512,128]{2,1,0:T(8,128)(2,1)S(1)}) custom-call(s32[4,18]{1,0:T(4,128)S(1)} %get-tuple-element.20.where_ref, s32[1,512]{1,0:T(1,128)S(1)} %get-tuple-element.21.recv_ref, bf16[160,128]{1,0:T(8,128)(2,1)S(1)} %get-tuple-element.22.g2_ref, ...), custom_call_target="tpu_custom_call" | custom-call | flops 335544320 | bytes 15501600 | tf_op jit(solution)/shard_map/pallas_call | solution.py:25
  54.2 3.9 %all-to-all-done.1 = bf16[64,2,128]{2,1,0:T(2,128)(2,1)S(1)} async-done(((bf16[64,2,128]{2,1,0:T(2,128)(2,1)}), bf16[64,2,128]{2,1,0:T(2,128)(2,1)S(1)}, u32[]{:S(2)}, u32[]{:S(2)}) %all-to-all-start.1) | async-done | bytes 32800 | tf_op jit(solution)/shard_map/all_to_all | solution.py:340
  58.1 1.2 %shard_map.91 = bf16[30,2048]{1,0:T(8,128)(2,1)} custom-call(f32[32,2048]{1,0:T(8,128)S(1)} %get-tuple-element.35.own_ref, bf16[128,128]{1,0:T(8,128)(2,1)S(1)} %bitcast.10, bf16[16,512,128]{2,1,0:T(8,128)(2,1)S(1)} %get-tuple-element.37.r_ref), custom_call_target="tpu_custom_call" | custom-call | flops 67108864 | bytes 2514944 | tf_op jit(solution)/shard_map/pallas_call | solution.py:25
Async XLA Ops:
  0.6 6.8 %collective-permute-start = (bf16[30,2048]{1,0:T(8,128)(2,1)}, bf16[30,2048]{1,0:T(8,128)(2,1)S(1)}, u32[]{:S(2)}, u32[]{:S(2)}) collective-permute-start(bf16[30,2048]{1,0:T(8,128)(2,1)} %own_hbm.1), channel_id=1, source_target_pairs={{1,0},{2,1},{3,2},{0,3},{5,4},{6,5},{7,6},{4,7},{9,8},{10,9},{11,1... | collective-permute-start | bytes 368648 | tf_op jit(solution)/shard_map/ppermute | solution.py:293
  4.3 8.8 %collective-permute-start.2 = (bf16[30,2048]{1,0:T(8,128)(2,1)}, bf16[30,2048]{1,0:T(8,128)(2,1)S(1)}, u32[]{:S(2)}, u32[]{:S(2)}) collective-permute-start(bf16[30,2048]{1,0:T(8,128)(2,1)} %own_hbm.1), channel_id=1, source_target_pairs={{3,0},{0,1},{1,2},{2,3},{7,4},{4,5},{5,6},{6,7},{11,8},{8,9},{9,10... | collective-permute-start | bytes 368648 | tf_op jit(solution)/shard_map/ppermute | solution.py:293
  4.3 8.8 %collective-permute-start.1 = (bf16[30,2048]{1,0:T(8,128)(2,1)}, bf16[30,2048]{1,0:T(8,128)(2,1)S(1)}, u32[]{:S(2)}, u32[]{:S(2)}) collective-permute-start(bf16[30,2048]{1,0:T(8,128)(2,1)} %own_hbm.1), channel_id=1, source_target_pairs={{2,0},{3,1},{0,2},{1,3},{6,4},{7,5},{4,6},{5,7},{10,8},{11,9},{8,1... | collective-permute-start | bytes 368648 | tf_op jit(solution)/shard_map/ppermute | solution.py:293
  15.3 23.2 %all-to-all-start = ((bf16[64,8,128]{2,1,0:T(8,128)(2,1)}), bf16[64,8,128]{2,1,0:T(8,128)(2,1)S(1)}, u32[]{:S(2)}, u32[]{:S(2)}) async-start(bf16[64,8,128]{2,1,0:T(8,128)(2,1)} %bitcast.5), calls=%async_computation | async-start | bytes 262144 | tf_op jit(solution)/shard_map/all_to_all | solution.py:325
  42.2 15.8 %all-to-all-start.1 = ((bf16[64,2,128]{2,1,0:T(2,128)(2,1)}), bf16[64,2,128]{2,1,0:T(2,128)(2,1)S(1)}, u32[]{:S(2)}, u32[]{:S(2)}) async-start(bf16[64,2,128]{2,1,0:T(2,128)(2,1)} %bitcast.7), calls=%async_computation.1 | async-start | bytes 65536 | tf_op jit(solution)/shard_map/all_to_all | solution.py:340

commit v8 on v7

--- a/solution.py
+++ b/solution.py
@@ -76,17 +76,12 @@
     return total.astype(bf16)
 
 
-def by_quarter(rows_ref, quarter):
-    return rows_ref[pl.ds(quarter, rows_ref.shape[0] // QUARTERS, stride=QUARTERS), :]
-
-
-def receive_table(recv_ref, r_ref, turned_ref):
+def receive_table(recv_ref, r_ref):
     slots = recv_ref.shape[1]
-    turned_ref[...] = jnp.broadcast_to(recv_ref[...].astype(f32), (LANES, slots)).T
-    lanes = lax.broadcasted_iota(i32, (slots // QUARTERS, LANES), 1)
-    for quarter in range(QUARTERS):
-        offset = by_quarter(turned_ref, quarter).astype(i32) - lanes
-        at = slice(quarter * slots // QUARTERS, (quarter + 1) * slots // QUARTERS)
+    lanes = lax.broadcasted_iota(i32, (LANES, LANES), 1)
+    for start in range(0, slots, LANES):
+        at = slice(start, start + LANES)
+        offset = jnp.broadcast_to(recv_ref[:, at].astype(f32), (LANES, LANES)).T.astype(i32) - lanes
         for block in range(r_ref.shape[0]):
             r_ref[block, at, :] = one_hot(offset == block * LANES)
 
@@ -185,11 +180,11 @@
 
 
 def between_kernel(steps, field_hbm, g_hbm, recv_ref, where_ref, blocks_ref,
-                   own_ref, r_ref, field_ref, g_ref, mixed_ref, stiff_ref, turned_ref, sems):
+                   own_ref, r_ref, field_ref, g_ref, mixed_ref, stiff_ref, sems):
     near = begin(sems, (field_hbm, field_ref), (g_hbm, g_ref))
     stored = where_ref.shape[0]
     copies = own_fetch(steps, stored, blocks_ref, stiff_ref, sems.at[pl.ds(len(near), steps)])
-    receive_table(recv_ref, r_ref, turned_ref)
+    receive_table(recv_ref, r_ref)
     finish(near)
     mix(stacked(g_ref[...]), field_ref, mixed_ref)
     per = own_ref.shape[0] // steps
@@ -202,33 +197,28 @@
 
 
 def second_kernel(own_ref, arrived_ref, r_ref, g2_ref, send_ref, where_ref, blocks_ref,
-                  packed_ref, turned_hbm, turned_ref, lines_ref, spread_ref, stiff_ref, sems):
+                  packed_ref, turned_hbm, turned_ref, spread_ref, stiff_ref, sems):
     near = begin(sems, (last_stored(blocks_ref, stiff_ref), stiff_ref))
-    lines_ref[...] = arrived_ref[...].astype(f32)
-    turned = jnp.concatenate([by_quarter(lines_ref, quarter).T.astype(bf16) for quarter in range(QUARTERS)], axis=1)
+    turned = arrived_ref[...].astype(f32).T.astype(bf16)
     turned_ref[...] = turned
     keeps = begin(sems.at[pl.ds(len(near), 1)], (turned_ref, turned_hbm))
     stored, out_blocks = where_ref.shape
     owned_blocks = own_ref.shape[0]
     terms = stiff_ref.shape[0]
-    mixer = g2_ref[...]
+    mixer = jnp.concatenate([g2_ref[term * PAD:(term + 1) * PAD, :] for term in range(terms)], axis=1)
     picks = []
     for row in range(owned_blocks, out_blocks):
         columns = [where_ref[c, row] for c in range(stored)]
         base = jnp.concatenate([own_ref[column] for column in columns], axis=1)
         table = jnp.concatenate([r_ref[column] for column in columns], axis=1)
-        field = (base + dot(turned, table)).astype(bf16)
-        mixed = dot(mixer, field).astype(bf16)
-        picks.append(jnp.concatenate([mixed[term * PAD:(term + 1) * PAD, :] for term in range(terms)], axis=1))
+        picks.append((base + dot(turned, table)).astype(bf16))
     width = send_ref.shape[1]
     lines = lax.broadcasted_iota(i32, (packed_ref.shape[0], width), 0) * QUARTERS
     place = jnp.concatenate([one_hot(send_ref[...] == lines + quarter) for quarter in range(QUARTERS)], axis=1)
     spread_ref[...] = jnp.zeros_like(spread_ref)
     finish(near)
-    depth = terms * stored * LANES
     part = jnp.concatenate(
-        [dot(picked, stiff_ref[:, at * stored:(at + 1) * stored].reshape(depth, LANES)) for at, picked in enumerate(picks)],
-        axis=1,
+        [mixed_row(picked, stiff_ref[:, at * stored:(at + 1) * stored], mixer) for at, picked in enumerate(picks)], axis=1
     ).astype(bf16)
     for quarter in range(QUARTERS):
         spread_ref[quarter * PAD:(quarter + 1) * PAD, quarter * width:(quarter + 1) * width] = part
@@ -237,12 +227,12 @@
 
 
 def own_kernel(groups, steps, where_ref, recv_ref, g2_ref, turned_hbm, own_ref, blocks_ref,
-               first_ref, own2_ref, r_ref, turned_ref, field_ref, mixed_ref, stiff_ref, rows_ref, sems):
+               first_hbm, own2_ref, r_ref, turned_ref, first_ref, field_ref, mixed_ref, stiff_ref, sems):
     stored = where_ref.shape[0]
     near = begin(sems, (turned_hbm, turned_ref))
     copies = own_fetch(steps, stored, blocks_ref, stiff_ref, sems.at[pl.ds(len(near), steps)])
     me = lax.axis_index("mode")
-    receive_table(recv_ref, r_ref, rows_ref)
+    receive_table(recv_ref, r_ref)
     owned_blocks, _, lanes = own_ref.shape
     finish(near)
     turned = turned_ref[...]
@@ -255,6 +245,7 @@
     mix(g2_ref[...], field_ref, mixed_ref)
     for block in range(owned_blocks):
         first_ref[:, block * lanes:(block + 1) * lanes] = field_ref[block, me, :first_ref.shape[0], :]
+    keeps = begin(sems.at[pl.ds(len(near) + steps, 1)], (first_ref, first_hbm))
     per = owned_blocks // steps
     for step in range(steps):
         copies[step].wait()
@@ -262,11 +253,16 @@
             own2_ref[:, row * lanes:(row + 1) * lanes] = block_row(
                 row, PAD, where_ref, mixed_ref, stiff_ref[:, row * stored:(row + 1) * stored]
             )
-
-
-def last_kernel(own_ref, arrived_ref, r_ref, out_ref):
-    turned = arrived_ref[...].astype(f32).T.astype(bf16)
-    by_slot = jnp.concatenate([turned[quarter * PAD:(quarter + 1) * PAD, :] for quarter in range(QUARTERS)], axis=1)
+    finish(keeps)
+
+
+def last_kernel(own_ref, arrived_ref, r_ref, out_ref, slots_ref):
+    arrived = arrived_ref[...].astype(f32)
+    lines = arrived.shape[0]
+    for quarter in range(QUARTERS):
+        turned = pltpu.roll(arrived, (QUARTERS - quarter) % QUARTERS * PAD, 1)
+        slots_ref[pl.ds(quarter, lines, stride=QUARTERS), :] = turned
+    by_slot = slots_ref[...].T[:PAD, :].astype(bf16)
     for block in range(0, r_ref.shape[0], 2):
         at = slice(block * LANES, (block + 2) * LANES)
         table = jnp.concatenate([r_ref[block], r_ref[block + 1]], axis=1)
@@ -306,7 +302,6 @@
     wide, narrow = (owned_blocks, terms * rows, blk), (owned_blocks, terms * PAD, blk)
 
     own_shape, table_shape = (owned_blocks, rows, blk), (owned_blocks, slots, blk)
-    turned_scratch = pltpu.VMEM((slots, LANES), f32)
 
     g, g2, place, send, recv, own_field, where, stiff = call(
         functools.partial(setup_kernel, groups),
@@ -328,29 +323,29 @@
         functools.partial(between_kernel, steps), [Shape(own_shape, f32), Shape(table_shape, bf16)],
         [pin(field), pin(g_kept), recv, where, blocks], [HBM, HBM, VMEM, SMEM, HBM], [VMEM] * 2,
         flops=block_flops * owned_blocks * rows,
-        scratch=[field_scratch, pltpu.VMEM(mixer_shape, bf16), pltpu.VMEM(wide, bf16), own_scratch, turned_scratch,
-                 dma((2 + steps,))],
+        scratch=[field_scratch, pltpu.VMEM(mixer_shape, bf16), pltpu.VMEM(wide, bf16), own_scratch, dma((2 + steps,))],
     )
     packed2, turned = call(
         second_kernel, [Shape((lines, QUARTERS * PAD), bf16), pltpu.HBM((rows, slots), bf16)],
         [own, arrived.reshape(slots, rows), r, g2, send, where, blocks], [VMEM] * 5 + [SMEM, HBM], [VMEM, HBM],
         flops=2 * slots * rows * owned,
-        scratch=[pltpu.VMEM((rows, slots), bf16), turned_scratch, pltpu.VMEM((QUARTERS * PAD, QUARTERS * interface), bf16), pltpu.VMEM(if_blocks, bf16), dma((2,))],
+        scratch=[pltpu.VMEM((rows, slots), bf16), pltpu.VMEM((QUARTERS * PAD, QUARTERS * interface), bf16), pltpu.VMEM(if_blocks, bf16), dma((2,))],
     )
     arrived2 = lax.all_to_all(
         packed2.reshape(peers, cap // QUARTERS, QUARTERS * PAD), "space", split_axis=0, concat_axis=0, tiled=True
     )
     first_apply, own2, r2 = call(
         functools.partial(own_kernel, groups, steps),
-        [Shape((modes_dev, owned), bf16), Shape((PAD, owned), f32), Shape(table_shape, bf16)],
-        [where, recv, g2, pin(turned), own, blocks], [SMEM, VMEM, VMEM, HBM, VMEM, HBM], [VMEM] * 3,
+        [pltpu.HBM((modes_dev, owned), bf16), Shape((PAD, owned), f32), Shape(table_shape, bf16)],
+        [where, recv, g2, pin(turned), own, blocks], [SMEM, VMEM, VMEM, HBM, VMEM, HBM], [HBM, VMEM, VMEM],
         flops=block_flops * owned_blocks * PAD,
-        scratch=[pltpu.VMEM((rows, slots), bf16), field_scratch, pltpu.VMEM(narrow, bf16), own_scratch, turned_scratch,
-                 dma((1 + steps,))],
+        scratch=[pltpu.VMEM((rows, slots), bf16), pltpu.VMEM((modes_dev, owned), bf16), field_scratch, pltpu.VMEM(narrow, bf16),
+                 own_scratch, dma((2 + steps,))],
     )
     second_apply = call(
         last_kernel, [Shape((modes_dev, owned), bf16)],
         [own2, arrived2.reshape(lines, QUARTERS * PAD), r2], [VMEM] * 3, [VMEM], flops=2 * slots * PAD * owned,
+        scratch=[pltpu.VMEM((slots, QUARTERS * PAD), f32)],
     )[0]
     return (first_apply, second_apply)
 

time: 59.5 us -> 59.7 us (level)
  transfers between devices with their start and end apart: 5 -> 5, of which waited for: 3 -> 3; matrix products, arithmetic and copies ran while one was open for 0% -> 0% of each run, Pallas kernels for 23% -> 22%
where the time goes in v8:
time: 59.7 us; the launch traced here: 59.4 us
  starting transfers between devices  24.6 us (41%)
  Pallas kernels  20.5 us (34%)
  waiting for transfers between devices  13.6 us (23%)
  between operations  0.7 us (1%)
    pallas_call x6, Pallas kernels, call(): pl.pallas_call(kernel, out_shape=outs, in_specs=in_specs, out_specs=out_s...  20.5 us
    all_to_all x1, starting transfers between devices, local(): lax.all_to_all(packed.reshape(peers, cap, rows), 'space', split_axis=0, c...  12.8 us
    all_to_all x1, starting transfers between devices, local(): lax.all_to_all(packed2.reshape(peers, cap // QUARTERS, QUARTERS * PAD), '...  6.54 us
    ppermute x3, waiting for transfers between devices, local(): lax.ppermute(modes_in, 'mode', [((to + s) % groups, to) for to in range(g...  5.64 us
    ppermute x3, starting transfers between devices, local(): lax.ppermute(modes_in, 'mode', [((to + s) % groups, to) for to in range(g...  5.29 us
    all_to_all x1, waiting for transfers between devices, local(): lax.all_to_all(packed2.reshape(peers, cap // QUARTERS, QUARTERS * PAD), '...  4.14 us
    all_to_all x1, waiting for transfers between devices, local(): lax.all_to_all(packed.reshape(peers, cap, rows), 'space', split_axis=0, c...  3.82 us
  transfers between devices with their start and end apart: 5, of which 3 were waited for; matrix products, arithmetic and copies ran while one was open for 0% of the time, Pallas kernels for 22%

profile of v8, /device:TPU:1, one launch (start us, length us, event | category | flops | bytes accessed | tf_op | source)
XLA Modules:
  0.0 59.4 jit_solution(11818856855766298790)
XLA Ops:
  0.6 3.6 %collective-permute-start = (bf16[30,2048]{1,0:T(8,128)(2,1)}, bf16[30,2048]{1,0:T(8,128)(2,1)S(1)}, u32[]{:S(2)}, u32[]{:S(2)}) collective-permute-start(bf16[30,2048]{1,0:T(8,128)(2,1)} %own_hbm.1), channel_id=1, source_target_pairs={{1,0},{2,1},{3,2},{0,3},{5,4},{6,5},{7,6},{4,7},{9,8},{10,9},{11,1... | collective-permute-start | bytes 368648 | tf_op jit(solution)/shard_map/ppermute | solution.py:289
  4.3 0.0 collective-permute-start.2
  4.3 1.6 %collective-permute-start.1 = (bf16[30,2048]{1,0:T(8,128)(2,1)}, bf16[30,2048]{1,0:T(8,128)(2,1)S(1)}, u32[]{:S(2)}, u32[]{:S(2)}) collective-permute-start(bf16[30,2048]{1,0:T(8,128)(2,1)} %own_hbm.1), channel_id=1, source_target_pairs={{2,0},{3,1},{0,2},{1,3},{6,4},{7,5},{4,6},{5,7},{10,8},{11,9},{8,1... | collective-permute-start | bytes 368648 | tf_op jit(solution)/shard_map/ppermute | solution.py:289
  5.9 1.5 %shard_map.86 = (bf16[128,640]{1,0:T(8,128)(2,1)S(1)}, bf16[160,128]{1,0:T(8,128)(2,1)S(1)}, bf16[512,256]{1,0:T(8,128)(2,1)S(1)}, s32[1,256]{1,0:T(1,128)S(1)},...) custom-call(s32[5,8,120]{2,1,0:T(8,128)} %bitcast.11, ...), custom_call_target="tpu_custom_call" | custom-call | flops 1000000 | bytes 13865024 | tf_op jit(solution)/shard_map/pallas_call | solution.py:25
  7.5 0.0 collective-permute-done.v1
  7.5 5.6 %collective-permute-done.2.v3 = bf16[30,2048]{1,0:T(8,128)(2,1)S(1)} collective-permute-done((bf16[30,2048]{1,0:T(8,128)(2,1)}, bf16[30,2048]{1,0:T(8,128)(2,1)S(1)}, u32[]{:S(2)}, u32[]{:S(2)}) %collective-permute-start.2) | collective-permute-done | bytes 122912 | tf_op jit(solution)/shard_map/ppermute | solution.py:289
  13.1 0.0 collective-permute-done.1.v2
  13.1 2.2 %shard_map.87 = (bf16[512,128]{1,0:T(8,128)(2,1)}, bf16[16,4,32,128]{3,2,1,0:T(8,128)(2,1)}, bf16[128,640]{1,0:T(8,128)(2,1)}) custom-call(bf16[30,2048]{1,0:T(8,128)(2,1)S(1)} %get-tuple-element.23.v0, bf16[30,2048]{1,0:T(8,128)(2,1)S(1)} %collective-permute-done.v1, bf16[30,2048]{1,0:T(8,128)(2,1)S(1)} %collective-permute-done.1.v2, ...), custom_call_target="tpu_custom_call" | custom-call | flops 167772160 | bytes 3047712 | tf_op jit(solution)/shard_map/pallas_call | solution.py:25
  15.3 12.8 %all-to-all-start = ((bf16[64,8,128]{2,1,0:T(8,128)(2,1)}), bf16[64,8,128]{2,1,0:T(8,128)(2,1)S(1)}, u32[]{:S(2)}, u32[]{:S(2)}) async-start(bf16[64,8,128]{2,1,0:T(8,128)(2,1)} %bitcast.5), calls=%async_computation | async-start | bytes 262144 | tf_op jit(solution)/shard_map/all_to_all | solution.py:320
  28.2 6.5 %shard_map.88 = (f32[16,128,128]{2,1,0:T(8,128)S(1)}, bf16[16,512,128]{2,1,0:T(8,128)(2,1)S(1)}) custom-call(bf16[16,4,32,128]{3,2,1,0:T(8,128)(2,1)} %get-tuple-element.27.field_hbm, bf16[128,640]{1,0:T(8,128)(2,1)} %get-tuple-element.28.g_hbm, s32[1,512]{1,0:T(1,128)S(1)} %get-tuple-element.21.recv_ref, s32[4,18]{1,0:T(4,128)S(1)} %get-tuple-element.20.where_ref, ...), custom_call_target="tpu_custom_call" | custom-call | flops 1342177280 | bytes 15632672 | tf_op jit(solution)/shard_map/pallas_call | solution.py:25
  34.7 3.8 %all-to-all-done = bf16[64,8,128]{2,1,0:T(8,128)(2,1)S(1)} async-done(((bf16[64,8,128]{2,1,0:T(8,128)(2,1)}), bf16[64,8,128]{2,1,0:T(8,128)(2,1)S(1)}, u32[]{:S(2)}, u32[]{:S(2)}) %all-to-all-start) | async-done | bytes 131104 | tf_op jit(solution)/shard_map/all_to_all | solution.py:320
  38.5 3.8 %shard_map.89 = (bf16[128,128]{1,0:T(8,128)(2,1)}, bf16[128,512]{1,0:T(8,128)(2,1)}) custom-call(f32[16,128,128]{2,1,0:T(8,128)S(1)} %get-tuple-element.29.own_ref, bf16[512,128]{1,0:T(8,128)(2,1)S(1)} %bitcast.9, bf16[16,512,128]{2,1,0:T(8,128)(2,1)S(1)} %get-tuple-element.31.r_ref, bf16[160,128]{1,0:T(8,128)(2,1)S(1)} %get-tuple-element.22.g2_ref, ...), custom_call_target="tpu_custom_call" | custom-call | flops 268435456 | bytes 15279392 | tf_op jit(solution)/shard_map/pallas_call | solution.py:25
  42.3 6.5 %all-to-all-start.1 = ((bf16[64,2,128]{2,1,0:T(2,128)(2,1)}), bf16[64,2,128]{2,1,0:T(2,128)(2,1)S(1)}, u32[]{:S(2)}, u32[]{:S(2)}) async-start(bf16[64,2,128]{2,1,0:T(2,128)(2,1)} %bitcast.7), calls=%async_computation.1 | async-start | bytes 65536 | tf_op jit(solution)/shard_map/all_to_all | solution.py:334
  48.9 5.1 %shard_map.90 = (bf16[30,2048]{1,0:T(8,128)(2,1)}, f32[32,2048]{1,0:T(8,128)S(1)}, bf16[16,512,128]{2,1,0:T(8,128)(2,1)S(1)}) custom-call(s32[4,18]{1,0:T(4,128)S(1)} %get-tuple-element.20.where_ref, s32[1,512]{1,0:T(1,128)S(1)} %get-tuple-element.21.recv_ref, bf16[160,128]{1,0:T(8,128)(2,1)S(1)} %get-tuple-element.22.g2_ref, ...), custom_call_target="tpu_custom_call" | custom-call | flops 335544320 | bytes 15501600 | tf_op jit(solution)/shard_map/pallas_call | solution.py:25
  54.0 4.1 %all-to-all-done.1 = bf16[64,2,128]{2,1,0:T(2,128)(2,1)S(1)} async-done(((bf16[64,2,128]{2,1,0:T(2,128)(2,1)}), bf16[64,2,128]{2,1,0:T(2,128)(2,1)S(1)}, u32[]{:S(2)}, u32[]{:S(2)}) %all-to-all-start.1) | async-done | bytes 32800 | tf_op jit(solution)/shard_map/all_to_all | solution.py:334
  58.1 1.3 %shard_map.91 = bf16[30,2048]{1,0:T(8,128)(2,1)} custom-call(f32[32,2048]{1,0:T(8,128)S(1)} %get-tuple-element.35.own_ref, bf16[128,128]{1,0:T(8,128)(2,1)S(1)} %bitcast.10, bf16[16,512,128]{2,1,0:T(8,128)(2,1)S(1)} %get-tuple-element.37.r_ref), custom_call_target="tpu_custom_call" | custom-call | flops 67108864 | bytes 2514944 | tf_op jit(solution)/shard_map/pallas_call | solution.py:25
Async XLA Ops:
  0.6 6.8 %collective-permute-start = (bf16[30,2048]{1,0:T(8,128)(2,1)}, bf16[30,2048]{1,0:T(8,128)(2,1)S(1)}, u32[]{:S(2)}, u32[]{:S(2)}) collective-permute-start(bf16[30,2048]{1,0:T(8,128)(2,1)} %own_hbm.1), channel_id=1, source_target_pairs={{1,0},{2,1},{3,2},{0,3},{5,4},{6,5},{7,6},{4,7},{9,8},{10,9},{11,1... | collective-permute-start | bytes 368648 | tf_op jit(solution)/shard_map/ppermute | solution.py:289
  4.3 8.8 %collective-permute-start.2 = (bf16[30,2048]{1,0:T(8,128)(2,1)}, bf16[30,2048]{1,0:T(8,128)(2,1)S(1)}, u32[]{:S(2)}, u32[]{:S(2)}) collective-permute-start(bf16[30,2048]{1,0:T(8,128)(2,1)} %own_hbm.1), channel_id=1, source_target_pairs={{3,0},{0,1},{1,2},{2,3},{7,4},{4,5},{5,6},{6,7},{11,8},{8,9},{9,10... | collective-permute-start | bytes 368648 | tf_op jit(solution)/shard_map/ppermute | solution.py:289
  4.3 8.8 %collective-permute-start.1 = (bf16[30,2048]{1,0:T(8,128)(2,1)}, bf16[30,2048]{1,0:T(8,128)(2,1)S(1)}, u32[]{:S(2)}, u32[]{:S(2)}) collective-permute-start(bf16[30,2048]{1,0:T(8,128)(2,1)} %own_hbm.1), channel_id=1, source_target_pairs={{2,0},{3,1},{0,2},{1,3},{6,4},{7,5},{4,6},{5,7},{10,8},{11,9},{8,1... | collective-permute-start | bytes 368648 | tf_op jit(solution)/shard_map/ppermute | solution.py:289
  15.3 23.2 %all-to-all-start = ((bf16[64,8,128]{2,1,0:T(8,128)(2,1)}), bf16[64,8,128]{2,1,0:T(8,128)(2,1)S(1)}, u32[]{:S(2)}, u32[]{:S(2)}) async-start(bf16[64,8,128]{2,1,0:T(8,128)(2,1)} %bitcast.5), calls=%async_computation | async-start | bytes 262144 | tf_op jit(solution)/shard_map/all_to_all | solution.py:320
  42.3 15.8 %all-to-all-start.1 = ((bf16[64,2,128]{2,1,0:T(2,128)(2,1)}), bf16[64,2,128]{2,1,0:T(2,128)(2,1)S(1)}, u32[]{:S(2)}, u32[]{:S(2)}) async-start(bf16[64,2,128]{2,1,0:T(2,128)(2,1)} %bitcast.7), calls=%async_computation.1 | async-start | bytes 65536 | tf_op jit(solution)/shard_map/all_to_all | solution.py:334

commit v9 on v8

--- a/solution.py
+++ b/solution.py
@@ -14,7 +14,6 @@
 WIDTH = 256
 
 VMEM = pl.BlockSpec(memory_space=pltpu.VMEM)
-SMEM = pl.BlockSpec(memory_space=pltpu.SMEM)
 HBM = pl.BlockSpec(memory_space=pltpu.HBM)
 VMEM_LIMIT = 32 * 1024 * 1024
 bf16, f32, i32 = jnp.bfloat16, jnp.float32, jnp.int32
@@ -147,8 +146,9 @@
     finish(copies[3:])
 
 
-def first_kernel(groups, v0, v1, v2, v3, g_ref, place_ref, where_ref, stiff_ref,
-                 packed_ref, field_hbm, g_hbm, field_ref, sems):
+def first_kernel(groups, v0, v1, v2, v3, g_ref, place_ref, where_near, stiff_ref,
+                 packed_ref, field_hbm, g_hbm, field_ref, where_ref, sems):
+    table = begin(sems.at[pl.ds(2, 1)], (where_near, where_ref))
     copies = begin(sems, (g_ref, g_hbm))
     me = lax.axis_index("mode")
     owned_blocks, _, _, lanes = field_ref.shape
@@ -159,6 +159,7 @@
         for block in range(owned_blocks):
             field_ref[block, group, :modes_dev, :] = source[:, block * lanes:(block + 1) * lanes]
     copies += begin(sems.at[pl.ds(1, 1)], (field_ref, field_hbm))
+    finish(table)
     mixer = g_ref[...]
     stored, out_blocks = where_ref.shape
     parts = []
@@ -179,9 +180,9 @@
     return begin(sems, *((blocks_ref.at[:, part], stiff_ref.at[:, part]) for part in parts))
 
 
-def between_kernel(steps, field_hbm, g_hbm, recv_ref, where_ref, blocks_ref,
-                   own_ref, r_ref, field_ref, g_ref, mixed_ref, stiff_ref, sems):
-    near = begin(sems, (field_hbm, field_ref), (g_hbm, g_ref))
+def between_kernel(steps, field_hbm, g_hbm, recv_ref, where_near, blocks_ref,
+                   own_ref, r_ref, field_ref, g_ref, mixed_ref, stiff_ref, where_ref, sems):
+    near = begin(sems, (field_hbm, field_ref), (g_hbm, g_ref), (where_near, where_ref))
     stored = where_ref.shape[0]
     copies = own_fetch(steps, stored, blocks_ref, stiff_ref, sems.at[pl.ds(len(near), steps)])
     receive_table(recv_ref, r_ref)
@@ -196,12 +197,14 @@
             )
 
 
-def second_kernel(own_ref, arrived_ref, r_ref, g2_ref, send_ref, where_ref, blocks_ref,
-                  packed_ref, turned_hbm, turned_ref, spread_ref, stiff_ref, sems):
+def second_kernel(own_ref, arrived_ref, r_ref, g2_ref, send_ref, where_near, blocks_ref,
+                  packed_ref, turned_hbm, turned_ref, spread_ref, stiff_ref, where_ref, sems):
+    table = begin(sems.at[pl.ds(2, 1)], (where_near, where_ref))
     near = begin(sems, (last_stored(blocks_ref, stiff_ref), stiff_ref))
     turned = arrived_ref[...].astype(f32).T.astype(bf16)
     turned_ref[...] = turned
     keeps = begin(sems.at[pl.ds(len(near), 1)], (turned_ref, turned_hbm))
+    finish(table)
     stored, out_blocks = where_ref.shape
     owned_blocks = own_ref.shape[0]
     terms = stiff_ref.shape[0]
@@ -226,10 +229,10 @@
     finish(keeps)
 
 
-def own_kernel(groups, steps, where_ref, recv_ref, g2_ref, turned_hbm, own_ref, blocks_ref,
-               first_hbm, own2_ref, r_ref, turned_ref, first_ref, field_ref, mixed_ref, stiff_ref, sems):
+def own_kernel(groups, steps, where_near, recv_ref, g2_ref, turned_hbm, own_ref, blocks_ref,
+               first_hbm, own2_ref, r_ref, turned_ref, first_ref, field_ref, mixed_ref, stiff_ref, where_ref, sems):
     stored = where_ref.shape[0]
-    near = begin(sems, (turned_hbm, turned_ref))
+    near = begin(sems, (turned_hbm, turned_ref), (where_near, where_ref))
     copies = own_fetch(steps, stored, blocks_ref, stiff_ref, sems.at[pl.ds(len(near), steps)])
     me = lax.axis_index("mode")
     receive_table(recv_ref, r_ref)
@@ -301,6 +304,7 @@
     block_flops = 2 * terms * stored * blk * blk
     wide, narrow = (owned_blocks, terms * rows, blk), (owned_blocks, terms * PAD, blk)
 
+    where_scratch = pltpu.SMEM(where.shape, i32)
     own_shape, table_shape = (owned_blocks, rows, blk), (owned_blocks, slots, blk)
 
     g, g2, place, send, recv, own_field, where, stiff = call(
@@ -314,22 +318,23 @@
         functools.partial(first_kernel, groups),
         [Shape((slots, rows), bf16), pltpu.HBM(field_shape, bf16), pltpu.HBM(mixer_shape, bf16)],
         [own_field, others[1], others[2], others[3], g, place, where, stiff],
-        [VMEM] * 6 + [SMEM, VMEM], [VMEM, HBM, HBM],
-        flops=block_flops * (out_blocks - owned_blocks) * rows, scratch=[field_scratch, dma((2,))],
+        [VMEM] * 8, [VMEM, HBM, HBM],
+        flops=block_flops * (out_blocks - owned_blocks) * rows, scratch=[field_scratch, where_scratch, dma((3,))],
     )
     arrived = lax.all_to_all(packed.reshape(peers, cap, rows), "space", split_axis=0, concat_axis=0, tiled=True)
     steps = owned_blocks // 2
     own, r = call(
         functools.partial(between_kernel, steps), [Shape(own_shape, f32), Shape(table_shape, bf16)],
-        [pin(field), pin(g_kept), recv, where, blocks], [HBM, HBM, VMEM, SMEM, HBM], [VMEM] * 2,
+        [pin(field), pin(g_kept), recv, where, blocks], [HBM, HBM, VMEM, VMEM, HBM], [VMEM] * 2,
         flops=block_flops * owned_blocks * rows,
-        scratch=[field_scratch, pltpu.VMEM(mixer_shape, bf16), pltpu.VMEM(wide, bf16), own_scratch, dma((2 + steps,))],
+        scratch=[field_scratch, pltpu.VMEM(mixer_shape, bf16), pltpu.VMEM(wide, bf16), own_scratch, where_scratch,
+                 dma((3 + steps,))],
     )
     packed2, turned = call(
         second_kernel, [Shape((lines, QUARTERS * PAD), bf16), pltpu.HBM((rows, slots), bf16)],
-        [own, arrived.reshape(slots, rows), r, g2, send, where, blocks], [VMEM] * 5 + [SMEM, HBM], [VMEM, HBM],
+        [own, arrived.reshape(slots, rows), r, g2, send, where, blocks], [VMEM] * 6 + [HBM], [VMEM, HBM],
         flops=2 * slots * rows * owned,
-        scratch=[pltpu.VMEM((rows, slots), bf16), pltpu.VMEM((QUARTERS * PAD, QUARTERS * interface), bf16), pltpu.VMEM(if_blocks, bf16), dma((2,))],
+        scratch=[pltpu.VMEM((rows, slots), bf16), pltpu.VMEM((QUARTERS * PAD, QUARTERS * interface), bf16), pltpu.VMEM(if_blocks, bf16), where_scratch, dma((3,))],
     )
     arrived2 = lax.all_to_all(
         packed2.reshape(peers, cap // QUARTERS, QUARTERS * PAD), "space", split_axis=0, concat_axis=0, tiled=True
@@ -337,10 +342,10 @@
     first_apply, own2, r2 = call(
         functools.partial(own_kernel, groups, steps),
         [pltpu.HBM((modes_dev, owned), bf16), Shape((PAD, owned), f32), Shape(table_shape, bf16)],
-        [where, recv, g2, pin(turned), own, blocks], [SMEM, VMEM, VMEM, HBM, VMEM, HBM], [HBM, VMEM, VMEM],
+        [where, recv, g2, pin(turned), own, blocks], [VMEM, VMEM, VMEM, HBM, VMEM, HBM], [HBM, VMEM, VMEM],
         flops=block_flops * owned_blocks * PAD,
         scratch=[pltpu.VMEM((rows, slots), bf16), pltpu.VMEM((modes_dev, owned), bf16), field_scratch, pltpu.VMEM(narrow, bf16),
-                 own_scratch, dma((2 + steps,))],
+                 own_scratch, where_scratch, dma((3 + steps,))],
     )
     second_apply = call(
         last_kernel, [Shape((modes_dev, owned), bf16)],

time: 59.7 us -> 58.3 us (0.977)
  Pallas kernels: 20.5 us -> 18.6 us
  waiting for transfers between devices: 13.6 us -> 14.7 us
    pallas_call x6, Pallas kernels: 20.5 us -> 18.6 us  [call(): pl.pallas_call(kernel, out_shape=outs, in_specs=in_specs, out_specs=out_s...]
  transfers between devices with their start and end apart: 5 -> 5, of which waited for: 3 -> 3; matrix products, arithmetic and copies ran while one was open for 0% -> 0% of each run, Pallas kernels for 22% -> 21%
where the time goes in v9:
time: 58.3 us; the launch traced here: 58.1 us
  starting transfers between devices  24.1 us (41%)
  Pallas kernels  18.6 us (32%)
  waiting for transfers between devices  14.7 us (25%)
  between operations  0.7 us (1%)
    pallas_call x6, Pallas kernels, call(): pl.pallas_call(kernel, out_shape=outs, in_specs=in_specs, out_specs=out_s...  18.6 us
    all_to_all x1, starting transfers between devices, local(): lax.all_to_all(packed.reshape(peers, cap, rows), 'space', split_axis=0, c...  12.8 us
    all_to_all x1, starting transfers between devices, local(): lax.all_to_all(packed2.reshape(peers, cap // QUARTERS, QUARTERS * PAD), '...  5.97 us
    ppermute x3, waiting for transfers between devices, local(): lax.ppermute(modes_in, 'mode', [((to + s) % groups, to) for to in range(g...  5.64 us
    ppermute x3, starting transfers between devices, local(): lax.ppermute(modes_in, 'mode', [((to + s) % groups, to) for to in range(g...  5.29 us
    all_to_all x1, waiting for transfers between devices, local(): lax.all_to_all(packed2.reshape(peers, cap // QUARTERS, QUARTERS * PAD), '...  4.7 us
    all_to_all x1, waiting for transfers between devices, local(): lax.all_to_all(packed.reshape(peers, cap, rows), 'space', split_axis=0, c...  4.38 us
  transfers between devices with their start and end apart: 5, of which 3 were waited for; matrix products, arithmetic and copies ran while one was open for 0% of the time, Pallas kernels for 21%

profile of v9, /device:TPU:1, one launch (start us, length us, event | category | flops | bytes accessed | tf_op | source)
XLA Modules:
  0.0 58.1 jit_solution(15109172178136306690)
XLA Ops:
  0.6 3.6 %collective-permute-start = (bf16[30,2048]{1,0:T(8,128)(2,1)}, bf16[30,2048]{1,0:T(8,128)(2,1)S(1)}, u32[]{:S(2)}, u32[]{:S(2)}) collective-permute-start(bf16[30,2048]{1,0:T(8,128)(2,1)} %own_hbm.1), channel_id=1, source_target_pairs={{1,0},{2,1},{3,2},{0,3},{5,4},{6,5},{7,6},{4,7},{9,8},{10,9},{11,1... | collective-permute-start | bytes 368648 | tf_op jit(solution)/shard_map/ppermute | solution.py:292
  4.3 0.0 collective-permute-start.2
  4.3 1.6 %collective-permute-start.1 = (bf16[30,2048]{1,0:T(8,128)(2,1)}, bf16[30,2048]{1,0:T(8,128)(2,1)S(1)}, u32[]{:S(2)}, u32[]{:S(2)}) collective-permute-start(bf16[30,2048]{1,0:T(8,128)(2,1)} %own_hbm.1), channel_id=1, source_target_pairs={{2,0},{3,1},{0,2},{1,3},{6,4},{7,5},{4,6},{5,7},{10,8},{11,9},{8,1... | collective-permute-start | bytes 368648 | tf_op jit(solution)/shard_map/ppermute | solution.py:292
  5.9 1.5 %shard_map.86 = (bf16[128,640]{1,0:T(8,128)(2,1)S(1)}, bf16[160,128]{1,0:T(8,128)(2,1)S(1)}, bf16[512,256]{1,0:T(8,128)(2,1)S(1)}, s32[1,256]{1,0:T(1,128)S(1)},...) custom-call(s32[5,8,120]{2,1,0:T(8,128)} %bitcast.11, ...), custom_call_target="tpu_custom_call" | custom-call | flops 1000000 | bytes 13865024 | tf_op jit(solution)/shard_map/pallas_call | solution.py:24
  7.5 0.0 collective-permute-done.v1
  7.5 5.6 %collective-permute-done.2.v3 = bf16[30,2048]{1,0:T(8,128)(2,1)S(1)} collective-permute-done((bf16[30,2048]{1,0:T(8,128)(2,1)}, bf16[30,2048]{1,0:T(8,128)(2,1)S(1)}, u32[]{:S(2)}, u32[]{:S(2)}) %collective-permute-start.2) | collective-permute-done | bytes 122912 | tf_op jit(solution)/shard_map/ppermute | solution.py:292
  13.1 0.0 collective-permute-done.1.v2
  13.1 2.3 %shard_map.87 = (bf16[512,128]{1,0:T(8,128)(2,1)}, bf16[16,4,32,128]{3,2,1,0:T(8,128)(2,1)}, bf16[128,640]{1,0:T(8,128)(2,1)}) custom-call(bf16[30,2048]{1,0:T(8,128)(2,1)S(1)} %get-tuple-element.23.v0, bf16[30,2048]{1,0:T(8,128)(2,1)S(1)} %collective-permute-done.v1, bf16[30,2048]{1,0:T(8,128)(2,1)S(1)} %collective-permute-done.1.v2, ...), custom_call_target="tpu_custom_call" | custom-call | flops 167772160 | bytes 3047712 | tf_op jit(solution)/shard_map/pallas_call | solution.py:24
  15.4 12.8 %all-to-all-start = ((bf16[64,8,128]{2,1,0:T(8,128)(2,1)}), bf16[64,8,128]{2,1,0:T(8,128)(2,1)S(1)}, u32[]{:S(2)}, u32[]{:S(2)}) async-start(bf16[64,8,128]{2,1,0:T(8,128)(2,1)} %bitcast.5), calls=%async_computation | async-start | bytes 262144 | tf_op jit(solution)/shard_map/all_to_all | solution.py:324
  28.2 6.0 %shard_map.88 = (f32[16,128,128]{2,1,0:T(8,128)S(1)}, bf16[16,512,128]{2,1,0:T(8,128)(2,1)S(1)}) custom-call(bf16[16,4,32,128]{3,2,1,0:T(8,128)(2,1)} %get-tuple-element.27.field_hbm, bf16[128,640]{1,0:T(8,128)(2,1)} %get-tuple-element.28.g_hbm, s32[1,512]{1,0:T(1,128)S(1)} %get-tuple-element.21.recv_ref, s32[4,18]{1,0:T(4,128)S(1)} %get-tuple-element.20.where_near, ...), custom_call_target="tpu_custom_call" | custom-call | flops 1342177280 | bytes 15632672 | tf_op jit(solution)/shard_map/pallas_call | solution.py:24
  34.2 4.4 %all-to-all-done = bf16[64,8,128]{2,1,0:T(8,128)(2,1)S(1)} async-done(((bf16[64,8,128]{2,1,0:T(8,128)(2,1)}), bf16[64,8,128]{2,1,0:T(8,128)(2,1)S(1)}, u32[]{:S(2)}, u32[]{:S(2)}) %all-to-all-start) | async-done | bytes 131104 | tf_op jit(solution)/shard_map/all_to_all | solution.py:324
  38.6 3.0 %shard_map.89 = (bf16[128,128]{1,0:T(8,128)(2,1)}, bf16[128,512]{1,0:T(8,128)(2,1)}) custom-call(f32[16,128,128]{2,1,0:T(8,128)S(1)} %get-tuple-element.29.own_ref, bf16[512,128]{1,0:T(8,128)(2,1)S(1)} %bitcast.9, bf16[16,512,128]{2,1,0:T(8,128)(2,1)S(1)} %get-tuple-element.31.r_ref, bf16[160,128]{1,0:T(8,128)(2,1)S(1)} %get-tuple-element.22.g2_ref, ...), custom_call_target="tpu_custom_call" | custom-call | flops 268435456 | bytes 15279392 | tf_op jit(solution)/shard_map/pallas_call | solution.py:24
  41.5 6.0 %all-to-all-start.1 = ((bf16[64,2,128]{2,1,0:T(2,128)(2,1)}), bf16[64,2,128]{2,1,0:T(2,128)(2,1)S(1)}, u32[]{:S(2)}, u32[]{:S(2)}) async-start(bf16[64,2,128]{2,1,0:T(2,128)(2,1)} %bitcast.7), calls=%async_computation.1 | async-start | bytes 65536 | tf_op jit(solution)/shard_map/all_to_all | solution.py:339
  47.5 4.6 %shard_map.90 = (bf16[30,2048]{1,0:T(8,128)(2,1)}, f32[32,2048]{1,0:T(8,128)S(1)}, bf16[16,512,128]{2,1,0:T(8,128)(2,1)S(1)}) custom-call(s32[4,18]{1,0:T(4,128)S(1)} %get-tuple-element.20.where_near, s32[1,512]{1,0:T(1,128)S(1)} %get-tuple-element.21.recv_ref, bf16[160,128]{1,0:T(8,128)(2,1)S(1)} %get-tuple-element.22.g2_ref, ...), custom_call_target="tpu_custom_call" | custom-call | flops 335544320 | bytes 15501600 | tf_op jit(solution)/shard_map/pallas_call | solution.py:24
  52.1 4.7 %all-to-all-done.1 = bf16[64,2,128]{2,1,0:T(2,128)(2,1)S(1)} async-done(((bf16[64,2,128]{2,1,0:T(2,128)(2,1)}), bf16[64,2,128]{2,1,0:T(2,128)(2,1)S(1)}, u32[]{:S(2)}, u32[]{:S(2)}) %all-to-all-start.1) | async-done | bytes 32800 | tf_op jit(solution)/shard_map/all_to_all | solution.py:339
  56.8 1.3 %shard_map.91 = bf16[30,2048]{1,0:T(8,128)(2,1)} custom-call(f32[32,2048]{1,0:T(8,128)S(1)} %get-tuple-element.35.own_ref, bf16[128,128]{1,0:T(8,128)(2,1)S(1)} %bitcast.10, bf16[16,512,128]{2,1,0:T(8,128)(2,1)S(1)} %get-tuple-element.37.r_ref), custom_call_target="tpu_custom_call" | custom-call | flops 67108864 | bytes 2514944 | tf_op jit(solution)/shard_map/pallas_call | solution.py:24
Async XLA Ops:
  0.6 6.8 %collective-permute-start = (bf16[30,2048]{1,0:T(8,128)(2,1)}, bf16[30,2048]{1,0:T(8,128)(2,1)S(1)}, u32[]{:S(2)}, u32[]{:S(2)}) collective-permute-start(bf16[30,2048]{1,0:T(8,128)(2,1)} %own_hbm.1), channel_id=1, source_target_pairs={{1,0},{2,1},{3,2},{0,3},{5,4},{6,5},{7,6},{4,7},{9,8},{10,9},{11,1... | collective-permute-start | bytes 368648 | tf_op jit(solution)/shard_map/ppermute | solution.py:292
  4.3 8.8 %collective-permute-start.2 = (bf16[30,2048]{1,0:T(8,128)(2,1)}, bf16[30,2048]{1,0:T(8,128)(2,1)S(1)}, u32[]{:S(2)}, u32[]{:S(2)}) collective-permute-start(bf16[30,2048]{1,0:T(8,128)(2,1)} %own_hbm.1), channel_id=1, source_target_pairs={{3,0},{0,1},{1,2},{2,3},{7,4},{4,5},{5,6},{6,7},{11,8},{8,9},{9,10... | collective-permute-start | bytes 368648 | tf_op jit(solution)/shard_map/ppermute | solution.py:292
  4.3 8.8 %collective-permute-start.1 = (bf16[30,2048]{1,0:T(8,128)(2,1)}, bf16[30,2048]{1,0:T(8,128)(2,1)S(1)}, u32[]{:S(2)}, u32[]{:S(2)}) collective-permute-start(bf16[30,2048]{1,0:T(8,128)(2,1)} %own_hbm.1), channel_id=1, source_target_pairs={{2,0},{3,1},{0,2},{1,3},{6,4},{7,5},{4,6},{5,7},{10,8},{11,9},{8,1... | collective-permute-start | bytes 368648 | tf_op jit(solution)/shard_map/ppermute | solution.py:292
  15.4 23.2 %all-to-all-start = ((bf16[64,8,128]{2,1,0:T(8,128)(2,1)}), bf16[64,8,128]{2,1,0:T(8,128)(2,1)S(1)}, u32[]{:S(2)}, u32[]{:S(2)}) async-start(bf16[64,8,128]{2,1,0:T(8,128)(2,1)} %bitcast.5), calls=%async_computation | async-start | bytes 262144 | tf_op jit(solution)/shard_map/all_to_all | solution.py:324
  41.5 15.3 %all-to-all-start.1 = ((bf16[64,2,128]{2,1,0:T(2,128)(2,1)}), bf16[64,2,128]{2,1,0:T(2,128)(2,1)S(1)}, u32[]{:S(2)}, u32[]{:S(2)}) async-start(bf16[64,2,128]{2,1,0:T(2,128)(2,1)} %bitcast.7), calls=%async_computation.1 | async-start | bytes 65536 | tf_op jit(solution)/shard_map/all_to_all | solution.py:339

commit v10 on v9

--- a/solution.py
+++ b/solution.py
@@ -75,14 +75,14 @@
     return total.astype(bf16)
 
 
-def receive_table(recv_ref, r_ref):
+def receive_table(recv_ref, r_ref, blocks):
     slots = recv_ref.shape[1]
     lanes = lax.broadcasted_iota(i32, (LANES, LANES), 1)
     for start in range(0, slots, LANES):
         at = slice(start, start + LANES)
         offset = jnp.broadcast_to(recv_ref[:, at].astype(f32), (LANES, LANES)).T.astype(i32) - lanes
-        for block in range(r_ref.shape[0]):
-            r_ref[block, at, :] = one_hot(offset == block * LANES)
+        for place, block in enumerate(blocks):
+            r_ref[place, at, :] = one_hot(offset == block * LANES)
 
 
 def block_row(row, rows, cols_ref, mixed_ref, stiff):
@@ -147,9 +147,8 @@
 
 
 def first_kernel(groups, v0, v1, v2, v3, g_ref, place_ref, where_near, stiff_ref,
-                 packed_ref, field_hbm, g_hbm, field_ref, where_ref, sems):
-    table = begin(sems.at[pl.ds(2, 1)], (where_near, where_ref))
-    copies = begin(sems, (g_ref, g_hbm))
+                 packed_ref, field_ref, where_ref, sems):
+    table = begin(sems, (where_near, where_ref))
     me = lax.axis_index("mode")
     owned_blocks, _, _, lanes = field_ref.shape
     modes_dev = v0.shape[0]
@@ -158,7 +157,6 @@
         group = lax.rem(me + slot, groups)
         for block in range(owned_blocks):
             field_ref[block, group, :modes_dev, :] = source[:, block * lanes:(block + 1) * lanes]
-    copies += begin(sems.at[pl.ds(1, 1)], (field_ref, field_hbm))
     finish(table)
     mixer = g_ref[...]
     stored, out_blocks = where_ref.shape
@@ -171,7 +169,6 @@
         parts.append(mixed_row(picked, stiff_ref[:, at:at + stored], mixer))
     part = jnp.concatenate(parts, axis=1).astype(bf16)
     packed_ref[...] = dot_t(place_ref[...], part).astype(bf16)
-    finish(copies)
 
 
 def own_fetch(steps, stored, blocks_ref, stiff_ref, sems):
@@ -180,14 +177,15 @@
     return begin(sems, *((blocks_ref.at[:, part], stiff_ref.at[:, part]) for part in parts))
 
 
-def between_kernel(steps, field_hbm, g_hbm, recv_ref, where_near, blocks_ref,
-                   own_ref, r_ref, field_ref, g_ref, mixed_ref, stiff_ref, where_ref, sems):
-    near = begin(sems, (field_hbm, field_ref), (g_hbm, g_ref), (where_near, where_ref))
+def between_kernel(steps, field_ref, g_ref, recv_ref, where_near, blocks_ref,
+                   own_ref, r_ref, mixed_ref, stiff_ref, where_ref, sems):
+    near = begin(sems, (where_near, where_ref))
     stored = where_ref.shape[0]
     copies = own_fetch(steps, stored, blocks_ref, stiff_ref, sems.at[pl.ds(len(near), steps)])
-    receive_table(recv_ref, r_ref)
+    mix(stacked(g_ref[...]), field_ref, mixed_ref)
     finish(near)
-    mix(stacked(g_ref[...]), field_ref, mixed_ref)
+    read = [(c, row) for row in range(own_ref.shape[0], where_ref.shape[1]) for c in range(stored)]
+    receive_table(recv_ref, r_ref, [where_ref[c, row] for c, row in read])
     per = own_ref.shape[0] // steps
     for step in range(steps):
         copies[step].wait()
@@ -213,7 +211,8 @@
     for row in range(owned_blocks, out_blocks):
         columns = [where_ref[c, row] for c in range(stored)]
         base = jnp.concatenate([own_ref[column] for column in columns], axis=1)
-        table = jnp.concatenate([r_ref[column] for column in columns], axis=1)
+        first = (row - owned_blocks) * stored
+        table = jnp.concatenate([r_ref[first + c] for c in range(stored)], axis=1)
         picks.append((base + dot(turned, table)).astype(bf16))
     width = send_ref.shape[1]
     lines = lax.broadcasted_iota(i32, (packed_ref.shape[0], width), 0) * QUARTERS
@@ -235,7 +234,7 @@
     near = begin(sems, (turned_hbm, turned_ref), (where_near, where_ref))
     copies = own_fetch(steps, stored, blocks_ref, stiff_ref, sems.at[pl.ds(len(near), steps)])
     me = lax.axis_index("mode")
-    receive_table(recv_ref, r_ref)
+    receive_table(recv_ref, r_ref, range(r_ref.shape[0]))
     owned_blocks, _, lanes = own_ref.shape
     finish(near)
     turned = turned_ref[...]
@@ -259,18 +258,24 @@
     finish(keeps)
 
 
-def last_kernel(own_ref, arrived_ref, r_ref, out_ref, slots_ref):
+def last_kernel(own_ref, arrived_ref, r_ref, out_hbm, slots_ref, out_ref, sems):
     arrived = arrived_ref[...].astype(f32)
     lines = arrived.shape[0]
     for quarter in range(QUARTERS):
         turned = pltpu.roll(arrived, (QUARTERS - quarter) % QUARTERS * PAD, 1)
         slots_ref[pl.ds(quarter, lines, stride=QUARTERS), :] = turned
     by_slot = slots_ref[...].T[:PAD, :].astype(bf16)
+    span = r_ref.shape[0] // sems.shape[0]
+    copies = []
     for block in range(0, r_ref.shape[0], 2):
         at = slice(block * LANES, (block + 2) * LANES)
         table = jnp.concatenate([r_ref[block], r_ref[block + 1]], axis=1)
         total = own_ref[:, at] + dot(by_slot, table)
         out_ref[:, at] = total.astype(bf16)[:out_ref.shape[0], :]
+        if (block + 2) % span == 0:
+            part = pl.ds((block + 2 - span) * LANES, span * LANES)
+            copies += begin(sems.at[pl.ds(len(copies), 1)], (out_ref.at[:, part], out_hbm.at[:, part]))
+    finish(copies)
 
 
 def local(groups, peers, modes_in, blocks, block_cols, send_slot, recv_row, mix_cols, mix_coef):
@@ -314,21 +319,20 @@
         [mix_cols, mix_coef, send, recv, pin(modes_in), where, blocks], [HBM] * 7, [VMEM] * 8, flops=10**6,
         scratch=[*tables, dma((7,))],
     )
-    packed, field, g_kept = call(
+    packed, field = call(
         functools.partial(first_kernel, groups),
-        [Shape((slots, rows), bf16), pltpu.HBM(field_shape, bf16), pltpu.HBM(mixer_shape, bf16)],
+        [Shape((slots, rows), bf16), Shape(field_shape, bf16)],
         [own_field, others[1], others[2], others[3], g, place, where, stiff],
-        [VMEM] * 8, [VMEM, HBM, HBM],
-        flops=block_flops * (out_blocks - owned_blocks) * rows, scratch=[field_scratch, where_scratch, dma((3,))],
+        [VMEM] * 8, [VMEM] * 2,
+        flops=block_flops * (out_blocks - owned_blocks) * rows, scratch=[where_scratch, dma((1,))],
     )
     arrived = lax.all_to_all(packed.reshape(peers, cap, rows), "space", split_axis=0, concat_axis=0, tiled=True)
     steps = owned_blocks // 2
     own, r = call(
-        functools.partial(between_kernel, steps), [Shape(own_shape, f32), Shape(table_shape, bf16)],
-        [pin(field), pin(g_kept), recv, where, blocks], [HBM, HBM, VMEM, VMEM, HBM], [VMEM] * 2,
+        functools.partial(between_kernel, steps), [Shape(own_shape, f32), Shape((if_blocks[1], slots, blk), bf16)],
+        [field, g, recv, where, blocks], [VMEM] * 4 + [HBM], [VMEM] * 2,
         flops=block_flops * owned_blocks * rows,
-        scratch=[field_scratch, pltpu.VMEM(mixer_shape, bf16), pltpu.VMEM(wide, bf16), own_scratch, where_scratch,
-                 dma((3 + steps,))],
+        scratch=[pltpu.VMEM(wide, bf16), own_scratch, where_scratch, dma((1 + steps,))],
     )
     packed2, turned = call(
         second_kernel, [Shape((lines, QUARTERS * PAD), bf16), pltpu.HBM((rows, slots), bf16)],
@@ -348,9 +352,9 @@
                  own_scratch, where_scratch, dma((3 + steps,))],
     )
     second_apply = call(
-        last_kernel, [Shape((modes_dev, owned), bf16)],
-        [own2, arrived2.reshape(lines, QUARTERS * PAD), r2], [VMEM] * 3, [VMEM], flops=2 * slots * PAD * owned,
-        scratch=[pltpu.VMEM((slots, QUARTERS * PAD), f32)],
+        last_kernel, [pltpu.HBM((modes_dev, owned), bf16)],
+        [own2, arrived2.reshape(lines, QUARTERS * PAD), r2], [VMEM] * 3, [HBM], flops=2 * slots * PAD * owned,
+        scratch=[pltpu.VMEM((slots, QUARTERS * PAD), f32), pltpu.VMEM((modes_dev, owned), bf16), dma((owned_blocks // 4,))],
     )[0]
     return (first_apply, second_apply)
 

time: 58.3 us -> 57.9 us (level)
  Pallas kernels: 18.6 us -> 18 us
  starting transfers between devices: 24.1 us -> 23.5 us
  waiting for transfers between devices: 14.7 us -> 15.3 us
    pallas_call x6, Pallas kernels: 18.6 us -> 18 us  [call(): pl.pallas_call(kernel, out_shape=outs, in_specs=in_specs, out_specs=out_s...]
  transfers between devices with their start and end apart: 5 -> 5, of which waited for: 3 -> 3; matrix products, arithmetic and copies ran while one was open for 0% -> 0% of each run, Pallas kernels for 21% -> 20%
where the time goes in v10:
time: 57.9 us; the launch traced here: 57.6 us
  starting transfers between devices  23.5 us (41%)
  Pallas kernels  18 us (31%)
  waiting for transfers between devices  15.3 us (26%)
  between operations  0.86 us (1%)
    pallas_call x6, Pallas kernels, call(): pl.pallas_call(kernel, out_shape=outs, in_specs=in_specs, out_specs=out_s...  18 us
    all_to_all x1, starting transfers between devices, local(): lax.all_to_all(packed.reshape(peers, cap, rows), 'space', split_axis=0, c...  12.8 us
    ppermute x3, waiting for transfers between devices, local(): lax.ppermute(modes_in, 'mode', [((to + s) % groups, to) for to in range(g...  5.64 us
    all_to_all x1, starting transfers between devices, local(): lax.all_to_all(packed2.reshape(peers, cap // QUARTERS, QUARTERS * PAD), '...  5.41 us
    ppermute x3, starting transfers between devices, local(): lax.ppermute(modes_in, 'mode', [((to + s) % groups, to) for to in range(g...  5.29 us
    all_to_all x1, waiting for transfers between devices, local(): lax.all_to_all(packed.reshape(peers, cap, rows), 'space', split_axis=0, c...  4.95 us
    all_to_all x1, waiting for transfers between devices, local(): lax.all_to_all(packed2.reshape(peers, cap // QUARTERS, QUARTERS * PAD), '...  4.7 us
  transfers between devices with their start and end apart: 5, of which 3 were waited for; matrix products, arithmetic and copies ran while one was open for 0% of the time, Pallas kernels for 20%

profile of v10, /device:TPU:1, one launch (start us, length us, event | category | flops | bytes accessed | tf_op | source)
XLA Modules:
  0.0 57.6 jit_solution(1017780872104904611)
XLA Ops:
  0.6 3.6 %collective-permute-start = (bf16[30,2048]{1,0:T(8,128)(2,1)}, bf16[30,2048]{1,0:T(8,128)(2,1)S(1)}, u32[]{:S(2)}, u32[]{:S(2)}) collective-permute-start(bf16[30,2048]{1,0:T(8,128)(2,1)} %own_hbm.1), channel_id=1, source_target_pairs={{1,0},{2,1},{3,2},{0,3},{5,4},{6,5},{7,6},{4,7},{9,8},{10,9},{11,1... | collective-permute-start | bytes 368648 | tf_op jit(solution)/shard_map/ppermute | solution.py:297
  4.3 0.0 collective-permute-start.2
  4.3 1.6 %collective-permute-start.1 = (bf16[30,2048]{1,0:T(8,128)(2,1)}, bf16[30,2048]{1,0:T(8,128)(2,1)S(1)}, u32[]{:S(2)}, u32[]{:S(2)}) collective-permute-start(bf16[30,2048]{1,0:T(8,128)(2,1)} %own_hbm.1), channel_id=1, source_target_pairs={{2,0},{3,1},{0,2},{1,3},{6,4},{7,5},{4,6},{5,7},{10,8},{11,9},{8,1... | collective-permute-start | bytes 368648 | tf_op jit(solution)/shard_map/ppermute | solution.py:297
  5.9 1.5 %shard_map.86 = (bf16[128,640]{1,0:T(8,128)(2,1)S(1)}, bf16[160,128]{1,0:T(8,128)(2,1)S(1)}, bf16[512,256]{1,0:T(8,128)(2,1)S(1)}, s32[1,256]{1,0:T(1,128)S(1)},...) custom-call(s32[5,8,120]{2,1,0:T(8,128)} %bitcast.11, ...), custom_call_target="tpu_custom_call" | custom-call | flops 1000000 | bytes 13865024 | tf_op jit(solution)/shard_map/pallas_call | solution.py:24
  7.5 0.0 collective-permute-done.v1
  7.5 5.6 %collective-permute-done.2.v3 = bf16[30,2048]{1,0:T(8,128)(2,1)S(1)} collective-permute-done((bf16[30,2048]{1,0:T(8,128)(2,1)}, bf16[30,2048]{1,0:T(8,128)(2,1)S(1)}, u32[]{:S(2)}, u32[]{:S(2)}) %collective-permute-start.2) | collective-permute-done | bytes 122912 | tf_op jit(solution)/shard_map/ppermute | solution.py:297
  13.1 0.0 collective-permute-done.1.v2
  13.1 2.3 %shard_map.87 = (bf16[512,128]{1,0:T(8,128)(2,1)}, bf16[16,4,32,128]{3,2,1,0:T(8,128)(2,1)S(1)}) custom-call(bf16[30,2048]{1,0:T(8,128)(2,1)S(1)} %get-tuple-element.22.v0, bf16[30,2048]{1,0:T(8,128)(2,1)S(1)} %collective-permute-done.v1, bf16[30,2048]{1,0:T(8,128)(2,1)S(1)} %collective-permute-done.1.v2, bf16[30,2048]{1,0:T(8,128)(2,1)S(1)} %collective-permute-done.2.v3, ...), custom_call_target="tpu_custom_call" | custom-call | flops 167772160 | bytes 2883872 | tf_op jit(solution)/shard_map/pallas_call | solution.py:24
  15.4 12.8 %all-to-all-start = ((bf16[64,8,128]{2,1,0:T(8,128)(2,1)}), bf16[64,8,128]{2,1,0:T(8,128)(2,1)S(1)}, u32[]{:S(2)}, u32[]{:S(2)}) async-start(bf16[64,8,128]{2,1,0:T(8,128)(2,1)} %bitcast.5), calls=%async_computation | async-start | bytes 262144 | tf_op jit(solution)/shard_map/all_to_all | solution.py:329
  28.2 5.4 %shard_map.88 = (f32[16,128,128]{2,1,0:T(8,128)S(1)}, bf16[8,512,128]{2,1,0:T(8,128)(2,1)S(1)}) custom-call(bf16[16,4,32,128]{3,2,1,0:T(8,128)(2,1)S(1)} %get-tuple-element.26.field_ref, bf16[128,640]{1,0:T(8,128)(2,1)S(1)} %get-tuple-element.23.g_ref, s32[1,512]{1,0:T(1,128)S(1)} %get-tuple-element.20.recv_ref, s32[4,18]{1,0:T(4,128)S(1)} %get-tuple-element.19.where_near, ...), custom_call_target="tpu_custom_call" | custom-call | flops 1342177280 | bytes 14584096 | tf_op jit(solution)/shard_map/pallas_call | solution.py:24
  33.6 5.0 %all-to-all-done = bf16[64,8,128]{2,1,0:T(8,128)(2,1)S(1)} async-done(((bf16[64,8,128]{2,1,0:T(8,128)(2,1)}), bf16[64,8,128]{2,1,0:T(8,128)(2,1)S(1)}, u32[]{:S(2)}, u32[]{:S(2)}) %all-to-all-start) | async-done | bytes 131104 | tf_op jit(solution)/shard_map/all_to_all | solution.py:329
  38.5 3.0 %shard_map.89 = (bf16[128,128]{1,0:T(8,128)(2,1)}, bf16[128,512]{1,0:T(8,128)(2,1)}) custom-call(f32[16,128,128]{2,1,0:T(8,128)S(1)} %get-tuple-element.27.own_ref, bf16[512,128]{1,0:T(8,128)(2,1)S(1)} %bitcast.9, bf16[8,512,128]{2,1,0:T(8,128)(2,1)S(1)} %get-tuple-element.29.r_ref, bf16[160,128]{1,0:T(8,128)(2,1)S(1)} %get-tuple-element.21.g2_ref, ...), custom_call_target="tpu_custom_call" | custom-call | flops 268435456 | bytes 14230816 | tf_op jit(solution)/shard_map/pallas_call | solution.py:24
  41.5 5.4 %all-to-all-start.1 = ((bf16[64,2,128]{2,1,0:T(2,128)(2,1)}), bf16[64,2,128]{2,1,0:T(2,128)(2,1)S(1)}, u32[]{:S(2)}, u32[]{:S(2)}) async-start(bf16[64,2,128]{2,1,0:T(2,128)(2,1)} %bitcast.7), calls=%async_computation.1 | async-start | bytes 65536 | tf_op jit(solution)/shard_map/all_to_all | solution.py:343
  46.9 4.6 %shard_map.90 = (bf16[30,2048]{1,0:T(8,128)(2,1)}, f32[32,2048]{1,0:T(8,128)S(1)}, bf16[16,512,128]{2,1,0:T(8,128)(2,1)S(1)}) custom-call(s32[4,18]{1,0:T(4,128)S(1)} %get-tuple-element.19.where_near, s32[1,512]{1,0:T(1,128)S(1)} %get-tuple-element.20.recv_ref, bf16[160,128]{1,0:T(8,128)(2,1)S(1)} %get-tuple-element.21.g2_ref, ...), custom_call_target="tpu_custom_call" | custom-call | flops 335544320 | bytes 15501600 | tf_op jit(solution)/shard_map/pallas_call | solution.py:24
  51.5 4.7 %all-to-all-done.1 = bf16[64,2,128]{2,1,0:T(2,128)(2,1)S(1)} async-done(((bf16[64,2,128]{2,1,0:T(2,128)(2,1)}), bf16[64,2,128]{2,1,0:T(2,128)(2,1)S(1)}, u32[]{:S(2)}, u32[]{:S(2)}) %all-to-all-start.1) | async-done | bytes 32800 | tf_op jit(solution)/shard_map/all_to_all | solution.py:343
  56.2 1.3 %shard_map.91 = bf16[30,2048]{1,0:T(8,128)(2,1)} custom-call(f32[32,2048]{1,0:T(8,128)S(1)} %get-tuple-element.33.own_ref, bf16[128,128]{1,0:T(8,128)(2,1)S(1)} %bitcast.10, bf16[16,512,128]{2,1,0:T(8,128)(2,1)S(1)} %get-tuple-element.35.r_ref), custom_call_target="tpu_custom_call" | custom-call | flops 67108864 | bytes 2514944 | tf_op jit(solution)/shard_map/pallas_call | solution.py:24
Async XLA Ops:
  0.6 6.8 %collective-permute-start = (bf16[30,2048]{1,0:T(8,128)(2,1)}, bf16[30,2048]{1,0:T(8,128)(2,1)S(1)}, u32[]{:S(2)}, u32[]{:S(2)}) collective-permute-start(bf16[30,2048]{1,0:T(8,128)(2,1)} %own_hbm.1), channel_id=1, source_target_pairs={{1,0},{2,1},{3,2},{0,3},{5,4},{6,5},{7,6},{4,7},{9,8},{10,9},{11,1... | collective-permute-start | bytes 368648 | tf_op jit(solution)/shard_map/ppermute | solution.py:297
  4.3 8.8 %collective-permute-start.2 = (bf16[30,2048]{1,0:T(8,128)(2,1)}, bf16[30,2048]{1,0:T(8,128)(2,1)S(1)}, u32[]{:S(2)}, u32[]{:S(2)}) collective-permute-start(bf16[30,2048]{1,0:T(8,128)(2,1)} %own_hbm.1), channel_id=1, source_target_pairs={{3,0},{0,1},{1,2},{2,3},{7,4},{4,5},{5,6},{6,7},{11,8},{8,9},{9,10... | collective-permute-start | bytes 368648 | tf_op jit(solution)/shard_map/ppermute | solution.py:297
  4.3 8.8 %collective-permute-start.1 = (bf16[30,2048]{1,0:T(8,128)(2,1)}, bf16[30,2048]{1,0:T(8,128)(2,1)S(1)}, u32[]{:S(2)}, u32[]{:S(2)}) collective-permute-start(bf16[30,2048]{1,0:T(8,128)(2,1)} %own_hbm.1), channel_id=1, source_target_pairs={{2,0},{3,1},{0,2},{1,3},{6,4},{7,5},{4,6},{5,7},{10,8},{11,9},{8,1... | collective-permute-start | bytes 368648 | tf_op jit(solution)/shard_map/ppermute | solution.py:297
  15.4 23.2 %all-to-all-start = ((bf16[64,8,128]{2,1,0:T(8,128)(2,1)}), bf16[64,8,128]{2,1,0:T(8,128)(2,1)S(1)}, u32[]{:S(2)}, u32[]{:S(2)}) async-start(bf16[64,8,128]{2,1,0:T(8,128)(2,1)} %bitcast.5), calls=%async_computation | async-start | bytes 262144 | tf_op jit(solution)/shard_map/all_to_all | solution.py:329
  41.5 14.7 %all-to-all-start.1 = ((bf16[64,2,128]{2,1,0:T(2,128)(2,1)}), bf16[64,2,128]{2,1,0:T(2,128)(2,1)S(1)}, u32[]{:S(2)}, u32[]{:S(2)}) async-start(bf16[64,2,128]{2,1,0:T(2,128)(2,1)} %bitcast.7), calls=%async_computation.1 | async-start | bytes 65536 | tf_op jit(solution)/shard_map/all_to_all | solution.py:343

commit v11 on v10

--- a/solution.py
+++ b/solution.py
@@ -11,7 +11,7 @@
 LANES = 128
 PAD = 32
 QUARTERS = 4
-WIDTH = 256
+TOGETHER = 2
 
 VMEM = pl.BlockSpec(memory_space=pltpu.VMEM)
 HBM = pl.BlockSpec(memory_space=pltpu.HBM)
@@ -187,9 +187,9 @@
     read = [(c, row) for row in range(own_ref.shape[0], where_ref.shape[1]) for c in range(stored)]
     receive_table(recv_ref, r_ref, [where_ref[c, row] for c, row in read])
     per = own_ref.shape[0] // steps
-    for step in range(steps):
-        copies[step].wait()
-        for row in range(step * per, (step + 1) * per):
+    for step in range(0, steps, TOGETHER):
+        finish(copies[step:step + TOGETHER])
+        for row in range(step * per, min(step + TOGETHER, steps) * per):
             own_ref[row] = block_row(
                 row, own_ref.shape[1], where_ref, mixed_ref, stiff_ref[:, row * stored:(row + 1) * stored]
             )
@@ -206,21 +206,24 @@
     stored, out_blocks = where_ref.shape
     owned_blocks = own_ref.shape[0]
     terms = stiff_ref.shape[0]
-    mixer = jnp.concatenate([g2_ref[term * PAD:(term + 1) * PAD, :] for term in range(terms)], axis=1)
+    mixer = g2_ref[...]
     picks = []
     for row in range(owned_blocks, out_blocks):
         columns = [where_ref[c, row] for c in range(stored)]
         base = jnp.concatenate([own_ref[column] for column in columns], axis=1)
         first = (row - owned_blocks) * stored
         table = jnp.concatenate([r_ref[first + c] for c in range(stored)], axis=1)
-        picks.append((base + dot(turned, table)).astype(bf16))
+        mixed = dot(mixer, (base + dot(turned, table)).astype(bf16)).astype(bf16)
+        picks.append(jnp.concatenate([mixed[term * PAD:(term + 1) * PAD, :] for term in range(terms)], axis=1))
     width = send_ref.shape[1]
     lines = lax.broadcasted_iota(i32, (packed_ref.shape[0], width), 0) * QUARTERS
     place = jnp.concatenate([one_hot(send_ref[...] == lines + quarter) for quarter in range(QUARTERS)], axis=1)
     spread_ref[...] = jnp.zeros_like(spread_ref)
     finish(near)
+    depth = terms * stored * LANES
     part = jnp.concatenate(
-        [mixed_row(picked, stiff_ref[:, at * stored:(at + 1) * stored], mixer) for at, picked in enumerate(picks)], axis=1
+        [dot(picked, stiff_ref[:, at * stored:(at + 1) * stored].reshape(depth, LANES)) for at, picked in enumerate(picks)],
+        axis=1,
     ).astype(bf16)
     for quarter in range(QUARTERS):
         spread_ref[quarter * PAD:(quarter + 1) * PAD, quarter * width:(quarter + 1) * width] = part
@@ -249,9 +252,9 @@
         first_ref[:, block * lanes:(block + 1) * lanes] = field_ref[block, me, :first_ref.shape[0], :]
     keeps = begin(sems.at[pl.ds(len(near) + steps, 1)], (first_ref, first_hbm))
     per = owned_blocks // steps
-    for step in range(steps):
-        copies[step].wait()
-        for row in range(step * per, (step + 1) * per):
+    for step in range(0, steps, TOGETHER):
+        finish(copies[step:step + TOGETHER])
+        for row in range(step * per, min(step + TOGETHER, steps) * per):
             own2_ref[:, row * lanes:(row + 1) * lanes] = block_row(
                 row, PAD, where_ref, mixed_ref, stiff_ref[:, row * stored:(row + 1) * stored]
             )

time: 57.9 us -> 57.4 us (level)
  no operation moved by 1% of the time
where the time goes in v11:
time: 57.4 us; the launch traced here: 57.1 us
  starting transfers between devices  23.4 us (41%)
  Pallas kernels  17.7 us (31%)
  waiting for transfers between devices  15.2 us (26%)
  between operations  0.86 us (1%)
    pallas_call x6, Pallas kernels, call(): pl.pallas_call(kernel, out_shape=outs, in_specs=in_specs, out_specs=out_s...  17.7 us
    all_to_all x1, starting transfers between devices, local(): lax.all_to_all(packed.reshape(peers, cap, rows), 'space', split_axis=0, c...  12.8 us
    ppermute x3, waiting for transfers between devices, local(): lax.ppermute(modes_in, 'mode', [((to + s) % groups, to) for to in range(g...  5.64 us
    all_to_all x1, starting transfers between devices, local(): lax.all_to_all(packed2.reshape(peers, cap // QUARTERS, QUARTERS * PAD), '...  5.29 us
    ppermute x3, starting transfers between devices, local(): lax.ppermute(modes_in, 'mode', [((to + s) % groups, to) for to in range(g...  5.29 us
    all_to_all x1, waiting for transfers between devices, local(): lax.all_to_all(packed.reshape(peers, cap, rows), 'space', split_axis=0, c...  5.07 us
    all_to_all x1, waiting for transfers between devices, local(): lax.all_to_all(packed2.reshape(peers, cap // QUARTERS, QUARTERS * PAD), '...  4.49 us
  transfers between devices with their start and end apart: 5, of which 3 were waited for; matrix products, arithmetic and copies ran while one was open for 0% of the time, Pallas kernels for 20%

profile of v11, /device:TPU:1, one launch (start us, length us, event | category | flops | bytes accessed | tf_op | source)
XLA Modules:
  0.0 57.1 jit_solution(2196559569538259665)
XLA Ops:
  0.6 3.6 %collective-permute-start = (bf16[30,2048]{1,0:T(8,128)(2,1)}, bf16[30,2048]{1,0:T(8,128)(2,1)S(1)}, u32[]{:S(2)}, u32[]{:S(2)}) collective-permute-start(bf16[30,2048]{1,0:T(8,128)(2,1)} %own_hbm.1), channel_id=1, source_target_pairs={{1,0},{2,1},{3,2},{0,3},{5,4},{6,5},{7,6},{4,7},{9,8},{10,9},{11,1... | collective-permute-start | bytes 368648 | tf_op jit(solution)/shard_map/ppermute | solution.py:300
  4.3 0.0 collective-permute-start.2
  4.3 1.6 %collective-permute-start.1 = (bf16[30,2048]{1,0:T(8,128)(2,1)}, bf16[30,2048]{1,0:T(8,128)(2,1)S(1)}, u32[]{:S(2)}, u32[]{:S(2)}) collective-permute-start(bf16[30,2048]{1,0:T(8,128)(2,1)} %own_hbm.1), channel_id=1, source_target_pairs={{2,0},{3,1},{0,2},{1,3},{6,4},{7,5},{4,6},{5,7},{10,8},{11,9},{8,1... | collective-permute-start | bytes 368648 | tf_op jit(solution)/shard_map/ppermute | solution.py:300
  5.9 1.5 %shard_map.86 = (bf16[128,640]{1,0:T(8,128)(2,1)S(1)}, bf16[160,128]{1,0:T(8,128)(2,1)S(1)}, bf16[512,256]{1,0:T(8,128)(2,1)S(1)}, s32[1,256]{1,0:T(1,128)S(1)},...) custom-call(s32[5,8,120]{2,1,0:T(8,128)} %bitcast.11, ...), custom_call_target="tpu_custom_call" | custom-call | flops 1000000 | bytes 13865024 | tf_op jit(solution)/shard_map/pallas_call | solution.py:24
  7.5 0.0 collective-permute-done.v1
  7.5 5.6 %collective-permute-done.2.v3 = bf16[30,2048]{1,0:T(8,128)(2,1)S(1)} collective-permute-done((bf16[30,2048]{1,0:T(8,128)(2,1)}, bf16[30,2048]{1,0:T(8,128)(2,1)S(1)}, u32[]{:S(2)}, u32[]{:S(2)}) %collective-permute-start.2) | collective-permute-done | bytes 122912 | tf_op jit(solution)/shard_map/ppermute | solution.py:300
  13.1 0.0 collective-permute-done.1.v2
  13.1 2.3 %shard_map.87 = (bf16[512,128]{1,0:T(8,128)(2,1)}, bf16[16,4,32,128]{3,2,1,0:T(8,128)(2,1)S(1)}) custom-call(bf16[30,2048]{1,0:T(8,128)(2,1)S(1)} %get-tuple-element.22.v0, bf16[30,2048]{1,0:T(8,128)(2,1)S(1)} %collective-permute-done.v1, bf16[30,2048]{1,0:T(8,128)(2,1)S(1)} %collective-permute-done.1.v2, bf16[30,2048]{1,0:T(8,128)(2,1)S(1)} %collective-permute-done.2.v3, ...), custom_call_target="tpu_custom_call" | custom-call | flops 167772160 | bytes 2883872 | tf_op jit(solution)/shard_map/pallas_call | solution.py:24
  15.4 12.8 %all-to-all-start = ((bf16[64,8,128]{2,1,0:T(8,128)(2,1)}), bf16[64,8,128]{2,1,0:T(8,128)(2,1)S(1)}, u32[]{:S(2)}, u32[]{:S(2)}) async-start(bf16[64,8,128]{2,1,0:T(8,128)(2,1)} %bitcast.5), calls=%async_computation | async-start | bytes 262144 | tf_op jit(solution)/shard_map/all_to_all | solution.py:332
  28.2 5.3 %shard_map.88 = (f32[16,128,128]{2,1,0:T(8,128)S(1)}, bf16[8,512,128]{2,1,0:T(8,128)(2,1)S(1)}) custom-call(bf16[16,4,32,128]{3,2,1,0:T(8,128)(2,1)S(1)} %get-tuple-element.26.field_ref, bf16[128,640]{1,0:T(8,128)(2,1)S(1)} %get-tuple-element.23.g_ref, s32[1,512]{1,0:T(1,128)S(1)} %get-tuple-element.20.recv_ref, s32[4,18]{1,0:T(4,128)S(1)} %get-tuple-element.19.where_near, ...), custom_call_target="tpu_custom_call" | custom-call | flops 1342177280 | bytes 14584096 | tf_op jit(solution)/shard_map/pallas_call | solution.py:24
  33.5 5.1 %all-to-all-done = bf16[64,8,128]{2,1,0:T(8,128)(2,1)S(1)} async-done(((bf16[64,8,128]{2,1,0:T(8,128)(2,1)}), bf16[64,8,128]{2,1,0:T(8,128)(2,1)S(1)}, u32[]{:S(2)}, u32[]{:S(2)}) %all-to-all-start) | async-done | bytes 131104 | tf_op jit(solution)/shard_map/all_to_all | solution.py:332
  38.5 2.6 %shard_map.89 = (bf16[128,128]{1,0:T(8,128)(2,1)}, bf16[128,512]{1,0:T(8,128)(2,1)}) custom-call(f32[16,128,128]{2,1,0:T(8,128)S(1)} %get-tuple-element.27.own_ref, bf16[512,128]{1,0:T(8,128)(2,1)S(1)} %bitcast.9, bf16[8,512,128]{2,1,0:T(8,128)(2,1)S(1)} %get-tuple-element.29.r_ref, bf16[160,128]{1,0:T(8,128)(2,1)S(1)} %get-tuple-element.21.g2_ref, ...), custom_call_target="tpu_custom_call" | custom-call | flops 268435456 | bytes 14230816 | tf_op jit(solution)/shard_map/pallas_call | solution.py:24
  41.1 5.3 %all-to-all-start.1 = ((bf16[64,2,128]{2,1,0:T(2,128)(2,1)}), bf16[64,2,128]{2,1,0:T(2,128)(2,1)S(1)}, u32[]{:S(2)}, u32[]{:S(2)}) async-start(bf16[64,2,128]{2,1,0:T(2,128)(2,1)} %bitcast.7), calls=%async_computation.1 | async-start | bytes 65536 | tf_op jit(solution)/shard_map/all_to_all | solution.py:346
  46.4 4.8 %shard_map.90 = (bf16[30,2048]{1,0:T(8,128)(2,1)}, f32[32,2048]{1,0:T(8,128)S(1)}, bf16[16,512,128]{2,1,0:T(8,128)(2,1)S(1)}) custom-call(s32[4,18]{1,0:T(4,128)S(1)} %get-tuple-element.19.where_near, s32[1,512]{1,0:T(1,128)S(1)} %get-tuple-element.20.recv_ref, bf16[160,128]{1,0:T(8,128)(2,1)S(1)} %get-tuple-element.21.g2_ref, ...), custom_call_target="tpu_custom_call" | custom-call | flops 335544320 | bytes 15501600 | tf_op jit(solution)/shard_map/pallas_call | solution.py:24
  51.2 4.5 %all-to-all-done.1 = bf16[64,2,128]{2,1,0:T(2,128)(2,1)S(1)} async-done(((bf16[64,2,128]{2,1,0:T(2,128)(2,1)}), bf16[64,2,128]{2,1,0:T(2,128)(2,1)S(1)}, u32[]{:S(2)}, u32[]{:S(2)}) %all-to-all-start.1) | async-done | bytes 32800 | tf_op jit(solution)/shard_map/all_to_all | solution.py:346
  55.7 1.3 %shard_map.91 = bf16[30,2048]{1,0:T(8,128)(2,1)} custom-call(f32[32,2048]{1,0:T(8,128)S(1)} %get-tuple-element.33.own_ref, bf16[128,128]{1,0:T(8,128)(2,1)S(1)} %bitcast.10, bf16[16,512,128]{2,1,0:T(8,128)(2,1)S(1)} %get-tuple-element.35.r_ref), custom_call_target="tpu_custom_call" | custom-call | flops 67108864 | bytes 2514944 | tf_op jit(solution)/shard_map/pallas_call | solution.py:24
Async XLA Ops:
  0.6 6.8 %collective-permute-start = (bf16[30,2048]{1,0:T(8,128)(2,1)}, bf16[30,2048]{1,0:T(8,128)(2,1)S(1)}, u32[]{:S(2)}, u32[]{:S(2)}) collective-permute-start(bf16[30,2048]{1,0:T(8,128)(2,1)} %own_hbm.1), channel_id=1, source_target_pairs={{1,0},{2,1},{3,2},{0,3},{5,4},{6,5},{7,6},{4,7},{9,8},{10,9},{11,1... | collective-permute-start | bytes 368648 | tf_op jit(solution)/shard_map/ppermute | solution.py:300
  4.3 8.8 %collective-permute-start.2 = (bf16[30,2048]{1,0:T(8,128)(2,1)}, bf16[30,2048]{1,0:T(8,128)(2,1)S(1)}, u32[]{:S(2)}, u32[]{:S(2)}) collective-permute-start(bf16[30,2048]{1,0:T(8,128)(2,1)} %own_hbm.1), channel_id=1, source_target_pairs={{3,0},{0,1},{1,2},{2,3},{7,4},{4,5},{5,6},{6,7},{11,8},{8,9},{9,10... | collective-permute-start | bytes 368648 | tf_op jit(solution)/shard_map/ppermute | solution.py:300
  4.3 8.8 %collective-permute-start.1 = (bf16[30,2048]{1,0:T(8,128)(2,1)}, bf16[30,2048]{1,0:T(8,128)(2,1)S(1)}, u32[]{:S(2)}, u32[]{:S(2)}) collective-permute-start(bf16[30,2048]{1,0:T(8,128)(2,1)} %own_hbm.1), channel_id=1, source_target_pairs={{2,0},{3,1},{0,2},{1,3},{6,4},{7,5},{4,6},{5,7},{10,8},{11,9},{8,1... | collective-permute-start | bytes 368648 | tf_op jit(solution)/shard_map/ppermute | solution.py:300
  15.4 23.2 %all-to-all-start = ((bf16[64,8,128]{2,1,0:T(8,128)(2,1)}), bf16[64,8,128]{2,1,0:T(8,128)(2,1)S(1)}, u32[]{:S(2)}, u32[]{:S(2)}) async-start(bf16[64,8,128]{2,1,0:T(8,128)(2,1)} %bitcast.5), calls=%async_computation | async-start | bytes 262144 | tf_op jit(solution)/shard_map/all_to_all | solution.py:332
  41.1 14.6 %all-to-all-start.1 = ((bf16[64,2,128]{2,1,0:T(2,128)(2,1)}), bf16[64,2,128]{2,1,0:T(2,128)(2,1)S(1)}, u32[]{:S(2)}, u32[]{:S(2)}) async-start(bf16[64,2,128]{2,1,0:T(2,128)(2,1)} %bitcast.7), calls=%async_computation.1 | async-start | bytes 65536 | tf_op jit(solution)/shard_map/all_to_all | solution.py:346

commit v12 on v11

--- a/solution.py
+++ b/solution.py
@@ -296,10 +296,10 @@
     def pin(x):
         return pltpu.with_memory_space_constraint(x, pltpu.HBM)
 
-    others = {
-        s: lax.ppermute(modes_in, "mode", [((to + s) % groups, to) for to in range(groups)])
-        for s in (2, 1, 3)
-    }
+    def from_group(field, s):
+        return lax.ppermute(field, "mode", [((to + s) % groups, to) for to in range(groups)])
+
+    others = {s: from_group(modes_in, s) for s in (3, 2)}
     blocks = pin(blocks)
     where = pin(block_cols.T)
     mix_cols, mix_coef = pin(mix_cols.transpose(0, 2, 1)), pin(mix_coef.transpose(0, 2, 1))
@@ -322,6 +322,7 @@
         [mix_cols, mix_coef, send, recv, pin(modes_in), where, blocks], [HBM] * 7, [VMEM] * 8, flops=10**6,
         scratch=[*tables, dma((7,))],
     )
+    others[1] = from_group(own_field, 1)
     packed, field = call(
         functools.partial(first_kernel, groups),
         [Shape((slots, rows), bf16), Shape(field_shape, bf16)],

time: 57.4 us -> 56.2 us (0.979)
  waiting for transfers between devices: 15.2 us -> 13.9 us
    ppermute x3, waiting for transfers between devices: 5.64 us -> 4.36 us  [from_group(): lax.ppermute(field, 'mode', [((to + s) % groups, to) for to in range(grou...]
    ppermute x3, starting transfers between devices: 5.29 us -> 5.97 us  [from_group(): lax.ppermute(field, 'mode', [((to + s) % groups, to) for to in range(grou...]
  transfers between devices with their start and end apart: 5 -> 5, of which waited for: 3 -> 4; matrix products, arithmetic and copies ran while one was open for 0% -> 0% of each run, Pallas kernels for 20% -> 21%
where the time goes in v12:
time: 56.2 us; the launch traced here: 56 us
  starting transfers between devices  23.5 us (42%)
  Pallas kernels  17.7 us (31%)
  waiting for transfers between devices  13.9 us (25%)
  between operations  0.85 us (2%)
    pallas_call x6, Pallas kernels, call(): pl.pallas_call(kernel, out_shape=outs, in_specs=in_specs, out_specs=out_s...  17.7 us
    all_to_all x1, starting transfers between devices, local(): lax.all_to_all(packed.reshape(peers, cap, rows), 'space', split_axis=0, c...  12.3 us
    ppermute x3, starting transfers between devices, from_group(): lax.ppermute(field, 'mode', [((to + s) % groups, to) for to in range(grou...  5.97 us
    all_to_all x1, starting transfers between devices, local(): lax.all_to_all(packed2.reshape(peers, cap // QUARTERS, QUARTERS * PAD), '...  5.29 us
    all_to_all x1, waiting for transfers between devices, local(): lax.all_to_all(packed.reshape(peers, cap, rows), 'space', split_axis=0, c...  5.06 us
    all_to_all x1, waiting for transfers between devices, local(): lax.all_to_all(packed2.reshape(peers, cap // QUARTERS, QUARTERS * PAD), '...  4.49 us
    ppermute x3, waiting for transfers between devices, from_group(): lax.ppermute(field, 'mode', [((to + s) % groups, to) for to in range(grou...  4.36 us
  transfers between devices with their start and end apart: 5, of which 4 were waited for; matrix products, arithmetic and copies ran while one was open for 0% of the time, Pallas kernels for 21%

profile of v12, /device:TPU:1, one launch (start us, length us, event | category | flops | bytes accessed | tf_op | source)
XLA Modules:
  0.0 56.0 jit_solution(9607351734178176671)
XLA Ops:
  0.6 2.2 %collective-permute-start.2 = (bf16[30,2048]{1,0:T(8,128)(2,1)}, bf16[30,2048]{1,0:T(8,128)(2,1)S(1)}, u32[]{:S(2)}, u32[]{:S(2)}) collective-permute-start(bf16[30,2048]{1,0:T(8,128)(2,1)} %own_hbm.1), channel_id=1, source_target_pairs={{3,0},{0,1},{1,2},{2,3},{7,4},{4,5},{5,6},{6,7},{11,8},{8,9},{9,10... | collective-permute-start | bytes 368648 | tf_op jit(solution)/shard_map/ppermute | solution.py:300
  2.8 2.6 %collective-permute-start.1 = (bf16[30,2048]{1,0:T(8,128)(2,1)}, bf16[30,2048]{1,0:T(8,128)(2,1)S(1)}, u32[]{:S(2)}, u32[]{:S(2)}) collective-permute-start(bf16[30,2048]{1,0:T(8,128)(2,1)} %own_hbm.1), channel_id=1, source_target_pairs={{2,0},{3,1},{0,2},{1,3},{6,4},{7,5},{4,6},{5,7},{10,8},{11,9},{8,1... | collective-permute-start | bytes 368648 | tf_op jit(solution)/shard_map/ppermute | solution.py:300
  5.5 1.5 %shard_map.86 = (bf16[128,640]{1,0:T(8,128)(2,1)S(1)}, bf16[160,128]{1,0:T(8,128)(2,1)S(1)}, bf16[512,256]{1,0:T(8,128)(2,1)S(1)}, s32[1,256]{1,0:T(1,128)S(1)},...) custom-call(s32[5,8,120]{2,1,0:T(8,128)} %bitcast.11, ...), custom_call_target="tpu_custom_call" | custom-call | flops 1000000 | bytes 13865024 | tf_op jit(solution)/shard_map/pallas_call | solution.py:24
  7.0 1.1 %collective-permute-start = (bf16[30,2048]{1,0:T(8,128)(2,1)S(1)}, bf16[30,2048]{1,0:T(8,128)(2,1)S(1)}, u32[]{:S(2)}, u32[]{:S(2)}) collective-permute-start(bf16[30,2048]{1,0:T(8,128)(2,1)S(1)} %get-tuple-element.22.v0), channel_id=1, source_target_pairs={{1,0},{2,1},{3,2},{0,3},{5,4},{6,5},{7,6},{4,7},{9,8},{10,9},{11,1... | collective-permute-start | bytes 368648 | tf_op jit(solution)/shard_map/ppermute | solution.py:300
  8.1 0.0 collective-permute-done.2.v3
  8.1 3.2 %collective-permute-done.1.v2 = bf16[30,2048]{1,0:T(8,128)(2,1)S(1)} collective-permute-done((bf16[30,2048]{1,0:T(8,128)(2,1)}, bf16[30,2048]{1,0:T(8,128)(2,1)S(1)}, u32[]{:S(2)}, u32[]{:S(2)}) %collective-permute-start.1) | collective-permute-done | bytes 122912 | tf_op jit(solution)/shard_map/ppermute | solution.py:300
  11.4 1.1 %collective-permute-done.v1 = bf16[30,2048]{1,0:T(8,128)(2,1)S(1)} collective-permute-done((bf16[30,2048]{1,0:T(8,128)(2,1)S(1)}, bf16[30,2048]{1,0:T(8,128)(2,1)S(1)}, u32[]{:S(2)}, u32[]{:S(2)}) %collective-permute-start) | collective-permute-done | bytes 122912 | tf_op jit(solution)/shard_map/ppermute | solution.py:300
  12.5 2.2 %shard_map.87 = (bf16[512,128]{1,0:T(8,128)(2,1)}, bf16[16,4,32,128]{3,2,1,0:T(8,128)(2,1)S(1)}) custom-call(bf16[30,2048]{1,0:T(8,128)(2,1)S(1)} %get-tuple-element.22.v0, bf16[30,2048]{1,0:T(8,128)(2,1)S(1)} %collective-permute-done.v1, bf16[30,2048]{1,0:T(8,128)(2,1)S(1)} %collective-permute-done.1.v2, bf16[30,2048]{1,0:T(8,128)(2,1)S(1)} %collective-permute-done.2.v3, ...), custom_call_target="tpu_custom_call" | custom-call | flops 167772160 | bytes 2883872 | tf_op jit(solution)/shard_map/pallas_call | solution.py:24
  14.8 12.3 %all-to-all-start = ((bf16[64,8,128]{2,1,0:T(8,128)(2,1)}), bf16[64,8,128]{2,1,0:T(8,128)(2,1)S(1)}, u32[]{:S(2)}, u32[]{:S(2)}) async-start(bf16[64,8,128]{2,1,0:T(8,128)(2,1)} %bitcast.5), calls=%async_computation | async-start | bytes 262144 | tf_op jit(solution)/shard_map/all_to_all | solution.py:333
  27.0 5.3 %shard_map.88 = (f32[16,128,128]{2,1,0:T(8,128)S(1)}, bf16[8,512,128]{2,1,0:T(8,128)(2,1)S(1)}) custom-call(bf16[16,4,32,128]{3,2,1,0:T(8,128)(2,1)S(1)} %get-tuple-element.26.field_ref, bf16[128,640]{1,0:T(8,128)(2,1)S(1)} %get-tuple-element.23.g_ref, s32[1,512]{1,0:T(1,128)S(1)} %get-tuple-element.20.recv_ref, s32[4,18]{1,0:T(4,128)S(1)} %get-tuple-element.19.where_near, ...), custom_call_target="tpu_custom_call" | custom-call | flops 1342177280 | bytes 14584096 | tf_op jit(solution)/shard_map/pallas_call | solution.py:24
  32.3 5.1 %all-to-all-done = bf16[64,8,128]{2,1,0:T(8,128)(2,1)S(1)} async-done(((bf16[64,8,128]{2,1,0:T(8,128)(2,1)}), bf16[64,8,128]{2,1,0:T(8,128)(2,1)S(1)}, u32[]{:S(2)}, u32[]{:S(2)}) %all-to-all-start) | async-done | bytes 131104 | tf_op jit(solution)/shard_map/all_to_all | solution.py:333
  37.4 2.6 %shard_map.89 = (bf16[128,128]{1,0:T(8,128)(2,1)}, bf16[128,512]{1,0:T(8,128)(2,1)}) custom-call(f32[16,128,128]{2,1,0:T(8,128)S(1)} %get-tuple-element.27.own_ref, bf16[512,128]{1,0:T(8,128)(2,1)S(1)} %bitcast.9, bf16[8,512,128]{2,1,0:T(8,128)(2,1)S(1)} %get-tuple-element.29.r_ref, bf16[160,128]{1,0:T(8,128)(2,1)S(1)} %get-tuple-element.21.g2_ref, ...), custom_call_target="tpu_custom_call" | custom-call | flops 268435456 | bytes 14230816 | tf_op jit(solution)/shard_map/pallas_call | solution.py:24
  40.0 5.3 %all-to-all-start.1 = ((bf16[64,2,128]{2,1,0:T(2,128)(2,1)}), bf16[64,2,128]{2,1,0:T(2,128)(2,1)S(1)}, u32[]{:S(2)}, u32[]{:S(2)}) async-start(bf16[64,2,128]{2,1,0:T(2,128)(2,1)} %bitcast.7), calls=%async_computation.1 | async-start | bytes 65536 | tf_op jit(solution)/shard_map/all_to_all | solution.py:347
  45.3 4.8 %shard_map.90 = (bf16[30,2048]{1,0:T(8,128)(2,1)}, f32[32,2048]{1,0:T(8,128)S(1)}, bf16[16,512,128]{2,1,0:T(8,128)(2,1)S(1)}) custom-call(s32[4,18]{1,0:T(4,128)S(1)} %get-tuple-element.19.where_near, s32[1,512]{1,0:T(1,128)S(1)} %get-tuple-element.20.recv_ref, bf16[160,128]{1,0:T(8,128)(2,1)S(1)} %get-tuple-element.21.g2_ref, ...), custom_call_target="tpu_custom_call" | custom-call | flops 335544320 | bytes 15501600 | tf_op jit(solution)/shard_map/pallas_call | solution.py:24
  50.1 4.5 %all-to-all-done.1 = bf16[64,2,128]{2,1,0:T(2,128)(2,1)S(1)} async-done(((bf16[64,2,128]{2,1,0:T(2,128)(2,1)}), bf16[64,2,128]{2,1,0:T(2,128)(2,1)S(1)}, u32[]{:S(2)}, u32[]{:S(2)}) %all-to-all-start.1) | async-done | bytes 32800 | tf_op jit(solution)/shard_map/all_to_all | solution.py:347
  54.6 1.3 %shard_map.91 = bf16[30,2048]{1,0:T(8,128)(2,1)} custom-call(f32[32,2048]{1,0:T(8,128)S(1)} %get-tuple-element.33.own_ref, bf16[128,128]{1,0:T(8,128)(2,1)S(1)} %bitcast.10, bf16[16,512,128]{2,1,0:T(8,128)(2,1)S(1)} %get-tuple-element.35.r_ref), custom_call_target="tpu_custom_call" | custom-call | flops 67108864 | bytes 2514944 | tf_op jit(solution)/shard_map/pallas_call | solution.py:24
Async XLA Ops:
  0.6 7.5 %collective-permute-start.2 = (bf16[30,2048]{1,0:T(8,128)(2,1)}, bf16[30,2048]{1,0:T(8,128)(2,1)S(1)}, u32[]{:S(2)}, u32[]{:S(2)}) collective-permute-start(bf16[30,2048]{1,0:T(8,128)(2,1)} %own_hbm.1), channel_id=1, source_target_pairs={{3,0},{0,1},{1,2},{2,3},{7,4},{4,5},{5,6},{6,7},{11,8},{8,9},{9,10... | collective-permute-start | bytes 368648 | tf_op jit(solution)/shard_map/ppermute | solution.py:300
  2.8 8.5 %collective-permute-start.1 = (bf16[30,2048]{1,0:T(8,128)(2,1)}, bf16[30,2048]{1,0:T(8,128)(2,1)S(1)}, u32[]{:S(2)}, u32[]{:S(2)}) collective-permute-start(bf16[30,2048]{1,0:T(8,128)(2,1)} %own_hbm.1), channel_id=1, source_target_pairs={{2,0},{3,1},{0,2},{1,3},{6,4},{7,5},{4,6},{5,7},{10,8},{11,9},{8,1... | collective-permute-start | bytes 368648 | tf_op jit(solution)/shard_map/ppermute | solution.py:300
  7.0 5.5 %collective-permute-start = (bf16[30,2048]{1,0:T(8,128)(2,1)S(1)}, bf16[30,2048]{1,0:T(8,128)(2,1)S(1)}, u32[]{:S(2)}, u32[]{:S(2)}) collective-permute-start(bf16[30,2048]{1,0:T(8,128)(2,1)S(1)} %get-tuple-element.22.v0), channel_id=1, source_target_pairs={{1,0},{2,1},{3,2},{0,3},{5,4},{6,5},{7,6},{4,7},{9,8},{10,9},{11,1... | collective-permute-start | bytes 368648 | tf_op jit(solution)/shard_map/ppermute | solution.py:300
  14.8 22.6 %all-to-all-start = ((bf16[64,8,128]{2,1,0:T(8,128)(2,1)}), bf16[64,8,128]{2,1,0:T(8,128)(2,1)S(1)}, u32[]{:S(2)}, u32[]{:S(2)}) async-start(bf16[64,8,128]{2,1,0:T(8,128)(2,1)} %bitcast.5), calls=%async_computation | async-start | bytes 262144 | tf_op jit(solution)/shard_map/all_to_all | solution.py:333
  40.0 14.6 %all-to-all-start.1 = ((bf16[64,2,128]{2,1,0:T(2,128)(2,1)}), bf16[64,2,128]{2,1,0:T(2,128)(2,1)S(1)}, u32[]{:S(2)}, u32[]{:S(2)}) async-start(bf16[64,2,128]{2,1,0:T(2,128)(2,1)} %bitcast.7), calls=%async_computation.1 | async-start | bytes 65536 | tf_op jit(solution)/shard_map/all_to_all | solution.py:347

commit v13 on v12

--- a/solution.py
+++ b/solution.py
@@ -126,8 +126,8 @@
 def setup_kernel(groups, cols_hbm, coef_hbm, send_hbm, recv_hbm, own_hbm, where_hbm, blocks_ref,
                  g_ref, g2_ref, place_ref, send_ref, recv_ref, own_ref, where_ref, stiff_ref, cols_ref, coef_ref, sems):
     copies = begin(
-        sems, (cols_hbm, cols_ref), (coef_hbm, coef_ref), (send_hbm, send_ref), (own_hbm, own_ref),
-        (where_hbm, where_ref), (recv_hbm, recv_ref), (last_stored(blocks_ref, stiff_ref), stiff_ref),
+        sems, (cols_hbm, cols_ref), (coef_hbm, coef_ref), (send_hbm, send_ref),
+        (last_stored(blocks_ref, stiff_ref), stiff_ref), (own_hbm, own_ref), (where_hbm, where_ref), (recv_hbm, recv_ref),
     )
     me = lax.axis_index("mode")
     modes = cols_ref.shape[2]
@@ -252,9 +252,9 @@
         first_ref[:, block * lanes:(block + 1) * lanes] = field_ref[block, me, :first_ref.shape[0], :]
     keeps = begin(sems.at[pl.ds(len(near) + steps, 1)], (first_ref, first_hbm))
     per = owned_blocks // steps
-    for step in range(0, steps, TOGETHER):
-        finish(copies[step:step + TOGETHER])
-        for row in range(step * per, min(step + TOGETHER, steps) * per):
+    for step in range(steps):
+        copies[step].wait()
+        for row in range(step * per, (step + 1) * per):
             own2_ref[:, row * lanes:(row + 1) * lanes] = block_row(
                 row, PAD, where_ref, mixed_ref, stiff_ref[:, row * stored:(row + 1) * stored]
             )

time: 56.2 us -> 56.2 us (level)
  transfers between devices with their start and end apart: 5 -> 5, of which waited for: 4 -> 4; matrix products, arithmetic and copies ran while one was open for 0% -> 0% of each run, Pallas kernels for 21% -> 20%
where the time goes in v13:
time: 56.2 us; the launch traced here: 55.9 us
  starting transfers between devices  23.4 us (42%)
  Pallas kernels  17.4 us (31%)
  waiting for transfers between devices  14.2 us (25%)
  between operations  0.85 us (2%)
    pallas_call x6, Pallas kernels, call(): pl.pallas_call(kernel, out_shape=outs, in_specs=in_specs, out_specs=out_s...  17.4 us
    all_to_all x1, starting transfers between devices, local(): lax.all_to_all(packed.reshape(peers, cap, rows), 'space', split_axis=0, c...  12.2 us
    ppermute x3, starting transfers between devices, from_group(): lax.ppermute(field, 'mode', [((to + s) % groups, to) for to in range(grou...  5.97 us
    all_to_all x1, starting transfers between devices, local(): lax.all_to_all(packed2.reshape(peers, cap // QUARTERS, QUARTERS * PAD), '...  5.29 us
    all_to_all x1, waiting for transfers between devices, local(): lax.all_to_all(packed.reshape(peers, cap, rows), 'space', split_axis=0, c...  5.06 us
    all_to_all x1, waiting for transfers between devices, local(): lax.all_to_all(packed2.reshape(peers, cap // QUARTERS, QUARTERS * PAD), '...  4.7 us
    ppermute x3, waiting for transfers between devices, from_group(): lax.ppermute(field, 'mode', [((to + s) % groups, to) for to in range(grou...  4.45 us
  transfers between devices with their start and end apart: 5, of which 4 were waited for; matrix products, arithmetic and copies ran while one was open for 0% of the time, Pallas kernels for 20%

profile of v13, /device:TPU:1, one launch (start us, length us, event | category | flops | bytes accessed | tf_op | source)
XLA Modules:
  0.0 55.9 jit_solution(17121540276122521261)
XLA Ops:
  0.6 2.2 %collective-permute-start.2 = (bf16[30,2048]{1,0:T(8,128)(2,1)}, bf16[30,2048]{1,0:T(8,128)(2,1)S(1)}, u32[]{:S(2)}, u32[]{:S(2)}) collective-permute-start(bf16[30,2048]{1,0:T(8,128)(2,1)} %own_hbm.1), channel_id=1, source_target_pairs={{3,0},{0,1},{1,2},{2,3},{7,4},{4,5},{5,6},{6,7},{11,8},{8,9},{9,10... | collective-permute-start | bytes 368648 | tf_op jit(solution)/shard_map/ppermute | solution.py:300
  2.8 2.6 %collective-permute-start.1 = (bf16[30,2048]{1,0:T(8,128)(2,1)}, bf16[30,2048]{1,0:T(8,128)(2,1)S(1)}, u32[]{:S(2)}, u32[]{:S(2)}) collective-permute-start(bf16[30,2048]{1,0:T(8,128)(2,1)} %own_hbm.1), channel_id=1, source_target_pairs={{2,0},{3,1},{0,2},{1,3},{6,4},{7,5},{4,6},{5,7},{10,8},{11,9},{8,1... | collective-permute-start | bytes 368648 | tf_op jit(solution)/shard_map/ppermute | solution.py:300
  5.5 1.4 %shard_map.86 = (bf16[128,640]{1,0:T(8,128)(2,1)S(1)}, bf16[160,128]{1,0:T(8,128)(2,1)S(1)}, bf16[512,256]{1,0:T(8,128)(2,1)S(1)}, s32[1,256]{1,0:T(1,128)S(1)},...) custom-call(s32[5,8,120]{2,1,0:T(8,128)} %bitcast.11, ...), custom_call_target="tpu_custom_call" | custom-call | flops 1000000 | bytes 13865024 | tf_op jit(solution)/shard_map/pallas_call | solution.py:24
  6.9 1.1 %collective-permute-start = (bf16[30,2048]{1,0:T(8,128)(2,1)S(1)}, bf16[30,2048]{1,0:T(8,128)(2,1)S(1)}, u32[]{:S(2)}, u32[]{:S(2)}) collective-permute-start(bf16[30,2048]{1,0:T(8,128)(2,1)S(1)} %get-tuple-element.22.v0), channel_id=1, source_target_pairs={{1,0},{2,1},{3,2},{0,3},{5,4},{6,5},{7,6},{4,7},{9,8},{10,9},{11,1... | collective-permute-start | bytes 368648 | tf_op jit(solution)/shard_map/ppermute | solution.py:300
  8.0 0.0 collective-permute-done.2.v3
  8.0 3.3 %collective-permute-done.1.v2 = bf16[30,2048]{1,0:T(8,128)(2,1)S(1)} collective-permute-done((bf16[30,2048]{1,0:T(8,128)(2,1)}, bf16[30,2048]{1,0:T(8,128)(2,1)S(1)}, u32[]{:S(2)}, u32[]{:S(2)}) %collective-permute-start.1) | collective-permute-done | bytes 122912 | tf_op jit(solution)/shard_map/ppermute | solution.py:300
  11.4 1.1 %collective-permute-done.v1 = bf16[30,2048]{1,0:T(8,128)(2,1)S(1)} collective-permute-done((bf16[30,2048]{1,0:T(8,128)(2,1)S(1)}, bf16[30,2048]{1,0:T(8,128)(2,1)S(1)}, u32[]{:S(2)}, u32[]{:S(2)}) %collective-permute-start) | collective-permute-done | bytes 122912 | tf_op jit(solution)/shard_map/ppermute | solution.py:300
  12.5 2.2 %shard_map.87 = (bf16[512,128]{1,0:T(8,128)(2,1)}, bf16[16,4,32,128]{3,2,1,0:T(8,128)(2,1)S(1)}) custom-call(bf16[30,2048]{1,0:T(8,128)(2,1)S(1)} %get-tuple-element.22.v0, bf16[30,2048]{1,0:T(8,128)(2,1)S(1)} %collective-permute-done.v1, bf16[30,2048]{1,0:T(8,128)(2,1)S(1)} %collective-permute-done.1.v2, bf16[30,2048]{1,0:T(8,128)(2,1)S(1)} %collective-permute-done.2.v3, ...), custom_call_target="tpu_custom_call" | custom-call | flops 167772160 | bytes 2883872 | tf_op jit(solution)/shard_map/pallas_call | solution.py:24
  14.7 12.2 %all-to-all-start = ((bf16[64,8,128]{2,1,0:T(8,128)(2,1)}), bf16[64,8,128]{2,1,0:T(8,128)(2,1)S(1)}, u32[]{:S(2)}, u32[]{:S(2)}) async-start(bf16[64,8,128]{2,1,0:T(8,128)(2,1)} %bitcast.5), calls=%async_computation | async-start | bytes 262144 | tf_op jit(solution)/shard_map/all_to_all | solution.py:333
  26.9 5.3 %shard_map.88 = (f32[16,128,128]{2,1,0:T(8,128)S(1)}, bf16[8,512,128]{2,1,0:T(8,128)(2,1)S(1)}) custom-call(bf16[16,4,32,128]{3,2,1,0:T(8,128)(2,1)S(1)} %get-tuple-element.26.field_ref, bf16[128,640]{1,0:T(8,128)(2,1)S(1)} %get-tuple-element.23.g_ref, s32[1,512]{1,0:T(1,128)S(1)} %get-tuple-element.20.recv_ref, s32[4,18]{1,0:T(4,128)S(1)} %get-tuple-element.19.where_near, ...), custom_call_target="tpu_custom_call" | custom-call | flops 1342177280 | bytes 14584096 | tf_op jit(solution)/shard_map/pallas_call | solution.py:24
  32.2 5.1 %all-to-all-done = bf16[64,8,128]{2,1,0:T(8,128)(2,1)S(1)} async-done(((bf16[64,8,128]{2,1,0:T(8,128)(2,1)}), bf16[64,8,128]{2,1,0:T(8,128)(2,1)S(1)}, u32[]{:S(2)}, u32[]{:S(2)}) %all-to-all-start) | async-done | bytes 131104 | tf_op jit(solution)/shard_map/all_to_all | solution.py:333
  37.3 2.6 %shard_map.89 = (bf16[128,128]{1,0:T(8,128)(2,1)}, bf16[128,512]{1,0:T(8,128)(2,1)}) custom-call(f32[16,128,128]{2,1,0:T(8,128)S(1)} %get-tuple-element.27.own_ref, bf16[512,128]{1,0:T(8,128)(2,1)S(1)} %bitcast.9, bf16[8,512,128]{2,1,0:T(8,128)(2,1)S(1)} %get-tuple-element.29.r_ref, bf16[160,128]{1,0:T(8,128)(2,1)S(1)} %get-tuple-element.21.g2_ref, ...), custom_call_target="tpu_custom_call" | custom-call | flops 268435456 | bytes 14230816 | tf_op jit(solution)/shard_map/pallas_call | solution.py:24
  39.9 5.3 %all-to-all-start.1 = ((bf16[64,2,128]{2,1,0:T(2,128)(2,1)}), bf16[64,2,128]{2,1,0:T(2,128)(2,1)S(1)}, u32[]{:S(2)}, u32[]{:S(2)}) async-start(bf16[64,2,128]{2,1,0:T(2,128)(2,1)} %bitcast.7), calls=%async_computation.1 | async-start | bytes 65536 | tf_op jit(solution)/shard_map/all_to_all | solution.py:347
  45.2 4.6 %shard_map.90 = (bf16[30,2048]{1,0:T(8,128)(2,1)}, f32[32,2048]{1,0:T(8,128)S(1)}, bf16[16,512,128]{2,1,0:T(8,128)(2,1)S(1)}) custom-call(s32[4,18]{1,0:T(4,128)S(1)} %get-tuple-element.19.where_near, s32[1,512]{1,0:T(1,128)S(1)} %get-tuple-element.20.recv_ref, bf16[160,128]{1,0:T(8,128)(2,1)S(1)} %get-tuple-element.21.g2_ref, ...), custom_call_target="tpu_custom_call" | custom-call | flops 335544320 | bytes 15501600 | tf_op jit(solution)/shard_map/pallas_call | solution.py:24
  49.8 4.7 %all-to-all-done.1 = bf16[64,2,128]{2,1,0:T(2,128)(2,1)S(1)} async-done(((bf16[64,2,128]{2,1,0:T(2,128)(2,1)}), bf16[64,2,128]{2,1,0:T(2,128)(2,1)S(1)}, u32[]{:S(2)}, u32[]{:S(2)}) %all-to-all-start.1) | async-done | bytes 32800 | tf_op jit(solution)/shard_map/all_to_all | solution.py:347
  54.5 1.3 %shard_map.91 = bf16[30,2048]{1,0:T(8,128)(2,1)} custom-call(f32[32,2048]{1,0:T(8,128)S(1)} %get-tuple-element.33.own_ref, bf16[128,128]{1,0:T(8,128)(2,1)S(1)} %bitcast.10, bf16[16,512,128]{2,1,0:T(8,128)(2,1)S(1)} %get-tuple-element.35.r_ref), custom_call_target="tpu_custom_call" | custom-call | flops 67108864 | bytes 2514944 | tf_op jit(solution)/shard_map/pallas_call | solution.py:24
Async XLA Ops:
  0.6 7.4 %collective-permute-start.2 = (bf16[30,2048]{1,0:T(8,128)(2,1)}, bf16[30,2048]{1,0:T(8,128)(2,1)S(1)}, u32[]{:S(2)}, u32[]{:S(2)}) collective-permute-start(bf16[30,2048]{1,0:T(8,128)(2,1)} %own_hbm.1), channel_id=1, source_target_pairs={{3,0},{0,1},{1,2},{2,3},{7,4},{4,5},{5,6},{6,7},{11,8},{8,9},{9,10... | collective-permute-start | bytes 368648 | tf_op jit(solution)/shard_map/ppermute | solution.py:300
  2.8 8.5 %collective-permute-start.1 = (bf16[30,2048]{1,0:T(8,128)(2,1)}, bf16[30,2048]{1,0:T(8,128)(2,1)S(1)}, u32[]{:S(2)}, u32[]{:S(2)}) collective-permute-start(bf16[30,2048]{1,0:T(8,128)(2,1)} %own_hbm.1), channel_id=1, source_target_pairs={{2,0},{3,1},{0,2},{1,3},{6,4},{7,5},{4,6},{5,7},{10,8},{11,9},{8,1... | collective-permute-start | bytes 368648 | tf_op jit(solution)/shard_map/ppermute | solution.py:300
  6.9 5.6 %collective-permute-start = (bf16[30,2048]{1,0:T(8,128)(2,1)S(1)}, bf16[30,2048]{1,0:T(8,128)(2,1)S(1)}, u32[]{:S(2)}, u32[]{:S(2)}) collective-permute-start(bf16[30,2048]{1,0:T(8,128)(2,1)S(1)} %get-tuple-element.22.v0), channel_id=1, source_target_pairs={{1,0},{2,1},{3,2},{0,3},{5,4},{6,5},{7,6},{4,7},{9,8},{10,9},{11,1... | collective-permute-start | bytes 368648 | tf_op jit(solution)/shard_map/ppermute | solution.py:300
  14.7 22.6 %all-to-all-start = ((bf16[64,8,128]{2,1,0:T(8,128)(2,1)}), bf16[64,8,128]{2,1,0:T(8,128)(2,1)S(1)}, u32[]{:S(2)}, u32[]{:S(2)}) async-start(bf16[64,8,128]{2,1,0:T(8,128)(2,1)} %bitcast.5), calls=%async_computation | async-start | bytes 262144 | tf_op jit(solution)/shard_map/all_to_all | solution.py:333
  39.9 14.6 %all-to-all-start.1 = ((bf16[64,2,128]{2,1,0:T(2,128)(2,1)}), bf16[64,2,128]{2,1,0:T(2,128)(2,1)S(1)}, u32[]{:S(2)}, u32[]{:S(2)}) async-start(bf16[64,2,128]{2,1,0:T(2,128)(2,1)} %bitcast.7), calls=%async_computation.1 | async-start | bytes 65536 | tf_op jit(solution)/shard_map/all_to_all | solution.py:347
